TPU v7x, 256 devices: a whole 4x4x8 slice. The times are simulated.
256 devices in a mesh: tok: 2 (over y_hi), fin: 32 (over x, z), fout: 4 (over y_lo, core).
Axes of the slice: x: 4, y: 4 (y_hi: 2, y_lo: 2; y = y_hi * 2 + y_lo), z: 8, core: 2. Of those that a mesh axis runs over, the one named last changes fastest.
Arguments:
- activations: float32 [4096, 8192], P('tok', 'fin'), may hold values from -0.09375 to 0.09375
- out_grad: float32 [4096, 8192], P(('tok', 'fin'), 'fout'), may hold values from -6 to 6
- weight: float32 [8192, 8192], P('fin', 'fout'), may hold values from -0.0625 to 0.0625
Outputs:
- in_grad: float32 [4096, 8192], P(('tok', 'fout'), 'fin')
- weight_grad: float32 [8192, 8192], P(('fin', 'tok'), 'fout')
All inputs are finite; a program needn't handle non-finite values.
Results may differ from a plain program's by a relative error of at most 0.000075.
Values sent between devices are 32-bit elements; how exact they have to be, the bound alone decides.
No kernel may reach another device: no remote copies, remote signals or barrier semaphores. Data moves between devices by JAX's collectives and lax.ppermute only.
A program may use at most 128 MiB of HBM per device.

v0:
```python
import jax
import jax.numpy as jnp
from jax import lax
from jax.sharding import PartitionSpec as P


def times_weight(grad_block, weight):
    return lax.dot_general(
        grad_block,
        weight,
        (((1,), (1,)), ((), ())),
        precision=lax.Precision.HIGHEST,
        preferred_element_type=jnp.float32,
    )


def outer_sum(act_block, grad_block):
    return lax.dot_general(
        act_block,
        grad_block,
        (((0,), (0,)), ((), ())),
        precision=lax.Precision.HIGHEST,
        preferred_element_type=jnp.float32,
    )


def local(activations, out_grad, weight):
    gathered = lax.all_gather(out_grad, "fin", axis=0, tiled=True)
    in_part = times_weight(gathered, weight)
    weight_part = outer_sum(activations, gathered)
    in_grad = lax.psum_scatter(in_part, "fout", scatter_dimension=0, tiled=True)
    weight_grad = lax.psum_scatter(weight_part, "tok", scatter_dimension=0, tiled=True)
    return (in_grad, weight_grad)


def solution(mesh):
    in_specs = (P("tok", "fin"), P(("tok", "fin"), "fout"), P("fin", "fout"))
    out_specs = (P(("tok", "fout"), "fin"), P(("fin", "tok"), "fout"))
    return jax.shard_map(local, mesh=mesh, in_specs=in_specs, out_specs=out_specs, check_vma=False)
```

profile of v0, /device:TPU:1, one launch (start us, length us, event | category | flops | bytes accessed | tf_op | source)
XLA Modules:
  0.0 247.9 jit_solution(18008182346156344990)
XLA Ops:
  7.2 0.0 copy-start
  7.2 0.0 all-gather.2.cloned.1.call-start
  7.2 0.7 all-gather.2.cloned.1.call-update
  7.9 0.0 reduce-scatter.3.cloned.1.call-start
  8.0 145.4 %all-gather.2.cloned.1.call-done = f32[2048,2048]{1,0:T(8,128)} async-done(((f32[64,2048]{1,0:T(8,128)}), f32[2048,2048]{1,0:T(8,128)}) %all-gather.2.cloned.1.call-update) | async-done | bytes 16777232 | tf_op jit(solution)/shard_map/all_gather | solution.py:28
  153.3 0.0 copy-done
  153.3 16.9 %fusion = f32[2048,256]{1,0:T(8,128)} fusion(f32[2048,2048]{1,0:T(8,128)} %all-gather.2.cloned.1.call-done, f32[256,2048]{1,0:T(8,128)S(1)} %copy-done), kind=kOutput, calls=%fused_computation | convolution fusion | flops 12884901888 | bytes 20971520 | tf_op jit(solution)/shard_map/dot_general | solution.py:8
  170.2 0.0 reduce-scatter.3.cloned.1.call-update
  170.2 0.0 reduce-scatter.5.cloned.1.call-start
  170.3 18.3 %fusion.1 = f32[256,2048]{1,0:T(8,128)} fusion(f32[2048,256]{1,0:T(8,128)} %param.3, f32[2048,2048]{1,0:T(8,128)} %all-gather.2.cloned.1.call-done), kind=kOutput, calls=%fused_computation.1 | convolution fusion | flops 12884901888 | bytes 20971520 | tf_op jit(solution)/shard_map/dot_general | solution.py:18
  188.6 0.0 reduce-scatter.5.cloned.1.call-update
  188.6 10.6 %reduce-scatter.3.cloned.1.call-done = f32[512,256]{1,0:T(8,128)} async-done(((f32[2048,256]{1,0:T(8,128)}), f32[512,256]{1,0:T(8,128)}) %reduce-scatter.3.cloned.1.call-update) | async-done | bytes 524304 | tf_op jit(solution)/shard_map/reduce_scatter | solution.py:31
  199.2 42.2 %reduce-scatter.5.cloned.1.call-done = f32[128,2048]{1,0:T(8,128)} async-done(((f32[256,2048]{1,0:T(8,128)}), f32[128,2048]{1,0:T(8,128)}) %reduce-scatter.5.cloned.1.call-update) | async-done | bytes 1048592 | tf_op jit(solution)/shard_map/reduce_scatter | solution.py:32
Async XLA Ops:
  7.2 146.2 %copy-start = (f32[256,2048]{1,0:T(8,128)S(1)}, f32[256,2048]{1,0:T(8,128)}, u32[]{:S(2)}) copy-start(f32[256,2048]{1,0:T(8,128)} %param.5) | copy-start | bytes 6291460
  7.2 146.1 %all-gather.2.cloned.1.call-start = ((), (), s32[]{:S(2)}) async-start(), calls=%async_computation.2 | async-start | bytes 17301504 | tf_op jit(solution)/shard_map/all_gather | solution.py:28
  7.9 191.3 %reduce-scatter.3.cloned.1.call-start = ((), (), s32[]{:S(2)}) async-start(), calls=%async_computation.3 | async-start | bytes 2621440 | tf_op jit(solution)/shard_map/reduce_scatter | solution.py:31
  170.2 71.1 %reduce-scatter.5.cloned.1.call-start = ((), (), s32[]{:S(2)}) async-start(), calls=%async_computation.4 | async-start | bytes 3145728 | tf_op jit(solution)/shard_map/reduce_scatter | solution.py:32
Sparse Core Ops, SparseCore 0:
  10.6 142.6 all-gather.1
  170.3 28.8 reduce-scatter.2
  202.3 39.0 reduce-scatter.4
where the time goes:
time: 248 us
  waiting for transfers between devices  199 us (80%)
  matrix products  35.2 us (14%)
  between operations  13.7 us (6%)
    all_gather x1, waiting for transfers between devices, local(): gathered = lax.all_gather(out_grad, 'fin', axis=0, tiled=True)  145 us
    reduce_scatter x1, waiting for transfers between devices, local(): lax.psum_scatter(weight_part, 'tok', scatter_dimension=0, tiled=True)  42.2 us
    dot_general x1, matrix products, outer_sum(): lax.dot_general(act_block, grad_block, (((0,), (0,)), ((), ())), precisio...  18.3 us
    dot_general x1, matrix products, times_weight(): lax.dot_general(grad_block, weight, (((1,), (1,)), ((), ())), precision=l...  16.9 us
    reduce_scatter x1, waiting for transfers between devices, local(): in_grad = lax.psum_scatter(in_part, 'fout', scatter_dimension=0, tiled=True)  10.6 us
  transfers between devices with their start and end apart: 3, of which 3 were waited for; matrix products, arithmetic and copies ran while one was open for 7% of the time, Pallas kernels for 0%

commit v1 on v0

--- a/solution.py
+++ b/solution.py
@@ -9,7 +9,7 @@
         grad_block,
         weight,
         (((1,), (1,)), ((), ())),
-        precision=lax.Precision.HIGHEST,
+        precision=lax.Precision.HIGH,
         preferred_element_type=jnp.float32,
     )
 
@@ -19,7 +19,7 @@
         act_block,
         grad_block,
         (((0,), (0,)), ((), ())),
-        precision=lax.Precision.HIGHEST,
+        precision=lax.Precision.HIGH,
         preferred_element_type=jnp.float32,
     )
 

time: 248 us -> 243 us (0.980)
  matrix products: 35.2 us -> 24.1 us
  waiting for transfers between devices: 199 us -> 205 us
    dot_general x1, matrix products: 18.3 us -> 12.4 us  [outer_sum(): lax.dot_general(act_block, grad_block, (((0,), (0,)), ((), ())), precisio...]
    reduce_scatter x1, waiting for transfers between devices: 10.6 us -> 16.5 us  [local(): in_grad = lax.psum_scatter(in_part, 'fout', scatter_dimension=0, tiled=True)]
    dot_general x1, matrix products: 16.9 us -> 11.7 us  [times_weight(): lax.dot_general(grad_block, weight, (((1,), (1,)), ((), ())), precision=l...]
  transfers between devices with their start and end apart: 3 -> 3, of which waited for: 3 -> 3; matrix products, arithmetic and copies ran while one was open for 7% -> 5% of each run, Pallas kernels for 0% -> 0%
where the time goes in v1:
time: 243 us
  waiting for transfers between devices  205 us (84%)
  matrix products  24.1 us (10%)
  between operations  13.7 us (6%)
    all_gather x1, waiting for transfers between devices, local(): gathered = lax.all_gather(out_grad, 'fin', axis=0, tiled=True)  145 us
    reduce_scatter x1, waiting for transfers between devices, local(): lax.psum_scatter(weight_part, 'tok', scatter_dimension=0, tiled=True)  42.2 us
    reduce_scatter x1, waiting for transfers between devices, local(): in_grad = lax.psum_scatter(in_part, 'fout', scatter_dimension=0, tiled=True)  16.5 us
    dot_general x1, matrix products, outer_sum(): lax.dot_general(act_block, grad_block, (((0,), (0,)), ((), ())), precisio...  12.4 us
    dot_general x1, matrix products, times_weight(): lax.dot_general(grad_block, weight, (((1,), (1,)), ((), ())), precision=l...  11.7 us
  transfers between devices with their start and end apart: 3, of which 3 were waited for; matrix products, arithmetic and copies ran while one was open for 5% of the time, Pallas kernels for 0%

profile of v1, /device:TPU:1, one launch (start us, length us, event | category | flops | bytes accessed | tf_op | source)
XLA Modules:
  0.0 242.7 jit_solution(11949740450050510951)
XLA Ops:
  7.2 0.0 copy-start
  7.2 0.0 all-gather.2.cloned.1.call-start
  7.2 0.7 all-gather.2.cloned.1.call-update
  7.9 0.0 reduce-scatter.3.cloned.1.call-start
  8.0 145.4 %all-gather.2.cloned.1.call-done = f32[2048,2048]{1,0:T(8,128)} async-done(((f32[64,2048]{1,0:T(8,128)}), f32[2048,2048]{1,0:T(8,128)}) %all-gather.2.cloned.1.call-update) | async-done | bytes 16777232 | tf_op jit(solution)/shard_map/all_gather | solution.py:28
  153.3 0.0 copy-done
  153.3 11.7 %fusion = f32[2048,256]{1,0:T(8,128)} fusion(f32[2048,2048]{1,0:T(8,128)} %all-gather.2.cloned.1.call-done, f32[256,2048]{1,0:T(8,128)S(1)} %copy-done), kind=kOutput, calls=%fused_computation | convolution fusion | flops 6442450944 | bytes 20971520 | tf_op jit(solution)/shard_map/dot_general | solution.py:8
  165.0 0.0 reduce-scatter.3.cloned.1.call-update
  165.0 0.0 reduce-scatter.5.cloned.1.call-start
  165.1 12.4 %fusion.1 = f32[256,2048]{1,0:T(8,128)} fusion(f32[2048,256]{1,0:T(8,128)} %param.3, f32[2048,2048]{1,0:T(8,128)} %all-gather.2.cloned.1.call-done), kind=kOutput, calls=%fused_computation.1 | convolution fusion | flops 6442450944 | bytes 20971520 | tf_op jit(solution)/shard_map/dot_general | solution.py:18
  177.5 0.0 reduce-scatter.5.cloned.1.call-update
  177.6 16.5 %reduce-scatter.3.cloned.1.call-done = f32[512,256]{1,0:T(8,128)} async-done(((f32[2048,256]{1,0:T(8,128)}), f32[512,256]{1,0:T(8,128)}) %reduce-scatter.3.cloned.1.call-update) | async-done | bytes 524304 | tf_op jit(solution)/shard_map/reduce_scatter | solution.py:31
  194.0 42.2 %reduce-scatter.5.cloned.1.call-done = f32[128,2048]{1,0:T(8,128)} async-done(((f32[256,2048]{1,0:T(8,128)}), f32[128,2048]{1,0:T(8,128)}) %reduce-scatter.5.cloned.1.call-update) | async-done | bytes 1048592 | tf_op jit(solution)/shard_map/reduce_scatter | solution.py:32
Async XLA Ops:
  7.2 146.2 %copy-start = (f32[256,2048]{1,0:T(8,128)S(1)}, f32[256,2048]{1,0:T(8,128)}, u32[]{:S(2)}) copy-start(f32[256,2048]{1,0:T(8,128)} %param.5) | copy-start | bytes 6291460
  7.2 146.1 %all-gather.2.cloned.1.call-start = ((), (), s32[]{:S(2)}) async-start(), calls=%async_computation.2 | async-start | bytes 17301504 | tf_op jit(solution)/shard_map/all_gather | solution.py:28
  7.9 186.1 %reduce-scatter.3.cloned.1.call-start = ((), (), s32[]{:S(2)}) async-start(), calls=%async_computation.3 | async-start | bytes 2621440 | tf_op jit(solution)/shard_map/reduce_scatter | solution.py:31
  165.0 71.1 %reduce-scatter.5.cloned.1.call-start = ((), (), s32[]{:S(2)}) async-start(), calls=%async_computation.4 | async-start | bytes 3145728 | tf_op jit(solution)/shard_map/reduce_scatter | solution.py:32
Sparse Core Ops, SparseCore 0:
  10.6 142.6 all-gather.1
  165.2 28.8 reduce-scatter.2
  197.1 39.0 reduce-scatter.4

commit v2 on v1

v2 whole, which is shorter than its diff:
```python
import functools

import jax
import jax.numpy as jnp
from jax import lax
from jax.experimental import pallas as pl
from jax.experimental.pallas import tpu as pltpu
from jax.sharding import PartitionSpec as P

AXES = ("tok", "fin", "fout")
NX, NZ = 4, 8
ROWS = 64
COLS = 1024
FEAT = 256
TILE = 256
GROUPS = ((0, 7, 1, 6, 2), (5, 3, 4))


def pairs(move):
    out = []
    for t in range(2):
        for x in range(NX):
            for z in range(NZ):
                for y in range(2):
                    for c in range(2):
                        a, b, d, e, f = move(t, x, z, y, c)
                        src = (t * NX * NZ + x * NZ + z) * 4 + 2 * y + c
                        dst = (a * NX * NZ + b * NZ + d % NZ) * 4 + 2 * e + f
                        out.append((src, dst))
    return out


ZUP = pairs(lambda t, x, z, y, c: (t, x, z + 1, y, c))
ZDOWN = pairs(lambda t, x, z, y, c: (t, x, z - 1 + NZ, y, c))
SIDE = pairs(lambda t, x, z, y, c: (t, x ^ 1, z, y, c))
MATE = pairs(lambda t, x, z, y, c: (t, x ^ 3, z, y, c))
CORE = pairs(lambda t, x, z, y, c: (t, x, z, y, 1 - c))
YLOW = pairs(lambda t, x, z, y, c: (t, x, z, 1 - y, c))
TOK = pairs(lambda t, x, z, y, c: (1 - t, x, z, y, c))
DIAG = pairs(lambda t, x, z, y, c: (1 - t, x ^ 3, z, y, c))


def send(value, perm):
    return lax.ppermute(value, AXES, perm)


def split(v):
    hi = v.astype(jnp.bfloat16)
    lo = (v - hi.astype(jnp.float32)).astype(jnp.bfloat16)
    return hi, lo


def dot(a, b, dims):
    return lax.dot_general(a, b, (dims, ((), ())), preferred_element_type=jnp.float32)


def group_body(layout, n, first, last, s_ref, *refs):
    refs = list(refs)
    take = lambda k: [refs.pop(0) for _ in range(k)]
    pieces = take(len(layout))
    own, mate = take(4 * n), take(4 * n)
    w_own, w_a, w_b = take(3)
    wg_in = None if first else take(1)[0]
    keep_ref, send_ref = take(2)
    wg_refs = take(4 if last else 1)
    ghi, glo, thi, tlo, wcat = refs
    span = n * ROWS
    spin, tok = s_ref[0], s_ref[1]
    step = pl.program_id(0)

    @pl.when(step == 0)
    def _():
        for g in range(n):
            for base, blocks in ((0, own), (FEAT, mate)):
                rows = jnp.concatenate([b[...] for b in blocks[4 * g : 4 * g + 4]], axis=0)
                hi, lo = split(rows.T)
                thi[pl.ds(base, FEAT), pl.ds(g * 256, 256)] = hi
                tlo[pl.ds(base, FEAT), pl.ds(g * 256, 256)] = lo

    for ref, parts in zip(pieces, layout):
        for start, e, k in parts:
            v = spin ^ e
            slot = (v & 1) * 2 + (v >> 1)
            hi, lo = split(ref[pl.ds(start, ROWS), :])
            rows = pl.ds(pl.multiple_of(slot * span + k * ROWS, ROWS), ROWS)
            ghi[rows, :] = hi
            glo[rows, :] = lo
    wcat[pl.ds(0, FEAT), :] = w_own[...]
    wcat[pl.ds(pl.multiple_of(FEAT + tok * 128, 128), 128), :] = w_a[...]
    wcat[pl.ds(pl.multiple_of(FEAT + (1 - tok) * 128, 128), 128), :] = w_b[...]
    whi, wlo = split(wcat[...])
    nt = ((1,), (1,))
    nn = ((1,), (0,))

    def gate(clear):
        for ref, base in ((keep_ref, 0), (send_ref, 2 * span)):
            for r in range(0, 2 * span, 128):
                rows = pl.ds(base + r, 128)
                hi = ghi[rows, :]
                term = dot(hi, whi, nt) + dot(hi, wlo, nt) + dot(glo[rows, :], whi, nt)
                if clear:
                    ref[pl.ds(r, 128), :] = term
                else:
                    ref[pl.ds(r, 128), :] += term

    pl.when(step == 0)(lambda: gate(True))
    pl.when(step > 0)(lambda: gate(False))

    for q in range(4):
        rows = pl.ds(q * 128, 128)
        acc = dot(thi[rows, :], ghi[...], nn) + dot(thi[rows, :], glo[...], nn) + dot(tlo[rows, :], ghi[...], nn)
        if not first:
            acc = acc + wg_in[rows, :]
        if not last:
            wg_refs[0][rows, :] = acc
        else:
            wcat[rows, :] = acc
    if last:
        for base, mine, other in ((0, wg_refs[0], wg_refs[1]), (FEAT, wg_refs[2], wg_refs[3])):
            mine[...] = wcat[pl.ds(pl.multiple_of(base + tok * 128, 128), 128), :]
            other[...] = wcat[pl.ds(pl.multiple_of(base + (1 - tok) * 128, 128), 128), :]


def group(index, scalars, pieces, layout, acts, a_near, a_far, weights, wg):
    turns = GROUPS[index]
    n = len(turns)
    first, last = wg is None, index == len(GROUPS) - 1
    span = n * ROWS
    tile = lambda rows: pl.BlockSpec((rows, TILE), lambda j, s: (0, j))

    def own_at(flip, r):
        return pl.BlockSpec((ROWS, FEAT), lambda j, s: ((s[2] ^ flip) * NZ + lax.rem(s[3] + r, NZ), 0))

    def mate_at(flip, r):
        return pl.BlockSpec((ROWS, FEAT), lambda j, s: ((s[4] ^ flip) * NZ + lax.rem(s[3] + r, NZ), 0))

    in_specs, args = [], []
    for v in pieces:
        in_specs.append(tile(v.shape[0]))
        args.append(v)
    for cr in range(2):
        for yr in range(2):
            for r in turns:
                in_specs.append(own_at(cr | yr << 1, r))
                args.append(acts)
    for cr in range(2):
        for yr in range(2):
            for r in turns:
                in_specs.append(mate_at(yr, r))
                args.append(a_far if cr else a_near)
    for v in weights:
        in_specs.append(tile(v.shape[0]))
        args.append(v)
    if not first:
        in_specs.append(tile(2 * FEAT))
        args.append(wg)
    whole = pl.BlockSpec((2 * span, 2 * FEAT), lambda j, s: (0, 0))
    share = jax.ShapeDtypeStruct((2 * span, 2 * FEAT), jnp.float32)
    if last:
        wg_specs = [tile(128)] * 4
        wg_shapes = [jax.ShapeDtypeStruct((128, COLS), jnp.float32)] * 4
    else:
        wg_specs = [tile(2 * FEAT)]
        wg_shapes = [jax.ShapeDtypeStruct((2 * FEAT, COLS), jnp.float32)]
    rows = 4 * span
    return pl.pallas_call(
        functools.partial(group_body, layout, n, first, last),
        grid_spec=pltpu.PrefetchScalarGridSpec(
            num_scalar_prefetch=1,
            grid=(COLS // TILE,),
            in_specs=in_specs,
            out_specs=[whole, whole, *wg_specs],
            scratch_shapes=[pltpu.VMEM((rows, TILE), jnp.bfloat16)] * 2
            + [pltpu.VMEM((2 * FEAT, rows), jnp.bfloat16)] * 2
            + [pltpu.VMEM((2 * FEAT, TILE), jnp.float32)],
        ),
        out_shape=[share, share, *wg_shapes],
        cost_estimate=pl.CostEstimate(
            flops=24 * rows * COLS * FEAT, bytes_accessed=4 * (rows * COLS + 4 * FEAT * COLS), transcendentals=0
        ),
    )(scalars, *args)


def pick(stacked, index, axis):
    return lax.dynamic_index_in_dim(stacked, index, axis, keepdims=False)


def local(acts, grad, weight):
    tok = lax.axis_index("tok")
    fin = lax.axis_index("fin")
    fout = lax.axis_index("fout")
    x, z = fin // NZ, fin % NZ
    y, c = fout // 2, fout % 2
    half = x // 2

    def side(v, which):
        return lax.dynamic_slice_in_dim(v, which * COLS, COLS, axis=1)

    m2 = send(side(grad, 1 - half), MATE)
    zs, ss, xs = {0: side(grad, half)}, {}, {}
    far = lax.dynamic_slice(weight, (tok * 128, (1 - half) * COLS), (128, COLS))
    w_a = send(far, MATE)
    w_b = send(w_a, TOK)
    w_own = side(weight, half)
    a_near = send(pick(acts.reshape(2, 2, 512, FEAT), c, 1).reshape(1024, FEAT), MATE)
    a_far = send(a_near, CORE)
    xs[0] = jnp.concatenate([m2, send(m2, SIDE)], axis=0)
    for s in range(1, 5):
        down, up = s, NZ - s
        zs[down] = send(zs[down - 1], ZDOWN)
        if s < 4:
            zs[up] = send(zs[(up + 1) % NZ], ZUP)
            xs[up] = send(xs[(up + 1) % NZ], ZUP)
            xs[down] = send(xs[down - 1], ZDOWN)
    x4 = (send(xs[5][:ROWS], ZUP), send(xs[3][ROWS:], ZDOWN))
    for r in range(NZ):
        ss[r] = send(zs[r], SIDE)

    scalars = jnp.stack([x ^ fout, tok, fout, z, y]).astype(jnp.int32)
    wg = None
    shares = {}
    for i, turns in enumerate(GROUPS):
        pieces, layout = [], []
        for k, r in enumerate(turns):
            pieces += [zs[r], ss[r]]
            layout += [((0, 0, k),), ((0, 1, k),)]
            if r == 4:
                pieces += list(x4)
                layout += [((0, 3, k),), ((0, 2, k),)]
            else:
                pieces.append(xs[r])
                layout.append(((0, 3, k), (ROWS, 2, k)))
        out = group(i, scalars, pieces, tuple(layout), acts, a_near, a_far, (w_own, w_a, w_b), wg)
        keep, give = out[:2]
        wg = out[2] if len(out) == 3 else out[2:]
        span = ROWS * len(turns)
        got = send(give, CORE)
        last = send(keep[span:] + got[span:], YLOW)
        mine = keep[:span] + got[:span] + last
        share = mine[:, :FEAT] + send(mine[:, FEAT:], MATE)
        for k, r in enumerate(turns):
            shares[r] = share[k * ROWS : (k + 1) * ROWS]

    rel = jnp.stack([shares[r] for r in range(NZ)])
    twice = jnp.concatenate([rel, rel], axis=0)
    in_grad = lax.dynamic_slice_in_dim(twice, (NZ - z) % NZ, NZ, axis=0).reshape(NZ * ROWS, FEAT)

    here = wg[0] + send(wg[1], TOK)
    there = send(wg[2], MATE) + send(wg[3], DIAG)
    weight_grad = jnp.where(half == 0, jnp.concatenate([here, there], axis=1), jnp.concatenate([there, here], axis=1))
    return (in_grad, weight_grad)


def solution(mesh):
    in_specs = (P("tok", "fin"), P(("tok", "fin"), "fout"), P("fin", "fout"))
    out_specs = (P(("tok", "fout"), "fin"), P(("fin", "tok"), "fout"))
    return jax.shard_map(local, mesh=mesh, in_specs=in_specs, out_specs=out_specs, check_vma=False)
```

time: 243 us -> 205 us (0.84)
  waiting for transfers between devices: 205 us -> 76.8 us
  starting transfers between devices: 0.12 us -> 65.2 us
  Pallas kernels: 0 us -> 39 us
  matrix products: 24.1 us -> 0 us
  local copies, waits for them, and re-layouts: 0.01 us -> 13 us
  between operations: 13.7 us -> 1.05 us
  other arithmetic: 0 us -> 8.73 us
    all_gather x1 -> x0, waiting for transfers between devices: 145 us -> none  [local(): gathered = lax.all_gather(out_grad, 'fin', axis=0, tiled=True)]
    ppermute x0 -> x38, waiting for transfers between devices: none -> 76.8 us  [send(): return lax.ppermute(value, AXES, perm)]
    ppermute x0 -> x38, starting transfers between devices: none -> 65.2 us  [send(): return lax.ppermute(value, AXES, perm)]
    reduce_scatter x2 -> x0, waiting for transfers between devices: 58.6 us -> none  [the longest x1 42.2 us: local(): lax.psum_scatter(weight_part, 'tok', scatter_dimension=0, tiled=True)]
    pallas_call x0 -> x2, Pallas kernels: none -> 39 us  [group(): pl.pallas_call(functools.partial(group_body, layout, n, first, last), gri...]
    dot_general x2 -> x0, matrix products: 24.1 us -> none  [the longest x1 12.4 us: outer_sum(): lax.dot_general(act_block, grad_block, (((0,), (0,)), ((), ())), precisio...]
    add x0 -> x8, other arithmetic: none -> 7.59 us  [the longest x2 2.75 us: local(): last = send(keep[span:] + got[span:], YLOW)]
    dynamic_slice x0 -> x5, local copies, waits for them, and re-layouts: none -> 6.6 us  [the longest x2 3.4 us: side(): return lax.dynamic_slice_in_dim(v, which * COLS, COLS, axis=1)]
  transfers between devices with their start and end apart: 3 -> 38, of which waited for: 3 -> 13; matrix products, arithmetic and copies ran while one was open for 5% -> 9% of each run, Pallas kernels for 0% -> 19%
where the time goes in v2:
time: 205 us; the launch traced here: 204 us
  waiting for transfers between devices  76.8 us (37%)
  starting transfers between devices  65.2 us (32%)
  Pallas kernels  39 us (19%)
  local copies, waits for them, and re-layouts  13 us (6%)
  other arithmetic  8.73 us (4%)
    ppermute x38, waiting for transfers between devices, send(): return lax.ppermute(value, AXES, perm)  76.8 us
    ppermute x38, starting transfers between devices, send(): return lax.ppermute(value, AXES, perm)  65.2 us
    pallas_call x2, Pallas kernels, group(): pl.pallas_call(functools.partial(group_body, layout, n, first, last), gri...  39 us
  transfers between devices with their start and end apart: 38, of which 13 were waited for; matrix products, arithmetic and copies ran while one was open for 9% of the time, Pallas kernels for 19%

profile of v2, /device:TPU:1, one launch (start us, length us, event | category | flops | bytes accessed | tf_op | source)
XLA Modules:
  0.0 203.7 jit_solution(13882390584162029865)
XLA Ops:
  0.7 1.1 constant_dynamic-slice_fusion.3
  1.8 3.4 %collective-permute-start.1 = (f32[64,1024]{1,0:T(8,128)S(1)}, f32[64,1024]{1,0:T(8,128)S(1)}, u32[]{:S(2)}, u32[]{:S(2)}) collective-permute-start(f32[64,1024]{1,0:T(8,128)S(1)} %get-tuple-element.20), channel_id=1, source_target_pairs={{0,96},{1,97},{2,98},{3,99},{4,100},{5,101},{6,102},{7,103},{8,104... | collective-permute-start | bytes 786440 | tf_op jit(solution)/shard_map/ppermute | solution.py:44
  5.1 5.0 %collective-permute-done.1 = f32[64,1024]{1,0:T(8,128)S(1)} collective-permute-done((f32[64,1024]{1,0:T(8,128)S(1)}, f32[64,1024]{1,0:T(8,128)S(1)}, u32[]{:S(2)}, u32[]{:S(2)}) %collective-permute-start.1) | collective-permute-done | bytes 262176 | tf_op jit(solution)/shard_map/ppermute | solution.py:44
  10.1 0.9 collective-permute-start.2
  11.1 1.3 constant_dynamic-slice_fusion.2
  12.4 2.6 %collective-permute-start.15 = (f32[1024,256]{1,0:T(8,128)S(1)}, f32[1024,256]{1,0:T(8,128)S(1)}, u32[]{:S(2)}, u32[]{:S(2)}) collective-permute-start(f32[1024,256]{1,0:T(8,128)S(1)} %bitcast.59), channel_id=1, source_target_pairs={{0,96},{1,97},{2,98},{3,99},{4,100},{5,101},{6,102},{7,103},{8,104... | collective-permute-start | bytes 3145736 | tf_op jit(solution)/shard_map/ppermute | solution.py:44
  14.9 0.9 collective-permute-start
  15.9 3.3 %collective-permute-start.5 = (f32[128,1024]{1,0:T(8,128)S(1)}, f32[128,1024]{1,0:T(8,128)S(1)}, u32[]{:S(2)}, u32[]{:S(2)}) collective-permute-start(f32[128,1024]{1,0:T(8,128)S(1)} %constant_dynamic-update-slice_fusion.refs_2_), channel_id=1, source_target_pairs={{0,4},{1,5},{2,6},{3,7},{4,8},{5,9},{6,10},{7,11},{8,12},{9,13},{1... | collective-permute-start | bytes 1572872 | tf_op jit(solution)/shard_map/ppermute | solution.py:44
  19.2 4.6 %collective-permute-start.8 = (f32[128,1024]{1,0:T(8,128)S(1)}, f32[128,1024]{1,0:T(8,128)}, u32[]{:S(2)}, u32[]{:S(2)}) collective-permute-start(f32[128,1024]{1,0:T(8,128)S(1)} %constant_dynamic-update-slice_fusion.refs_2_), channel_id=1, source_target_pairs={{0,28},{1,29},{2,30},{3,31},{4,0},{5,1},{6,2},{7,3},{8,4},{9,5},{1... | collective-permute-start | bytes 1572872 | tf_op jit(solution)/shard_map/ppermute | solution.py:44
  23.8 5.0 %collective-permute-start.6 = (f32[64,1024]{1,0:T(8,128)S(1)}, f32[64,1024]{1,0:T(8,128)S(1)}, u32[]{:S(2)}, u32[]{:S(2)}) collective-permute-start(f32[64,1024]{1,0:T(8,128)S(1)} %get-tuple-element.21.refs_0_), channel_id=1, source_target_pairs={{0,28},{1,29},{2,30},{3,31},{4,0},{5,1},{6,2},{7,3},{8,4},{9,5},{1... | collective-permute-start | bytes 786440 | tf_op jit(solution)/shard_map/ppermute | solution.py:44
  28.8 8.0 %collective-permute-done.3.refs_3_ = f32[64,1024]{1,0:T(8,128)} collective-permute-done((f32[64,1024]{1,0:T(8,128)S(1)}, f32[64,1024]{1,0:T(8,128)}, u32[]{:S(2)}, u32[]{:S(2)}) %collective-permute-start.3) | collective-permute-done | bytes 262176 | tf_op jit(solution)/shard_map/ppermute | solution.py:44
  36.9 0.7 collective-permute-start.4
  37.6 0.7 collective-permute-start.7
  38.4 2.7 %collective-permute-start.14 = (f32[128,1024]{1,0:T(8,128)}, f32[128,1024]{1,0:T(8,128)}, u32[]{:S(2)}, u32[]{:S(2)}) collective-permute-start(f32[128,1024]{1,0:T(8,128)} %collective-permute-done.8.refs_8_), channel_id=1, source_target_pairs={{0,28},{1,29},{2,30},{3,31},{4,0},{5,1},{6,2},{7,3},{8,4},{9,5},{1... | collective-permute-start | bytes 1572872 | tf_op jit(solution)/shard_map/ppermute | solution.py:44
  41.0 1.4 collective-permute-done.4.refs_4_
  42.4 1.1 dynamic_slice.23
  43.5 2.3 %collective-permute-done.7.refs_7_ = f32[64,1024]{1,0:T(8,128)S(1)} collective-permute-done((f32[64,1024]{1,0:T(8,128)S(1)}, f32[64,1024]{1,0:T(8,128)S(1)}, u32[]{:S(2)}, u32[]{:S(2)}) %collective-permute-start.7) | collective-permute-done | bytes 262176 | tf_op jit(solution)/shard_map/ppermute | solution.py:44
  45.9 2.0 collective-permute-start.17
  47.9 5.5 %collective-permute-done.9.refs_9_ = f32[64,1024]{1,0:T(8,128)} collective-permute-done((f32[64,1024]{1,0:T(8,128)}, f32[64,1024]{1,0:T(8,128)}, u32[]{:S(2)}, u32[]{:S(2)}) %collective-permute-start.9) | collective-permute-done | bytes 262176 | tf_op jit(solution)/shard_map/ppermute | solution.py:44
  53.4 2.2 %collective-permute-start.12 = (f32[64,1024]{1,0:T(8,128)}, f32[64,1024]{1,0:T(8,128)}, u32[]{:S(2)}, u32[]{:S(2)}) collective-permute-start(f32[64,1024]{1,0:T(8,128)} %copy-done.11), channel_id=1, source_target_pairs={{0,28},{1,29},{2,30},{3,31},{4,0},{5,1},{6,2},{7,3},{8,4},{9,5},{1... | collective-permute-start | bytes 786440 | tf_op jit(solution)/shard_map/ppermute | solution.py:44
  55.6 5.6 %collective-permute-start.16 = (f32[1024,256]{1,0:T(8,128)S(1)}, f32[1024,256]{1,0:T(8,128)S(1)}, u32[]{:S(2)}, u32[]{:S(2)}) collective-permute-start(f32[1024,256]{1,0:T(8,128)S(1)} %collective-permute-done.15.refs_35_.refs_36_.refs_37_.refs_38_.refs_39_.refs_40_.refs_41_.refs_42_.refs_43_.refs_44_.refs_22_, ...), channel_id=1, source_target_pairs={{0,1},{1,0},{2,3},{3,2},{4,5},{5,4},{6,7},{7,6},{8,9},{9,8},{10,11... | collective-permute-start | bytes 3145736 | tf_op jit(solution)/shard_map/ppermute | solution.py:44
  61.2 0.2 collective-permute-start.24
  61.4 2.5 %collective-permute-start.27 = (f32[128,1024]{1,0:T(8,128)}, f32[128,1024]{1,0:T(8,128)}, u32[]{:S(2)}, u32[]{:S(2)}) collective-permute-start(f32[128,1024]{1,0:T(8,128)} %collective-permute-done.14.refs_14_), channel_id=1, source_target_pairs={{0,28},{1,29},{2,30},{3,31},{4,0},{5,1},{6,2},{7,3},{8,4},{9,5},{1... | collective-permute-start | bytes 1572872 | tf_op jit(solution)/shard_map/ppermute | solution.py:44
  63.9 0.7 collective-permute-start.10
  64.7 5.0 %collective-permute-done.10.refs_10_ = f32[64,1024]{1,0:T(8,128)S(1)} collective-permute-done((f32[64,1024]{1,0:T(8,128)}, f32[64,1024]{1,0:T(8,128)S(1)}, u32[]{:S(2)}, u32[]{:S(2)}) %collective-permute-start.10) | collective-permute-done | bytes 262176 | tf_op jit(solution)/shard_map/ppermute | solution.py:44
  69.7 0.7 copy-done.13
  70.4 2.9 %collective-permute-start.18 = (f32[128,1024]{1,0:T(8,128)S(1)}, f32[128,1024]{1,0:T(8,128)S(1)}, u32[]{:S(2)}, u32[]{:S(2)}) collective-permute-start(f32[128,1024]{1,0:T(8,128)S(1)} %collective-permute-done.17.refs_56_.refs_35_), channel_id=1, source_target_pairs={{0,128},{1,129},{2,130},{3,131},{4,132},{5,133},{6,134},{7,135},{8... | collective-permute-start | bytes 1572872 | tf_op jit(solution)/shard_map/ppermute | solution.py:44
  73.3 8.0 %collective-permute-done.25.refs_3_ = f32[64,1024]{1,0:T(8,128)} collective-permute-done((f32[64,1024]{1,0:T(8,128)}, f32[64,1024]{1,0:T(8,128)}, u32[]{:S(2)}, u32[]{:S(2)}) %collective-permute-start.25) | collective-permute-done | bytes 262176 | tf_op jit(solution)/shard_map/ppermute | solution.py:44
  81.3 0.7 collective-permute-start.13
  82.1 3.5 %collective-permute-start.28 = (f32[64,1024]{1,0:T(8,128)}, f32[64,1024]{1,0:T(8,128)}, u32[]{:S(2)}, u32[]{:S(2)}) collective-permute-start(f32[64,1024]{1,0:T(8,128)} %collective-permute-done.25.refs_3_), channel_id=1, source_target_pairs={{0,28},{1,29},{2,30},{3,31},{4,0},{5,1},{6,2},{7,3},{8,4},{9,5},{1... | collective-permute-start | bytes 786440 | tf_op jit(solution)/shard_map/ppermute | solution.py:44
  85.5 0.6 stack.48.s_ref
  86.2 2.3 %constant_dynamic-slice_fusion.1.refs_55_.refs_34_ = f32[256,1024]{1,0:T(8,128)} fusion(f32[256,2048]{1,0:T(8,128)} %param.5, s32[]{:T(128)S(6)} %select_n.55), kind=kLoop, calls=%fused_computation.36 | loop fusion | bytes 2097156 | tf_op jit(solution)/shard_map/dynamic_slice | solution.py:197
  88.5 1.7 slice.95
  90.2 1.7 slice.96
  91.8 0.7 collective-permute-start.26
  92.6 0.7 collective-permute-start.23
  93.3 0.7 collective-permute-start.29
  94.1 2.7 %collective-permute-start.31 = (f32[64,1024]{1,0:T(8,128)}, f32[64,1024]{1,0:T(8,128)S(1)}, u32[]{:S(2)}, u32[]{:S(2)}) collective-permute-start(f32[64,1024]{1,0:T(8,128)} %slice.96), channel_id=1, source_target_pairs={{0,28},{1,29},{2,30},{3,31},{4,0},{5,1},{6,2},{7,3},{8,4},{9,5},{1... | collective-permute-start | bytes 786440 | tf_op jit(solution)/shard_map/ppermute | solution.py:44
  96.7 23.0 %shard_map.50 = (f32[640,512]{1,0:T(8,128)}, f32[640,512]{1,0:T(8,128)}, f32[512,1024]{1,0:T(8,128)}) custom-call(s32[5]{0:T(128)} %stack.48.s_ref, f32[64,1024]{1,0:T(8,128)} %copy-done.6, f32[64,1024]{1,0:T(8,128)} %copy-done.10, f32[128,1024]{1,0:T(8,128)} %copy-done.5, f32[64,1024]{1,0:T(8,128)} %collective-permute-done.3.refs_3_, ...), custom_call_target="tpu_custom_call" | custom-call | flops 8053063680 | bytes 9437184 | tf_op jit(solution)/shard_map/pallas_call | solution.py:166
  119.8 3.4 %collective-permute-start.19 = (f32[640,512]{1,0:T(8,128)}, f32[640,512]{1,0:T(8,128)S(1)}, u32[]{:S(2)}, u32[]{:S(2)}) collective-permute-start(f32[640,512]{1,0:T(8,128)} %get-tuple-element.12), channel_id=1, source_target_pairs={{0,1},{1,0},{2,3},{3,2},{4,5},{5,4},{6,7},{7,6},{8,9},{9,8},{10,11... | collective-permute-start | bytes 3932168 | tf_op jit(solution)/shard_map/ppermute | solution.py:44
  123.2 0.7 copy-done.15
  123.9 0.7 copy-done.16
  124.6 16.0 %shard_map.51 = (f32[384,512]{1,0:T(8,128)}, f32[384,512]{1,0:T(8,128)}, f32[128,1024]{1,0:T(8,128)}, f32[128,1024]{1,0:T(8,128)}, f32[128,1024]{1,0:T(8,128)}, /*index=5*/f32[128,1024]{1,0:T(8,128)}) custom-call(s32[5]{0:T(128)} %stack.48.s_ref, f32[64,1024]{1,0:T(8,128)} %collective-permute-done.22.refs_0_, f32[64,1024]{1,0:T(8,128)} %collective-permute-done.23.refs_1_, ...), custom_call_target="tpu_custom_call" | custom-call | flops 4831838208 | bytes 7340032 | tf_op jit(solution)/shard_map/pallas_call | solution.py:166
  140.6 0.1 collective-permute-start.32
  140.8 2.3 %collective-permute-start.36 = (f32[128,1024]{1,0:T(8,128)}, f32[128,1024]{1,0:T(8,128)}, u32[]{:S(2)}, u32[]{:S(2)}) collective-permute-start(f32[128,1024]{1,0:T(8,128)} %get-tuple-element.18), channel_id=1, source_target_pairs={{0,96},{1,97},{2,98},{3,99},{4,100},{5,101},{6,102},{7,103},{8,104... | collective-permute-start | bytes 1572872 | tf_op jit(solution)/shard_map/ppermute | solution.py:44
  143.1 3.1 %collective-permute-start.37 = (f32[128,1024]{1,0:T(8,128)}, f32[128,1024]{1,0:T(8,128)}, u32[]{:S(2)}, u32[]{:S(2)}) collective-permute-start(f32[128,1024]{1,0:T(8,128)} %get-tuple-element.19), channel_id=1, source_target_pairs={{0,224},{1,225},{2,226},{3,227},{4,228},{5,229},{6,230},{7,231},{8... | collective-permute-start | bytes 1572872 | tf_op jit(solution)/shard_map/ppermute | solution.py:44
  146.2 1.8 slice_add_fusion.2
  148.0 1.3 collective-permute-start.33
  149.3 0.9 slice_add_fusion
  150.3 0.2 collective-permute-start.20
  150.4 5.0 %collective-permute-done.36 = f32[128,1024]{1,0:T(8,128)} collective-permute-done((f32[128,1024]{1,0:T(8,128)}, f32[128,1024]{1,0:T(8,128)}, u32[]{:S(2)}, u32[]{:S(2)}) %collective-permute-start.36) | collective-permute-done | bytes 524320 | tf_op jit(solution)/shard_map/ppermute | solution.py:44
  155.4 13.9 %collective-permute-done.37 = f32[128,1024]{1,0:T(8,128)} collective-permute-done((f32[128,1024]{1,0:T(8,128)}, f32[128,1024]{1,0:T(8,128)}, u32[]{:S(2)}, u32[]{:S(2)}) %collective-permute-start.37) | collective-permute-done | bytes 524320 | tf_op jit(solution)/shard_map/ppermute | solution.py:44
  169.4 1.3 add.78
  170.6 1.1 collective-permute-done.35
  171.7 1.1 add.77
  172.8 5.7 %collective-permute-done.33 = f32[192,512]{1,0:T(8,128)} collective-permute-done((f32[192,512]{1,0:T(8,128)}, f32[192,512]{1,0:T(8,128)}, u32[]{:S(2)}, u32[]{:S(2)}) %collective-permute-start.33) | collective-permute-done | bytes 393248 | tf_op jit(solution)/shard_map/ppermute | solution.py:44
  178.5 1.1 fusion.1
  179.7 2.3 %collective-permute-start.34 = (f32[192,256]{1,0:T(8,128)S(1)}, f32[192,256]{1,0:T(8,128)S(1)}, u32[]{:S(2)}, u32[]{:S(2)}) collective-permute-start(f32[192,256]{1,0:T(8,128)S(1)} %slice.100), channel_id=1, source_target_pairs={{0,96},{1,97},{2,98},{3,99},{4,100},{5,101},{6,102},{7,103},{8,104... | collective-permute-start | bytes 589832 | tf_op jit(solution)/shard_map/ppermute | solution.py:44
  182.0 10.6 %collective-permute-done.20 = f32[320,512]{1,0:T(8,128)} collective-permute-done((f32[320,512]{1,0:T(8,128)}, f32[320,512]{1,0:T(8,128)}, u32[]{:S(2)}, u32[]{:S(2)}) %collective-permute-start.20) | collective-permute-done | bytes 655392 | tf_op jit(solution)/shard_map/ppermute | solution.py:44
  192.6 1.3 fusion
  193.9 2.3 %collective-permute-start.21 = (f32[320,256]{1,0:T(8,128)S(1)}, f32[320,256]{1,0:T(8,128)S(1)}, u32[]{:S(2)}, u32[]{:S(2)}) collective-permute-start(f32[320,256]{1,0:T(8,128)S(1)} %slice.91), channel_id=1, source_target_pairs={{0,96},{1,97},{2,98},{3,99},{4,100},{5,101},{6,102},{7,103},{8,104... | collective-permute-start | bytes 983048 | tf_op jit(solution)/shard_map/ppermute | solution.py:44
  196.2 1.1 maximum_select_fusion
  197.4 5.2 %collective-permute-done.21 = f32[320,256]{1,0:T(8,128)S(1)} collective-permute-done((f32[320,256]{1,0:T(8,128)S(1)}, f32[320,256]{1,0:T(8,128)S(1)}, u32[]{:S(2)}, u32[]{:S(2)}) %collective-permute-start.21) | collective-permute-done | bytes 327712 | tf_op jit(solution)/shard_map/ppermute | solution.py:44
  202.9 0.8 constant_dynamic-slice_fusion
  (85 shorter events, 0.5 us)
Async XLA Ops:
  1.8 22.1 %copy-start.6 = (f32[64,1024]{1,0:T(8,128)}, f32[64,1024]{1,0:T(8,128)S(1)}, u32[]{:S(2)}) copy-start(f32[64,1024]{1,0:T(8,128)S(1)} %get-tuple-element.21.refs_0_) | copy-start | bytes 786436
  1.8 8.4 %collective-permute-start.1 = (f32[64,1024]{1,0:T(8,128)S(1)}, f32[64,1024]{1,0:T(8,128)S(1)}, u32[]{:S(2)}, u32[]{:S(2)}) collective-permute-start(f32[64,1024]{1,0:T(8,128)S(1)} %get-tuple-element.20), channel_id=1, source_target_pairs={{0,96},{1,97},{2,98},{3,99},{4,100},{5,101},{6,102},{7,103},{8,104... | collective-permute-start | bytes 786440 | tf_op jit(solution)/shard_map/ppermute | solution.py:44
  10.1 5.7 %collective-permute-start.2 = (f32[64,1024]{1,0:T(8,128)S(1)}, f32[64,1024]{1,0:T(8,128)S(1)}, u32[]{:S(2)}, u32[]{:S(2)}) collective-permute-start(f32[64,1024]{1,0:T(8,128)S(1)} %collective-permute-done.1), channel_id=1, source_target_pairs={{0,32},{1,33},{2,34},{3,35},{4,36},{5,37},{6,38},{7,39},{8,40},{9,... | collective-permute-start | bytes 786440 | tf_op jit(solution)/shard_map/ppermute | solution.py:44
  12.4 43.2 %collective-permute-start.15 = (f32[1024,256]{1,0:T(8,128)S(1)}, f32[1024,256]{1,0:T(8,128)S(1)}, u32[]{:S(2)}, u32[]{:S(2)}) collective-permute-start(f32[1024,256]{1,0:T(8,128)S(1)} %bitcast.59), channel_id=1, source_target_pairs={{0,96},{1,97},{2,98},{3,99},{4,100},{5,101},{6,102},{7,103},{8,104... | collective-permute-start | bytes 3145736 | tf_op jit(solution)/shard_map/ppermute | solution.py:44
  14.9 8.9 %collective-permute-start = (f32[64,1024]{1,0:T(8,128)S(1)}, f32[64,1024]{1,0:T(8,128)S(1)}, u32[]{:S(2)}, u32[]{:S(2)}) collective-permute-start(f32[64,1024]{1,0:T(8,128)S(1)} %get-tuple-element.21.refs_0_), channel_id=1, source_target_pairs={{0,32},{1,33},{2,34},{3,35},{4,36},{5,37},{6,38},{7,39},{8,40},{9,... | collective-permute-start | bytes 786440 | tf_op jit(solution)/shard_map/ppermute | solution.py:44
  15.9 3.3 %copy-start.5 = (f32[128,1024]{1,0:T(8,128)}, f32[128,1024]{1,0:T(8,128)S(1)}, u32[]{:S(2)}) copy-start(f32[128,1024]{1,0:T(8,128)S(1)} %constant_dynamic-update-slice_fusion.refs_2_) | copy-start | bytes 1572868
  15.9 22.5 %collective-permute-start.5 = (f32[128,1024]{1,0:T(8,128)S(1)}, f32[128,1024]{1,0:T(8,128)S(1)}, u32[]{:S(2)}, u32[]{:S(2)}) collective-permute-start(f32[128,1024]{1,0:T(8,128)S(1)} %constant_dynamic-update-slice_fusion.refs_2_), channel_id=1, source_target_pairs={{0,4},{1,5},{2,6},{3,7},{4,8},{5,9},{6,10},{7,11},{8,12},{9,13},{1... | collective-permute-start | bytes 1572872 | tf_op jit(solution)/shard_map/ppermute | solution.py:44
  19.2 19.2 %collective-permute-start.8 = (f32[128,1024]{1,0:T(8,128)S(1)}, f32[128,1024]{1,0:T(8,128)}, u32[]{:S(2)}, u32[]{:S(2)}) collective-permute-start(f32[128,1024]{1,0:T(8,128)S(1)} %constant_dynamic-update-slice_fusion.refs_2_), channel_id=1, source_target_pairs={{0,28},{1,29},{2,30},{3,31},{4,0},{5,1},{6,2},{7,3},{8,4},{9,5},{1... | collective-permute-start | bytes 1572872 | tf_op jit(solution)/shard_map/ppermute | solution.py:44
  23.8 13.1 %collective-permute-start.3 = (f32[64,1024]{1,0:T(8,128)S(1)}, f32[64,1024]{1,0:T(8,128)}, u32[]{:S(2)}, u32[]{:S(2)}) collective-permute-start(f32[64,1024]{1,0:T(8,128)S(1)} %get-tuple-element.21.refs_0_), channel_id=1, source_target_pairs={{0,4},{1,5},{2,6},{3,7},{4,8},{5,9},{6,10},{7,11},{8,12},{9,13},{1... | collective-permute-start | bytes 786440 | tf_op jit(solution)/shard_map/ppermute | solution.py:44
  23.8 19.7 %copy-start.10 = (f32[64,1024]{1,0:T(8,128)}, f32[64,1024]{1,0:T(8,128)S(1)}, u32[]{:S(2)}) copy-start(f32[64,1024]{1,0:T(8,128)S(1)} %collective-permute-done.refs_1_) | copy-start | bytes 786436
  23.8 13.8 %collective-permute-start.6 = (f32[64,1024]{1,0:T(8,128)S(1)}, f32[64,1024]{1,0:T(8,128)S(1)}, u32[]{:S(2)}, u32[]{:S(2)}) collective-permute-start(f32[64,1024]{1,0:T(8,128)S(1)} %get-tuple-element.21.refs_0_), channel_id=1, source_target_pairs={{0,28},{1,29},{2,30},{3,31},{4,0},{5,1},{6,2},{7,3},{8,4},{9,5},{1... | collective-permute-start | bytes 786440 | tf_op jit(solution)/shard_map/ppermute | solution.py:44
  36.9 5.5 %collective-permute-start.4 = (f32[64,1024]{1,0:T(8,128)}, f32[64,1024]{1,0:T(8,128)}, u32[]{:S(2)}, u32[]{:S(2)}) collective-permute-start(f32[64,1024]{1,0:T(8,128)} %collective-permute-done.3.refs_3_), channel_id=1, source_target_pairs={{0,32},{1,33},{2,34},{3,35},{4,36},{5,37},{6,38},{7,39},{8,40},{9,... | collective-permute-start | bytes 786440 | tf_op jit(solution)/shard_map/ppermute | solution.py:44
  37.6 5.9 %copy-start.11 = (f32[64,1024]{1,0:T(8,128)}, f32[64,1024]{1,0:T(8,128)S(1)}, u32[]{:S(2)}) copy-start(f32[64,1024]{1,0:T(8,128)S(1)} %collective-permute-done.6.refs_6_) | copy-start | bytes 786436
  37.6 8.2 %collective-permute-start.7 = (f32[64,1024]{1,0:T(8,128)S(1)}, f32[64,1024]{1,0:T(8,128)S(1)}, u32[]{:S(2)}, u32[]{:S(2)}) collective-permute-start(f32[64,1024]{1,0:T(8,128)S(1)} %collective-permute-done.6.refs_6_), channel_id=1, source_target_pairs={{0,32},{1,33},{2,34},{3,35},{4,36},{5,37},{6,38},{7,39},{8,40},{9,... | collective-permute-start | bytes 786440 | tf_op jit(solution)/shard_map/ppermute | solution.py:44
  38.4 26.3 %copy-start.8 = (f32[128,1024]{1,0:T(8,128)}, f32[128,1024]{1,0:T(8,128)S(1)}, u32[]{:S(2)}) copy-start(f32[128,1024]{1,0:T(8,128)S(1)} %collective-permute-done.5.refs_5_) | copy-start | bytes 1572868
  38.4 22.8 %collective-permute-start.11 = (f32[128,1024]{1,0:T(8,128)S(1)}, f32[128,1024]{1,0:T(8,128)}, u32[]{:S(2)}, u32[]{:S(2)}) collective-permute-start(f32[128,1024]{1,0:T(8,128)S(1)} %collective-permute-done.5.refs_5_), channel_id=1, source_target_pairs={{0,4},{1,5},{2,6},{3,7},{4,8},{5,9},{6,10},{7,11},{8,12},{9,13},{1... | collective-permute-start | bytes 1572872 | tf_op jit(solution)/shard_map/ppermute | solution.py:44
  38.4 23.0 %collective-permute-start.14 = (f32[128,1024]{1,0:T(8,128)}, f32[128,1024]{1,0:T(8,128)}, u32[]{:S(2)}, u32[]{:S(2)}) collective-permute-start(f32[128,1024]{1,0:T(8,128)} %collective-permute-done.8.refs_8_), channel_id=1, source_target_pairs={{0,28},{1,29},{2,30},{3,31},{4,0},{5,1},{6,2},{7,3},{8,4},{9,5},{1... | collective-permute-start | bytes 1572872 | tf_op jit(solution)/shard_map/ppermute | solution.py:44
  42.4 11.0 %collective-permute-start.9 = (f32[64,1024]{1,0:T(8,128)}, f32[64,1024]{1,0:T(8,128)}, u32[]{:S(2)}, u32[]{:S(2)}) collective-permute-start(f32[64,1024]{1,0:T(8,128)} %collective-permute-done.3.refs_3_), channel_id=1, source_target_pairs={{0,4},{1,5},{2,6},{3,7},{4,8},{5,9},{6,10},{7,11},{8,12},{9,13},{1... | collective-permute-start | bytes 786440 | tf_op jit(solution)/shard_map/ppermute | solution.py:44
  45.9 44.3 %copy-start.12 = (f32[64,1024]{1,0:T(8,128)}, f32[64,1024]{1,0:T(8,128)S(1)}, u32[]{:S(2)}) copy-start(f32[64,1024]{1,0:T(8,128)S(1)} %collective-permute-done.7.refs_7_) | copy-start | bytes 786436
  45.9 18.7 %collective-permute-start.17 = (f32[128,1024]{1,0:T(8,128)S(1)}, f32[128,1024]{1,0:T(8,128)S(1)}, u32[]{:S(2)}, u32[]{:S(2)}) collective-permute-start(f32[128,1024]{1,0:T(8,128)S(1)} %dynamic_slice.23), channel_id=1, source_target_pairs={{0,96},{1,97},{2,98},{3,99},{4,100},{5,101},{6,102},{7,103},{8,104... | collective-permute-start | bytes 1572872 | tf_op jit(solution)/shard_map/ppermute | solution.py:44
  53.4 10.5 %collective-permute-start.12 = (f32[64,1024]{1,0:T(8,128)}, f32[64,1024]{1,0:T(8,128)}, u32[]{:S(2)}, u32[]{:S(2)}) collective-permute-start(f32[64,1024]{1,0:T(8,128)} %copy-done.11), channel_id=1, source_target_pairs={{0,28},{1,29},{2,30},{3,31},{4,0},{5,1},{6,2},{7,3},{8,4},{9,5},{1... | collective-permute-start | bytes 786440 | tf_op jit(solution)/shard_map/ppermute | solution.py:44
  55.6 34.5 %copy-start = (f32[1024,256]{1,0:T(8,128)}, f32[1024,256]{1,0:T(8,128)S(1)}, u32[]{:S(2)}) copy-start(f32[1024,256]{1,0:T(8,128)S(1)} %collective-permute-done.15.refs_35_.refs_36_.refs_37_.refs_38_.refs_39_.refs_40_.refs_41_.refs_42_.refs_43_.refs_44_.refs_22_.refs_23_.refs_24_.refs_25_.refs_26_.refs_27_) | copy-start | bytes 3145732
  55.6 38.5 %collective-permute-start.16 = (f32[1024,256]{1,0:T(8,128)S(1)}, f32[1024,256]{1,0:T(8,128)S(1)}, u32[]{:S(2)}, u32[]{:S(2)}) collective-permute-start(f32[1024,256]{1,0:T(8,128)S(1)} %collective-permute-done.15.refs_35_.refs_36_.refs_37_.refs_38_.refs_39_.refs_40_.refs_41_.refs_42_.refs_43_.refs_44_.refs_22_, ...), channel_id=1, source_target_pairs={{0,1},{1,0},{2,3},{3,2},{4,5},{5,4},{6,7},{7,6},{8,9},{9,8},{10,11... | collective-permute-start | bytes 3145736 | tf_op jit(solution)/shard_map/ppermute | solution.py:44
  61.2 20.9 %collective-permute-start.24 = (f32[128,1024]{1,0:T(8,128)}, f32[128,1024]{1,0:T(8,128)}, u32[]{:S(2)}, u32[]{:S(2)}) collective-permute-start(f32[128,1024]{1,0:T(8,128)} %collective-permute-done.11.refs_11_), channel_id=1, source_target_pairs={{0,4},{1,5},{2,6},{3,7},{4,8},{5,9},{6,10},{7,11},{8,12},{9,13},{1... | collective-permute-start | bytes 1572872 | tf_op jit(solution)/shard_map/ppermute | solution.py:44
  61.4 20.7 %collective-permute-start.27 = (f32[128,1024]{1,0:T(8,128)}, f32[128,1024]{1,0:T(8,128)}, u32[]{:S(2)}, u32[]{:S(2)}) collective-permute-start(f32[128,1024]{1,0:T(8,128)} %collective-permute-done.14.refs_14_), channel_id=1, source_target_pairs={{0,28},{1,29},{2,30},{3,31},{4,0},{5,1},{6,2},{7,3},{8,4},{9,5},{1... | collective-permute-start | bytes 1572872 | tf_op jit(solution)/shard_map/ppermute | solution.py:44
  63.9 5.8 %collective-permute-start.10 = (f32[64,1024]{1,0:T(8,128)}, f32[64,1024]{1,0:T(8,128)S(1)}, u32[]{:S(2)}, u32[]{:S(2)}) collective-permute-start(f32[64,1024]{1,0:T(8,128)} %collective-permute-done.9.refs_9_), channel_id=1, source_target_pairs={{0,32},{1,33},{2,34},{3,35},{4,36},{5,37},{6,38},{7,39},{8,40},{9,... | collective-permute-start | bytes 786440 | tf_op jit(solution)/shard_map/ppermute | solution.py:44
  64.6 25.6 %copy-start.2 = (f32[128,1024]{1,0:T(8,128)}, f32[128,1024]{1,0:T(8,128)S(1)}, u32[]{:S(2)}) copy-start(f32[128,1024]{1,0:T(8,128)S(1)} %collective-permute-done.17.refs_56_.refs_35_) | copy-start | bytes 1572868
  64.6 16.7 %collective-permute-start.25 = (f32[64,1024]{1,0:T(8,128)}, f32[64,1024]{1,0:T(8,128)}, u32[]{:S(2)}, u32[]{:S(2)}) collective-permute-start(f32[64,1024]{1,0:T(8,128)} %collective-permute-done.12.refs_12_), channel_id=1, source_target_pairs={{0,28},{1,29},{2,30},{3,31},{4,0},{5,1},{6,2},{7,3},{8,4},{9,5},{1... | collective-permute-start | bytes 786440 | tf_op jit(solution)/shard_map/ppermute | solution.py:44
  69.7 0.7 copy-start.13
  70.4 23.6 %collective-permute-start.18 = (f32[128,1024]{1,0:T(8,128)S(1)}, f32[128,1024]{1,0:T(8,128)S(1)}, u32[]{:S(2)}, u32[]{:S(2)}) collective-permute-start(f32[128,1024]{1,0:T(8,128)S(1)} %collective-permute-done.17.refs_56_.refs_35_), channel_id=1, source_target_pairs={{0,128},{1,129},{2,130},{3,131},{4,132},{5,133},{6,134},{7,135},{8... | collective-permute-start | bytes 1572872 | tf_op jit(solution)/shard_map/ppermute | solution.py:44
  81.3 10.5 %collective-permute-start.13 = (f32[64,1024]{1,0:T(8,128)}, f32[64,1024]{1,0:T(8,128)}, u32[]{:S(2)}, u32[]{:S(2)}) collective-permute-start(f32[64,1024]{1,0:T(8,128)} %collective-permute-done.12.refs_12_), channel_id=1, source_target_pairs={{0,32},{1,33},{2,34},{3,35},{4,36},{5,37},{6,38},{7,39},{8,40},{9,... | collective-permute-start | bytes 786440 | tf_op jit(solution)/shard_map/ppermute | solution.py:44
  82.1 10.5 %collective-permute-start.22 = (f32[64,1024]{1,0:T(8,128)}, f32[64,1024]{1,0:T(8,128)}, u32[]{:S(2)}, u32[]{:S(2)}) collective-permute-start(f32[64,1024]{1,0:T(8,128)} %collective-permute-done.9.refs_9_), channel_id=1, source_target_pairs={{0,4},{1,5},{2,6},{3,7},{4,8},{5,9},{6,10},{7,11},{8,12},{9,13},{1... | collective-permute-start | bytes 786440 | tf_op jit(solution)/shard_map/ppermute | solution.py:44
  82.1 11.2 %collective-permute-start.28 = (f32[64,1024]{1,0:T(8,128)}, f32[64,1024]{1,0:T(8,128)}, u32[]{:S(2)}, u32[]{:S(2)}) collective-permute-start(f32[64,1024]{1,0:T(8,128)} %collective-permute-done.25.refs_3_), channel_id=1, source_target_pairs={{0,28},{1,29},{2,30},{3,31},{4,0},{5,1},{6,2},{7,3},{8,4},{9,5},{1... | collective-permute-start | bytes 786440 | tf_op jit(solution)/shard_map/ppermute | solution.py:44
  91.8 31.3 %collective-permute-start.26 = (f32[64,1024]{1,0:T(8,128)}, f32[64,1024]{1,0:T(8,128)S(1)}, u32[]{:S(2)}, u32[]{:S(2)}) collective-permute-start(f32[64,1024]{1,0:T(8,128)} %collective-permute-done.25.refs_3_), channel_id=1, source_target_pairs={{0,32},{1,33},{2,34},{3,35},{4,36},{5,37},{6,38},{7,39},{8,40},{9,... | collective-permute-start | bytes 786440 | tf_op jit(solution)/shard_map/ppermute | solution.py:44
  92.6 27.2 %collective-permute-start.23 = (f32[64,1024]{1,0:T(8,128)}, f32[64,1024]{1,0:T(8,128)}, u32[]{:S(2)}, u32[]{:S(2)}) collective-permute-start(f32[64,1024]{1,0:T(8,128)} %collective-permute-done.22.refs_0_), channel_id=1, source_target_pairs={{0,32},{1,33},{2,34},{3,35},{4,36},{5,37},{6,38},{7,39},{8,40},{9,... | collective-permute-start | bytes 786440 | tf_op jit(solution)/shard_map/ppermute | solution.py:44
  93.3 29.9 %collective-permute-start.29 = (f32[64,1024]{1,0:T(8,128)}, f32[64,1024]{1,0:T(8,128)}, u32[]{:S(2)}, u32[]{:S(2)}) collective-permute-start(f32[64,1024]{1,0:T(8,128)} %collective-permute-done.28.refs_6_), channel_id=1, source_target_pairs={{0,32},{1,33},{2,34},{3,35},{4,36},{5,37},{6,38},{7,39},{8,40},{9,... | collective-permute-start | bytes 786440 | tf_op jit(solution)/shard_map/ppermute | solution.py:44
  94.0 2.7 %copy-start.3 = (f32[128,1024]{1,0:T(8,128)}, f32[128,1024]{1,0:T(8,128)S(1)}, u32[]{:S(2)}) copy-start(f32[128,1024]{1,0:T(8,128)S(1)} %collective-permute-done.18.refs_57_.refs_36_) | copy-start | bytes 1572868
  94.0 29.1 %collective-permute-start.30 = (f32[64,1024]{1,0:T(8,128)}, f32[64,1024]{1,0:T(8,128)S(1)}, u32[]{:S(2)}, u32[]{:S(2)}) collective-permute-start(f32[64,1024]{1,0:T(8,128)} %slice.95), channel_id=1, source_target_pairs={{0,4},{1,5},{2,6},{3,7},{4,8},{5,9},{6,10},{7,11},{8,12},{9,13},{1... | collective-permute-start | bytes 786440 | tf_op jit(solution)/shard_map/ppermute | solution.py:44
  94.1 2.7 %copy-start.1 = (f32[1024,256]{1,0:T(8,128)}, f32[1024,256]{1,0:T(8,128)S(1)}, u32[]{:S(2)}) copy-start(f32[1024,256]{1,0:T(8,128)S(1)} %collective-permute-done.16.refs_45_.refs_46_.refs_47_.refs_48_.refs_49_.refs_50_.refs_51_.refs_52_.refs_53_.refs_54_.refs_28_.refs_29_.refs_30_.refs_31_.refs_32_.refs_33_) | copy-start | bytes 3145732
  94.1 29.1 %collective-permute-start.31 = (f32[64,1024]{1,0:T(8,128)}, f32[64,1024]{1,0:T(8,128)S(1)}, u32[]{:S(2)}, u32[]{:S(2)}) collective-permute-start(f32[64,1024]{1,0:T(8,128)} %slice.96), channel_id=1, source_target_pairs={{0,28},{1,29},{2,30},{3,31},{4,0},{5,1},{6,2},{7,3},{8,4},{9,5},{1... | collective-permute-start | bytes 786440 | tf_op jit(solution)/shard_map/ppermute | solution.py:44
  119.8 29.5 %collective-permute-start.19 = (f32[640,512]{1,0:T(8,128)}, f32[640,512]{1,0:T(8,128)S(1)}, u32[]{:S(2)}, u32[]{:S(2)}) collective-permute-start(f32[640,512]{1,0:T(8,128)} %get-tuple-element.12), channel_id=1, source_target_pairs={{0,1},{1,0},{2,3},{3,2},{4,5},{5,4},{6,7},{7,6},{8,9},{9,8},{10,11... | collective-permute-start | bytes 3932168 | tf_op jit(solution)/shard_map/ppermute | solution.py:44
  123.2 1.5 copy-start.14
  123.2 0.8 copy-start.15
  123.9 0.7 copy-start.16
  124.6 24.7 %copy-start.4 = (f32[640,512]{1,0:T(8,128)S(1)}, f32[640,512]{1,0:T(8,128)}, u32[]{:S(2)}) copy-start(f32[640,512]{1,0:T(8,128)} %get-tuple-element.11) | copy-start | bytes 3932164
  140.6 5.6 %collective-permute-start.32 = (f32[384,512]{1,0:T(8,128)}, f32[384,512]{1,0:T(8,128)S(1)}, u32[]{:S(2)}, u32[]{:S(2)}) collective-permute-start(f32[384,512]{1,0:T(8,128)} %get-tuple-element.15), channel_id=1, source_target_pairs={{0,1},{1,0},{2,3},{3,2},{4,5},{5,4},{6,7},{7,6},{8,9},{9,8},{10,11... | collective-permute-start | bytes 2359304 | tf_op jit(solution)/shard_map/ppermute | solution.py:44
  140.8 14.6 %collective-permute-start.36 = (f32[128,1024]{1,0:T(8,128)}, f32[128,1024]{1,0:T(8,128)}, u32[]{:S(2)}, u32[]{:S(2)}) collective-permute-start(f32[128,1024]{1,0:T(8,128)} %get-tuple-element.18), channel_id=1, source_target_pairs={{0,96},{1,97},{2,98},{3,99},{4,100},{5,101},{6,102},{7,103},{8,104... | collective-permute-start | bytes 1572872 | tf_op jit(solution)/shard_map/ppermute | solution.py:44
  143.1 26.3 %collective-permute-start.37 = (f32[128,1024]{1,0:T(8,128)}, f32[128,1024]{1,0:T(8,128)}, u32[]{:S(2)}, u32[]{:S(2)}) collective-permute-start(f32[128,1024]{1,0:T(8,128)} %get-tuple-element.19), channel_id=1, source_target_pairs={{0,224},{1,225},{2,226},{3,227},{4,228},{5,229},{6,230},{7,231},{8... | collective-permute-start | bytes 1572872 | tf_op jit(solution)/shard_map/ppermute | solution.py:44
  146.2 25.6 %collective-permute-start.35 = (f32[128,1024]{1,0:T(8,128)}, f32[128,1024]{1,0:T(8,128)}, u32[]{:S(2)}, u32[]{:S(2)}) collective-permute-start(f32[128,1024]{1,0:T(8,128)} %get-tuple-element.17), channel_id=1, source_target_pairs={{0,128},{1,129},{2,130},{3,131},{4,132},{5,133},{6,134},{7,135},{8... | collective-permute-start | bytes 1572872 | tf_op jit(solution)/shard_map/ppermute | solution.py:44
  148.0 30.5 %collective-permute-start.33 = (f32[192,512]{1,0:T(8,128)}, f32[192,512]{1,0:T(8,128)}, u32[]{:S(2)}, u32[]{:S(2)}) collective-permute-start(f32[192,512]{1,0:T(8,128)} %slice_add_fusion.2), channel_id=1, source_target_pairs={{0,2},{1,3},{2,0},{3,1},{4,6},{5,7},{6,4},{7,5},{8,10},{9,11},{10,... | collective-permute-start | bytes 1179656 | tf_op jit(solution)/shard_map/ppermute | solution.py:44
  150.3 42.3 %collective-permute-start.20 = (f32[320,512]{1,0:T(8,128)}, f32[320,512]{1,0:T(8,128)}, u32[]{:S(2)}, u32[]{:S(2)}) collective-permute-start(f32[320,512]{1,0:T(8,128)} %slice_add_fusion), channel_id=1, source_target_pairs={{0,2},{1,3},{2,0},{3,1},{4,6},{5,7},{6,4},{7,5},{8,10},{9,11},{10,... | collective-permute-start | bytes 1966088 | tf_op jit(solution)/shard_map/ppermute | solution.py:44
  150.4 21.3 %copy-start.9 = (f32[128,1024]{1,0:T(8,128)S(1)}, f32[128,1024]{1,0:T(8,128)}, u32[]{:S(2)}) copy-start(f32[128,1024]{1,0:T(8,128)} %get-tuple-element.16) | copy-start | bytes 1572868
  150.4 28.1 %copy-start.7 = (f32[384,512]{1,0:T(8,128)S(1)}, f32[384,512]{1,0:T(8,128)}, u32[]{:S(2)}) copy-start(f32[384,512]{1,0:T(8,128)} %get-tuple-element.14) | copy-start | bytes 2359300
  179.7 17.7 %collective-permute-start.34 = (f32[192,256]{1,0:T(8,128)S(1)}, f32[192,256]{1,0:T(8,128)S(1)}, u32[]{:S(2)}, u32[]{:S(2)}) collective-permute-start(f32[192,256]{1,0:T(8,128)S(1)} %slice.100), channel_id=1, source_target_pairs={{0,96},{1,97},{2,98},{3,99},{4,100},{5,101},{6,102},{7,103},{8,104... | collective-permute-start | bytes 589832 | tf_op jit(solution)/shard_map/ppermute | solution.py:44
  193.9 8.7 %collective-permute-start.21 = (f32[320,256]{1,0:T(8,128)S(1)}, f32[320,256]{1,0:T(8,128)S(1)}, u32[]{:S(2)}, u32[]{:S(2)}) collective-permute-start(f32[320,256]{1,0:T(8,128)S(1)} %slice.91), channel_id=1, source_target_pairs={{0,96},{1,97},{2,98},{3,99},{4,100},{5,101},{6,102},{7,103},{8,104... | collective-permute-start | bytes 983048 | tf_op jit(solution)/shard_map/ppermute | solution.py:44

commit v3 on v2

v3 whole, which is shorter than its diff:
```python
import functools

import jax
import jax.numpy as jnp
from jax import lax
from jax.experimental import pallas as pl
from jax.experimental.pallas import tpu as pltpu
from jax.sharding import PartitionSpec as P

AXES = ("tok", "fin", "fout")
NX, NZ = 4, 8
ROWS = 64
COLS = 1024
FEAT = 256
GROUPS = ((0, 7, 1, 6, 2), (5, 3, 4))
TILES = (256, 256)


def pairs(move):
    out = []
    for t in range(2):
        for x in range(NX):
            for z in range(NZ):
                for y in range(2):
                    for c in range(2):
                        a, b, d, e, f = move(t, x, z, y, c)
                        src = (t * NX * NZ + x * NZ + z) * 4 + 2 * y + c
                        dst = (a * NX * NZ + b * NZ + d % NZ) * 4 + 2 * e + f
                        out.append((src, dst))
    return out


ZUP = pairs(lambda t, x, z, y, c: (t, x, z + 1, y, c))
ZDOWN = pairs(lambda t, x, z, y, c: (t, x, z - 1 + NZ, y, c))
SIDE = pairs(lambda t, x, z, y, c: (t, x ^ 1, z, y, c))
MATE = pairs(lambda t, x, z, y, c: (t, x ^ 3, z, y, c))
CORE = pairs(lambda t, x, z, y, c: (t, x, z, y, 1 - c))
YLOW = pairs(lambda t, x, z, y, c: (t, x, z, 1 - y, c))
TOK = pairs(lambda t, x, z, y, c: (1 - t, x, z, y, c))
DIAG = pairs(lambda t, x, z, y, c: (1 - t, x ^ 3, z, y, c))


def send(value, perm):
    return lax.ppermute(value, AXES, perm)


def split(v):
    hi = v.astype(jnp.bfloat16)
    lo = (v - hi.astype(jnp.float32)).astype(jnp.bfloat16)
    return hi, lo


def dot(a, b, dims):
    return lax.dot_general(a, b, (dims, ((), ())), preferred_element_type=jnp.float32)


def group_body(layout, turns, tile, first, last, s_ref, *refs):
    refs = list(refs)
    take = lambda k: [refs.pop(0) for _ in range(k)]
    pieces = take(len(layout))
    a_own, a_near, a_far, w_own, w_a, w_b = take(6)
    wg_in = None if first else take(1)[0]
    keep_ref, send_ref = take(2)
    wg_refs = take(4 if last else 1)
    gl, thi, tlo, wcat = refs
    n = len(turns)
    span = n * ROWS
    spin, tok, fout, z, y = (s_ref[k] for k in range(5))
    nt = ((1,), (1,))
    nn = ((1,), (0,))

    def rows_of(ref, where, r):
        at = (where * NZ + lax.rem(z + r, NZ)) * ROWS
        return ref[pl.ds(pl.multiple_of(at, ROWS), ROWS), :]

    slots = [(cr, yr, r) for cr in range(2) for yr in range(2) for r in turns]
    for g in range(n):
        four = slots[4 * g : 4 * g + 4]
        own = [rows_of(a_own, fout ^ (cr | yr << 1), r) for cr, yr, r in four]
        mate = [rows_of(a_far if cr else a_near, y ^ yr, r) for cr, yr, r in four]
        for base, blocks in ((0, own), (FEAT, mate)):
            hi, lo = split(jnp.concatenate(blocks, axis=0).T)
            thi[pl.ds(base, FEAT), pl.ds(g * 256, 256)] = hi
            tlo[pl.ds(base, FEAT), pl.ds(g * 256, 256)] = lo

    keep_ref[...] = jnp.zeros_like(keep_ref)
    send_ref[...] = jnp.zeros_like(send_ref)
    mine = lambda base: pl.ds(pl.multiple_of(base + tok * 128, 128), 128)
    other = lambda base: pl.ds(pl.multiple_of(base + (1 - tok) * 128, 128), 128)
    high, low = pl.ds(0, tile), pl.ds(tile, tile)

    @pl.loop(0, COLS // tile)
    def _(step):
        cols = pl.ds(pl.multiple_of(step * tile, tile), tile)
        for ref, parts in zip(pieces, layout):
            for start, e, k in parts:
                v = spin ^ e
                slot = (v & 1) * 2 + (v >> 1)
                hi, lo = split(ref[pl.ds(start, ROWS), cols])
                rows = pl.ds(pl.multiple_of(slot * span + k * ROWS, ROWS), ROWS)
                gl[rows, high] = hi
                gl[rows, low] = lo
        wcat[pl.ds(0, FEAT), :] = w_own[:, cols]
        wcat[mine(FEAT), :] = w_a[:, cols]
        wcat[other(FEAT), :] = w_b[:, cols]
        whi, wlo = split(wcat[...])
        w2 = jnp.concatenate([whi, whi], axis=1)
        sums = dot(gl[...], w2, nt) + dot(gl[:, high], wlo, nt)
        keep_ref[...] += sums[: 2 * span]
        send_ref[...] += sums[2 * span :]
        acc = dot(thi[...], gl[:, high], nn) + dot(thi[...], gl[:, low], nn) + dot(tlo[...], gl[:, high], nn)
        if not first:
            acc = acc + wg_in[:, cols]
        if last:
            wcat[...] = acc
            wg_refs[0][:, cols] = wcat[mine(0), :]
            wg_refs[1][:, cols] = wcat[other(0), :]
            wg_refs[2][:, cols] = wcat[mine(FEAT), :]
            wg_refs[3][:, cols] = wcat[other(FEAT), :]
        else:
            wg_refs[0][:, cols] = acc


def group(index, scalars, pieces, layout, acts, weights, wg):
    turns, tile = GROUPS[index], TILES[index]
    first, last = wg is None, index == len(GROUPS) - 1
    span = len(turns) * ROWS
    rows = 4 * span
    args = [scalars, *pieces, *acts, *weights]
    if not first:
        args.append(wg)
    vmem = pl.BlockSpec(memory_space=pltpu.VMEM)
    share = jax.ShapeDtypeStruct((2 * span, 2 * FEAT), jnp.float32)
    if last:
        grads = [jax.ShapeDtypeStruct((128, COLS), jnp.float32)] * 4
    else:
        grads = [jax.ShapeDtypeStruct((2 * FEAT, COLS), jnp.float32)]
    return pl.pallas_call(
        functools.partial(group_body, layout, turns, tile, first, last),
        in_specs=[pl.BlockSpec(memory_space=pltpu.SMEM)] + [vmem] * (len(args) - 1),
        out_specs=[vmem] * (2 + len(grads)),
        out_shape=[share, share, *grads],
        scratch_shapes=[pltpu.VMEM((rows, 2 * tile), jnp.bfloat16)]
        + [pltpu.VMEM((2 * FEAT, rows), jnp.bfloat16)] * 2
        + [pltpu.VMEM((2 * FEAT, tile), jnp.float32)],
        input_output_aliases={} if first or last else {len(args) - 1: 2},
        compiler_params=pltpu.CompilerParams(vmem_limit_bytes=20 << 20),
        cost_estimate=pl.CostEstimate(
            flops=24 * rows * COLS * FEAT, bytes_accessed=4 * (rows * COLS + 4 * FEAT * COLS), transcendentals=0
        ),
    )(*args)


def pick(stacked, index, axis):
    return lax.dynamic_index_in_dim(stacked, index, axis, keepdims=False)


def local(acts, grad, weight):
    tok = lax.axis_index("tok")
    fin = lax.axis_index("fin")
    fout = lax.axis_index("fout")
    x, z = fin // NZ, fin % NZ
    y, c = fout // 2, fout % 2
    half = x // 2

    def side(v, which):
        return lax.dynamic_slice_in_dim(v, which * COLS, COLS, axis=1)

    m2 = send(side(grad, 1 - half), MATE)
    zs, ss, xs = {0: side(grad, half)}, {}, {}
    far = lax.dynamic_slice(weight, (tok * 128, (1 - half) * COLS), (128, COLS))
    w_a = send(far, MATE)
    w_b = send(w_a, TOK)
    w_own = side(weight, half)
    a_near = send(pick(acts.reshape(2, 2, 512, FEAT), c, 1).reshape(1024, FEAT), MATE)
    a_far = send(a_near, CORE)
    xs[0] = jnp.concatenate([m2, send(m2, SIDE)], axis=0)
    for s in range(1, 5):
        down, up = s, NZ - s
        zs[down] = send(zs[down - 1], ZDOWN)
        if s < 4:
            zs[up] = send(zs[(up + 1) % NZ], ZUP)
            xs[up] = send(xs[(up + 1) % NZ], ZUP)
            xs[down] = send(xs[down - 1], ZDOWN)
    for r in range(NZ):
        ss[r] = send(zs[r], SIDE)

    scalars = jnp.stack([x ^ fout, tok, fout, z, y]).astype(jnp.int32)
    wg = None
    shares = []
    for i, turns in enumerate(GROUPS):
        pieces, layout = [], []
        if i == 1:
            x5, x3, wg = lax.optimization_barrier((xs[5], xs[3], wg))
            x4 = (send(x5[:ROWS], ZUP), send(x3[ROWS:], ZDOWN))
        for k, r in enumerate(turns):
            pieces += [zs[r], ss[r]]
            layout += [((0, 0, k),), ((0, 1, k),)]
            if r == 4:
                pieces += list(x4)
                layout += [((0, 3, k),), ((0, 2, k),)]
            else:
                pieces.append(xs[r])
                layout.append(((0, 3, k), (ROWS, 2, k)))
        out = group(i, scalars, pieces, tuple(layout), (acts, a_near, a_far), (w_own, w_a, w_b), wg)
        keep, give = out[:2]
        wg = out[2] if len(out) == 3 else out[2:]
        span = ROWS * len(turns)
        got = send(give, CORE)
        both = keep[:, :FEAT] + got[:, :FEAT] + send(keep[:, FEAT:] + got[:, FEAT:], MATE)
        shares.append((both[:span], send(both[span:], YLOW)))

    far = [send(wg[1], TOK), send(wg[2], MATE), send(wg[3], DIAG)]
    far, last = lax.optimization_barrier((far, [v[1] for v in shares]))
    parts = {}
    for turns, (mine, _), other in zip(GROUPS, shares, last):
        total = mine + other
        for k, r in enumerate(turns):
            parts[r] = total[k * ROWS : (k + 1) * ROWS]
    rel = jnp.stack([parts[r] for r in range(NZ)])
    twice = jnp.concatenate([rel, rel], axis=0)
    in_grad = lax.dynamic_slice_in_dim(twice, (NZ - z) % NZ, NZ, axis=0).reshape(NZ * ROWS, FEAT)
    here, there = wg[0] + far[0], far[1] + far[2]
    weight_grad = jnp.where(half == 0, jnp.concatenate([here, there], axis=1), jnp.concatenate([there, here], axis=1))
    return (in_grad, weight_grad)


def solution(mesh):
    in_specs = (P("tok", "fin"), P(("tok", "fin"), "fout"), P("fin", "fout"))
    out_specs = (P(("tok", "fout"), "fin"), P(("fin", "tok"), "fout"))
    return jax.shard_map(local, mesh=mesh, in_specs=in_specs, out_specs=out_specs, check_vma=False)
```

time: 205 us -> 196 us (0.956)
  Pallas kernels: 39 us -> 22.9 us
  waiting for transfers between devices: 76.8 us -> 90 us
  other arithmetic: 8.73 us -> 4.1 us
    pallas_call x2, Pallas kernels: 39 us -> 22.9 us  [group(): pl.pallas_call(functools.partial(group_body, layout, turns, tile, first,...]
    ppermute x38, waiting for transfers between devices: 76.8 us -> 90 us  [send(): return lax.ppermute(value, AXES, perm)]
    add x8, other arithmetic: 7.59 us -> 2.97 us  [the longest x2 2.36 us: local(): here, there = (wg[0] + far[0], far[1] + far[2])]
    unnamed x50 -> x40, local copies, waits for them, and re-layouts: 2.33 us -> 6.75 us
    slice x4, local copies, waits for them, and re-layouts: 3.38 us -> 0.07 us  [the longest x2 0.04 us: local(): shares.append((both[:span], send(both[span:], YLOW)))]
  transfers between devices with their start and end apart: 38 -> 38, of which waited for: 13 -> 14; matrix products, arithmetic and copies ran while one was open for 9% -> 2% of each run, Pallas kernels for 19% -> 12%
where the time goes in v3:
time: 196 us; the launch traced here: 195 us
  waiting for transfers between devices  90 us (46%)
  starting transfers between devices  64.6 us (33%)
  Pallas kernels  22.9 us (12%)
  local copies, waits for them, and re-layouts  12.6 us (6%)
  other arithmetic  4.1 us (2%)
    ppermute x38, waiting for transfers between devices, send(): return lax.ppermute(value, AXES, perm)  90 us
    ppermute x38, starting transfers between devices, send(): return lax.ppermute(value, AXES, perm)  64.6 us
    pallas_call x2, Pallas kernels, group(): pl.pallas_call(functools.partial(group_body, layout, turns, tile, first,...  22.9 us
    unnamed x40, local copies, waits for them, and re-layouts  6.75 us
  transfers between devices with their start and end apart: 38, of which 14 were waited for; matrix products, arithmetic and copies ran while one was open for 2% of the time, Pallas kernels for 12%

profile of v3, /device:TPU:1, one launch (start us, length us, event | category | flops | bytes accessed | tf_op | source)
XLA Modules:
  0.0 195.3 jit_solution(15551536312027504520)
XLA Ops:
  0.7 2.3 %constant_dynamic-slice_fusion.2 = f32[2,1,512,256]{3,2,1,0:T(8,128)} fusion(f32[2,2,512,256]{3,2,1,0:T(8,128)} %bitcast.58, s32[]{:T(128)S(6)} %select_n.58), kind=kLoop, calls=%fused_computation.37 | loop fusion | bytes 2097156 | tf_op jit(solution)/shard_map/jit(dynamic_index_in_dim)/dynamic_slice | solution.py:155
  3.0 3.3 %collective-permute-start.15 = (f32[1024,256]{1,0:T(8,128)}, f32[1024,256]{1,0:T(8,128)}, u32[]{:S(2)}, u32[]{:S(2)}) collective-permute-start(f32[1024,256]{1,0:T(8,128)} %bitcast.6), channel_id=1, source_target_pairs={{0,96},{1,97},{2,98},{3,99},{4,100},{5,101},{6,102},{7,103},{8,104... | collective-permute-start | bytes 3145736 | tf_op jit(solution)/shard_map/ppermute | solution.py:44
  6.3 0.1 collective-permute-start.1
  6.4 1.8 collective-permute-start.3
  8.3 1.1 dynamic_slice.23
  9.3 2.6 %collective-permute-start.17 = (f32[128,1024]{1,0:T(8,128)S(1)}, f32[128,1024]{1,0:T(8,128)}, u32[]{:S(2)}, u32[]{:S(2)}) collective-permute-start(f32[128,1024]{1,0:T(8,128)S(1)} %dynamic_slice.23), channel_id=1, source_target_pairs={{0,96},{1,97},{2,98},{3,99},{4,100},{5,101},{6,102},{7,103},{8,104... | collective-permute-start | bytes 1572872 | tf_op jit(solution)/shard_map/ppermute | solution.py:44
  11.9 3.9 %collective-permute-start.6 = (f32[64,1024]{1,0:T(8,128)S(1)}, f32[64,1024]{1,0:T(8,128)S(1)}, u32[]{:S(2)}, u32[]{:S(2)}) collective-permute-start(f32[64,1024]{1,0:T(8,128)S(1)} %get-tuple-element.37.refs_0_), channel_id=1, source_target_pairs={{0,28},{1,29},{2,30},{3,31},{4,0},{5,1},{6,2},{7,3},{8,4},{9,5},{1... | collective-permute-start | bytes 786440 | tf_op jit(solution)/shard_map/ppermute | solution.py:44
  15.8 18.1 %collective-permute-done.1 = f32[64,1024]{1,0:T(8,128)} collective-permute-done((f32[64,1024]{1,0:T(8,128)S(1)}, f32[64,1024]{1,0:T(8,128)}, u32[]{:S(2)}, u32[]{:S(2)}) %collective-permute-start.1) | collective-permute-done | bytes 262176 | tf_op jit(solution)/shard_map/ppermute | solution.py:44
  33.9 1.0 collective-permute-start.2
  35.0 0.4 collective-permute-start
  35.4 1.0 constant_dynamic-update-slice_fusion.1
  36.4 2.8 %collective-permute-start.9 = (f32[64,1024]{1,0:T(8,128)S(1)}, f32[64,1024]{1,0:T(8,128)S(1)}, u32[]{:S(2)}, u32[]{:S(2)}) collective-permute-start(f32[64,1024]{1,0:T(8,128)S(1)} %collective-permute-done.3.refs_3_), channel_id=1, source_target_pairs={{0,4},{1,5},{2,6},{3,7},{4,8},{5,9},{6,10},{7,11},{8,12},{9,13},{1... | collective-permute-start | bytes 786440 | tf_op jit(solution)/shard_map/ppermute | solution.py:44
  39.2 0.6 collective-permute-done.2
  39.8 6.6 %collective-permute-start.12 = (f32[64,1024]{1,0:T(8,128)S(1)}, f32[64,1024]{1,0:T(8,128)}, u32[]{:S(2)}, u32[]{:S(2)}) collective-permute-start(f32[64,1024]{1,0:T(8,128)S(1)} %collective-permute-done.6.refs_6_), channel_id=1, source_target_pairs={{0,28},{1,29},{2,30},{3,31},{4,0},{5,1},{6,2},{7,3},{8,4},{9,5},{1... | collective-permute-start | bytes 786440 | tf_op jit(solution)/shard_map/ppermute | solution.py:44
  46.4 0.7 copy-done.3
  47.1 1.3 collective-permute-start.5
  48.5 3.9 %collective-permute-start.8 = (f32[128,1024]{1,0:T(8,128)S(1)}, f32[128,1024]{1,0:T(8,128)}, u32[]{:S(2)}, u32[]{:S(2)}) collective-permute-start(f32[128,1024]{1,0:T(8,128)S(1)} %constant_dynamic-update-slice_fusion.refs_2_), channel_id=1, source_target_pairs={{0,28},{1,29},{2,30},{3,31},{4,0},{5,1},{6,2},{7,3},{8,4},{9,5},{1... | collective-permute-start | bytes 1572872 | tf_op jit(solution)/shard_map/ppermute | solution.py:44
  52.4 4.2 %collective-permute-start.16 = (f32[1024,256]{1,0:T(8,128)}, f32[1024,256]{1,0:T(8,128)}, u32[]{:S(2)}, u32[]{:S(2)}) collective-permute-start(f32[1024,256]{1,0:T(8,128)} %collective-permute-done.15.refs_16_.refs_11_), channel_id=1, source_target_pairs={{0,1},{1,0},{2,3},{3,2},{4,5},{5,4},{6,7},{7,6},{8,9},{9,8},{10,11... | collective-permute-start | bytes 3145736 | tf_op jit(solution)/shard_map/ppermute | solution.py:44
  56.6 1.5 collective-permute-start.7
  58.0 6.4 %collective-permute-done.4.refs_4_ = f32[64,1024]{1,0:T(8,128)S(1)} collective-permute-done((f32[64,1024]{1,0:T(8,128)S(1)}, f32[64,1024]{1,0:T(8,128)S(1)}, u32[]{:S(2)}, u32[]{:S(2)}) %collective-permute-start.4) | collective-permute-done | bytes 262176 | tf_op jit(solution)/shard_map/ppermute | solution.py:44
  64.4 0.7 copy-done.5
  65.2 4.8 %collective-permute-done.7.refs_7_ = f32[64,1024]{1,0:T(8,128)S(1)} collective-permute-done((f32[64,1024]{1,0:T(8,128)S(1)}, f32[64,1024]{1,0:T(8,128)S(1)}, u32[]{:S(2)}, u32[]{:S(2)}) %collective-permute-start.7) | collective-permute-done | bytes 262176 | tf_op jit(solution)/shard_map/ppermute | solution.py:44
  70.0 0.7 copy-done.7
  70.7 2.9 %collective-permute-start.18 = (f32[128,1024]{1,0:T(8,128)}, f32[128,1024]{1,0:T(8,128)}, u32[]{:S(2)}, u32[]{:S(2)}) collective-permute-start(f32[128,1024]{1,0:T(8,128)} %collective-permute-done.17.refs_19_.refs_14_), channel_id=1, source_target_pairs={{0,128},{1,129},{2,130},{3,131},{4,132},{5,133},{6,134},{7,135},{8... | collective-permute-start | bytes 1572872 | tf_op jit(solution)/shard_map/ppermute | solution.py:44
  73.6 2.7 %collective-permute-start.14 = (f32[128,1024]{1,0:T(8,128)}, f32[128,1024]{1,0:T(8,128)}, u32[]{:S(2)}, u32[]{:S(2)}) collective-permute-start(f32[128,1024]{1,0:T(8,128)} %collective-permute-done.8.refs_8_), channel_id=1, source_target_pairs={{0,28},{1,29},{2,30},{3,31},{4,0},{5,1},{6,2},{7,3},{8,4},{9,5},{1... | collective-permute-start | bytes 1572872 | tf_op jit(solution)/shard_map/ppermute | solution.py:44
  76.3 0.7 copy-done.9
  77.0 0.1 stack.48.s_ref
  77.1 1.4 constant_dynamic-slice_fusion.1.refs_18_.refs_13_
  78.5 4.3 %collective-permute-done.13.refs_13_ = f32[64,1024]{1,0:T(8,128)} collective-permute-done((f32[64,1024]{1,0:T(8,128)}, f32[64,1024]{1,0:T(8,128)}, u32[]{:S(2)}, u32[]{:S(2)}) %collective-permute-start.13) | collective-permute-done | bytes 262176 | tf_op jit(solution)/shard_map/ppermute | solution.py:44
  82.8 1.1 collective-permute-start.24
  83.9 0.5 collective-permute-done.18.refs_20_.refs_15_
  84.5 2.3 %collective-permute-done.11.refs_11_ = f32[128,1024]{1,0:T(8,128)} collective-permute-done((f32[128,1024]{1,0:T(8,128)}, f32[128,1024]{1,0:T(8,128)}, u32[]{:S(2)}, u32[]{:S(2)}) %collective-permute-start.11) | collective-permute-done | bytes 524320 | tf_op jit(solution)/shard_map/ppermute | solution.py:44
  86.8 2.7 %collective-permute-start.26 = (f32[128,1024]{1,0:T(8,128)}, f32[128,1024]{1,0:T(8,128)S(1)}, u32[]{:S(2)}, u32[]{:S(2)}) collective-permute-start(f32[128,1024]{1,0:T(8,128)} %collective-permute-done.14.refs_14_), channel_id=1, source_target_pairs={{0,28},{1,29},{2,30},{3,31},{4,0},{5,1},{6,2},{7,3},{8,4},{9,5},{1... | collective-permute-start | bytes 1572872 | tf_op jit(solution)/shard_map/ppermute | solution.py:44
  89.5 0.9 copy-done.6
  90.5 0.9 copy-done.8
  91.4 0.9 copy-done.10
  92.4 13.2 %shard_map.50 = (f32[640,512]{1,0:T(8,128)S(1)}, f32[640,512]{1,0:T(8,128)S(1)}, f32[512,1024]{1,0:T(8,128)S(1)}) custom-call(s32[5]{0:T(128)S(1)} %stack.48.s_ref, f32[64,1024]{1,0:T(8,128)S(1)} %get-tuple-element.37.refs_0_, f32[64,1024]{1,0:T(8,128)S(1)} %copy-done.4, f32[128,1024]{1,0:T(8,128)S(1)} %constant_dynamic-update-slice_fusion.refs_2_, ...), custom_call_target="tpu_custom_call" | custom-call | flops 8053063680 | bytes 9437184 | tf_op jit(solution)/shard_map/pallas_call | solution.py:138
  105.6 5.5 %collective-permute-start.19 = (f32[640,512]{1,0:T(8,128)S(1)}, f32[640,512]{1,0:T(8,128)S(1)}, u32[]{:S(2)}, u32[]{:S(2)}) collective-permute-start(f32[640,512]{1,0:T(8,128)S(1)} %get-tuple-element.20), channel_id=1, source_target_pairs={{0,1},{1,0},{2,3},{3,2},{4,5},{5,4},{6,7},{7,6},{8,9},{9,8},{10,11... | collective-permute-start | bytes 3932168 | tf_op jit(solution)/shard_map/ppermute | solution.py:44
  111.1 0.1 collective-permute-start.22
  111.2 7.7 %collective-permute-done.27.refs_6_ = f32[64,1024]{1,0:T(8,128)S(1)} collective-permute-done((f32[64,1024]{1,0:T(8,128)S(1)}, f32[64,1024]{1,0:T(8,128)S(1)}, u32[]{:S(2)}, u32[]{:S(2)}) %collective-permute-start.27) | collective-permute-done | bytes 262176 | tf_op jit(solution)/shard_map/ppermute | solution.py:44
  118.9 1.5 collective-permute-start.28
  120.4 0.1 collective-permute-start.29
  120.5 3.0 %collective-permute-start.30 = (f32[64,1024]{1,0:T(8,128)S(1)}, f32[64,1024]{1,0:T(8,128)S(1)}, u32[]{:S(2)}, u32[]{:S(2)}) collective-permute-start(f32[64,1024]{1,0:T(8,128)S(1)} %slice.72), channel_id=1, source_target_pairs={{0,28},{1,29},{2,30},{3,31},{4,0},{5,1},{6,2},{7,3},{8,4},{9,5},{1... | collective-permute-start | bytes 786440 | tf_op jit(solution)/shard_map/ppermute | solution.py:44
  123.5 2.3 %collective-permute-done.25.refs_4_ = f32[64,1024]{1,0:T(8,128)S(1)} collective-permute-done((f32[64,1024]{1,0:T(8,128)S(1)}, f32[64,1024]{1,0:T(8,128)S(1)}, u32[]{:S(2)}, u32[]{:S(2)}) %collective-permute-start.25) | collective-permute-done | bytes 262176 | tf_op jit(solution)/shard_map/ppermute | solution.py:44
  125.8 5.6 %collective-permute-done.28.refs_7_ = f32[64,1024]{1,0:T(8,128)S(1)} collective-permute-done((f32[64,1024]{1,0:T(8,128)S(1)}, f32[64,1024]{1,0:T(8,128)S(1)}, u32[]{:S(2)}, u32[]{:S(2)}) %collective-permute-start.28) | collective-permute-done | bytes 262176 | tf_op jit(solution)/shard_map/ppermute | solution.py:44
  131.4 9.7 %shard_map.51 = (f32[384,512]{1,0:T(8,128)S(1)}, f32[384,512]{1,0:T(8,128)S(1)}, f32[128,1024]{1,0:T(8,128)S(1)}, f32[128,1024]{1,0:T(8,128)}, f32[128,1024]{1,0:T(8,128)}, /*index=5*/f32[128,1024]{1,0:T(8,128)S(1)}) custom-call(s32[5]{0:T(128)S(1)} %stack.48.s_ref, f32[64,1024]{1,0:T(8,128)S(1)} %collective-permute-done.21.refs_0_, ...), custom_call_target="tpu_custom_call" | custom-call | flops 4831838208 | bytes 7340032 | tf_op jit(solution)/shard_map/pallas_call | solution.py:138
  141.1 1.8 collective-permute-start.35
  142.9 0.1 slice_add_fusion
  143.1 2.6 %collective-permute-start.20 = (f32[640,256]{1,0:T(8,128)S(1)}, f32[640,256]{1,0:T(8,128)S(1)}, u32[]{:S(2)}, u32[]{:S(2)}) collective-permute-start(f32[640,256]{1,0:T(8,128)S(1)} %slice_add_fusion), channel_id=1, source_target_pairs={{0,96},{1,97},{2,98},{3,99},{4,100},{5,101},{6,102},{7,103},{8,104... | collective-permute-start | bytes 1966088 | tf_op jit(solution)/shard_map/ppermute | solution.py:44
  145.7 1.8 collective-permute-start.36
  147.5 1.0 collective-permute-start.32
  148.5 4.3 %collective-permute-start.33 = (f32[128,1024]{1,0:T(8,128)S(1)}, f32[128,1024]{1,0:T(8,128)}, u32[]{:S(2)}, u32[]{:S(2)}) collective-permute-start(f32[128,1024]{1,0:T(8,128)S(1)} %get-tuple-element.27), channel_id=1, source_target_pairs={{0,224},{1,225},{2,226},{3,227},{4,228},{5,229},{6,230},{7,231},{8... | collective-permute-start | bytes 1572872 | tf_op jit(solution)/shard_map/ppermute | solution.py:44
  152.9 7.9 %collective-permute-done.20 = f32[640,256]{1,0:T(8,128)S(1)} collective-permute-done((f32[640,256]{1,0:T(8,128)S(1)}, f32[640,256]{1,0:T(8,128)S(1)}, u32[]{:S(2)}, u32[]{:S(2)}) %collective-permute-start.20) | collective-permute-done | bytes 655392 | tf_op jit(solution)/shard_map/ppermute | solution.py:44
  160.8 0.2 fusion
  161.0 0.1 collective-permute-start.34
  161.1 8.0 %collective-permute-done.36 = f32[384,256]{1,0:T(8,128)S(1)} collective-permute-done((f32[384,256]{1,0:T(8,128)S(1)}, f32[384,256]{1,0:T(8,128)S(1)}, u32[]{:S(2)}, u32[]{:S(2)}) %collective-permute-start.36) | collective-permute-done | bytes 393248 | tf_op jit(solution)/shard_map/ppermute | solution.py:44
  169.1 0.1 fusion.1
  169.2 0.1 collective-permute-start.37
  169.4 11.1 %collective-permute-done.32 = f32[128,1024]{1,0:T(8,128)} collective-permute-done((f32[128,1024]{1,0:T(8,128)}, f32[128,1024]{1,0:T(8,128)}, u32[]{:S(2)}, u32[]{:S(2)}) %collective-permute-start.32) | collective-permute-done | bytes 524320 | tf_op jit(solution)/shard_map/ppermute | solution.py:44
  180.4 10.2 %collective-permute-done.33 = f32[128,1024]{1,0:T(8,128)} collective-permute-done((f32[128,1024]{1,0:T(8,128)S(1)}, f32[128,1024]{1,0:T(8,128)}, u32[]{:S(2)}, u32[]{:S(2)}) %collective-permute-start.33) | collective-permute-done | bytes 524320 | tf_op jit(solution)/shard_map/ppermute | solution.py:44
  190.9 1.1 add.77
  192.0 1.3 add.78
  193.3 0.8 constant_dynamic-slice_fusion
  194.1 1.1 maximum_select_fusion
  (75 shorter events, 0.5 us)
Async XLA Ops:
  0.6 5.7 %copy-start.11 = (f32[64,2048]{1,0:T(8,128)S(1)}, f32[64,2048]{1,0:T(8,128)}, u32[]{:S(2)}) copy-start(f32[64,2048]{1,0:T(8,128)} %param.4) | copy-start | bytes 1572868
  3.0 49.4 %collective-permute-start.15 = (f32[1024,256]{1,0:T(8,128)}, f32[1024,256]{1,0:T(8,128)}, u32[]{:S(2)}, u32[]{:S(2)}) collective-permute-start(f32[1024,256]{1,0:T(8,128)} %bitcast.6), channel_id=1, source_target_pairs={{0,96},{1,97},{2,98},{3,99},{4,100},{5,101},{6,102},{7,103},{8,104... | collective-permute-start | bytes 3145736 | tf_op jit(solution)/shard_map/ppermute | solution.py:44
  6.3 27.6 %collective-permute-start.1 = (f32[64,1024]{1,0:T(8,128)S(1)}, f32[64,1024]{1,0:T(8,128)}, u32[]{:S(2)}, u32[]{:S(2)}) collective-permute-start(f32[64,1024]{1,0:T(8,128)S(1)} %get-tuple-element.36), channel_id=1, source_target_pairs={{0,96},{1,97},{2,98},{3,99},{4,100},{5,101},{6,102},{7,103},{8,104... | collective-permute-start | bytes 786440 | tf_op jit(solution)/shard_map/ppermute | solution.py:44
  6.4 28.6 %collective-permute-start.3 = (f32[64,1024]{1,0:T(8,128)S(1)}, f32[64,1024]{1,0:T(8,128)S(1)}, u32[]{:S(2)}, u32[]{:S(2)}) collective-permute-start(f32[64,1024]{1,0:T(8,128)S(1)} %get-tuple-element.37.refs_0_), channel_id=1, source_target_pairs={{0,4},{1,5},{2,6},{3,7},{4,8},{5,9},{6,10},{7,11},{8,12},{9,13},{1... | collective-permute-start | bytes 786440 | tf_op jit(solution)/shard_map/ppermute | solution.py:44
  9.3 39.1 %collective-permute-start.17 = (f32[128,1024]{1,0:T(8,128)S(1)}, f32[128,1024]{1,0:T(8,128)}, u32[]{:S(2)}, u32[]{:S(2)}) collective-permute-start(f32[128,1024]{1,0:T(8,128)S(1)} %dynamic_slice.23), channel_id=1, source_target_pairs={{0,96},{1,97},{2,98},{3,99},{4,100},{5,101},{6,102},{7,103},{8,104... | collective-permute-start | bytes 1572872 | tf_op jit(solution)/shard_map/ppermute | solution.py:44
  11.9 24.5 %collective-permute-start.6 = (f32[64,1024]{1,0:T(8,128)S(1)}, f32[64,1024]{1,0:T(8,128)S(1)}, u32[]{:S(2)}, u32[]{:S(2)}) collective-permute-start(f32[64,1024]{1,0:T(8,128)S(1)} %get-tuple-element.37.refs_0_), channel_id=1, source_target_pairs={{0,28},{1,29},{2,30},{3,31},{4,0},{5,1},{6,2},{7,3},{8,4},{9,5},{1... | collective-permute-start | bytes 786440 | tf_op jit(solution)/shard_map/ppermute | solution.py:44
  33.9 5.8 %collective-permute-start.2 = (f32[64,1024]{1,0:T(8,128)}, f32[64,1024]{1,0:T(8,128)S(1)}, u32[]{:S(2)}, u32[]{:S(2)}) collective-permute-start(f32[64,1024]{1,0:T(8,128)} %collective-permute-done.1), channel_id=1, source_target_pairs={{0,32},{1,33},{2,34},{3,35},{4,36},{5,37},{6,38},{7,39},{8,40},{9,... | collective-permute-start | bytes 786440 | tf_op jit(solution)/shard_map/ppermute | solution.py:44
  35.0 11.4 %collective-permute-start = (f32[64,1024]{1,0:T(8,128)S(1)}, f32[64,1024]{1,0:T(8,128)S(1)}, u32[]{:S(2)}, u32[]{:S(2)}) collective-permute-start(f32[64,1024]{1,0:T(8,128)S(1)} %get-tuple-element.37.refs_0_), channel_id=1, source_target_pairs={{0,32},{1,33},{2,34},{3,35},{4,36},{5,37},{6,38},{7,39},{8,40},{9,... | collective-permute-start | bytes 786440 | tf_op jit(solution)/shard_map/ppermute | solution.py:44
  36.4 53.1 %copy-start = (f32[2048,256]{1,0:T(8,128)S(1)}, f32[2048,256]{1,0:T(8,128)}, u32[]{:S(2)}) copy-start(f32[2048,256]{1,0:T(8,128)} %refs_10_.1) | copy-start | bytes 6291460
  36.4 20.2 %collective-permute-start.9 = (f32[64,1024]{1,0:T(8,128)S(1)}, f32[64,1024]{1,0:T(8,128)S(1)}, u32[]{:S(2)}, u32[]{:S(2)}) collective-permute-start(f32[64,1024]{1,0:T(8,128)S(1)} %collective-permute-done.3.refs_3_), channel_id=1, source_target_pairs={{0,4},{1,5},{2,6},{3,7},{4,8},{5,9},{6,10},{7,11},{8,12},{9,13},{1... | collective-permute-start | bytes 786440 | tf_op jit(solution)/shard_map/ppermute | solution.py:44
  39.8 16.8 %collective-permute-start.12 = (f32[64,1024]{1,0:T(8,128)S(1)}, f32[64,1024]{1,0:T(8,128)}, u32[]{:S(2)}, u32[]{:S(2)}) collective-permute-start(f32[64,1024]{1,0:T(8,128)S(1)} %collective-permute-done.6.refs_6_), channel_id=1, source_target_pairs={{0,28},{1,29},{2,30},{3,31},{4,0},{5,1},{6,2},{7,3},{8,4},{9,5},{1... | collective-permute-start | bytes 786440 | tf_op jit(solution)/shard_map/ppermute | solution.py:44
  46.4 0.7 copy-start.3
  47.1 26.4 %collective-permute-start.5 = (f32[128,1024]{1,0:T(8,128)S(1)}, f32[128,1024]{1,0:T(8,128)}, u32[]{:S(2)}, u32[]{:S(2)}) collective-permute-start(f32[128,1024]{1,0:T(8,128)S(1)} %constant_dynamic-update-slice_fusion.refs_2_), channel_id=1, source_target_pairs={{0,4},{1,5},{2,6},{3,7},{4,8},{5,9},{6,10},{7,11},{8,12},{9,13},{1... | collective-permute-start | bytes 1572872 | tf_op jit(solution)/shard_map/ppermute | solution.py:44
  48.5 25.1 %collective-permute-start.8 = (f32[128,1024]{1,0:T(8,128)S(1)}, f32[128,1024]{1,0:T(8,128)}, u32[]{:S(2)}, u32[]{:S(2)}) collective-permute-start(f32[128,1024]{1,0:T(8,128)S(1)} %constant_dynamic-update-slice_fusion.refs_2_), channel_id=1, source_target_pairs={{0,28},{1,29},{2,30},{3,31},{4,0},{5,1},{6,2},{7,3},{8,4},{9,5},{1... | collective-permute-start | bytes 1572872 | tf_op jit(solution)/shard_map/ppermute | solution.py:44
  52.4 37.1 %collective-permute-start.16 = (f32[1024,256]{1,0:T(8,128)}, f32[1024,256]{1,0:T(8,128)}, u32[]{:S(2)}, u32[]{:S(2)}) collective-permute-start(f32[1024,256]{1,0:T(8,128)} %collective-permute-done.15.refs_16_.refs_11_), channel_id=1, source_target_pairs={{0,1},{1,0},{2,3},{3,2},{4,5},{5,4},{6,7},{7,6},{8,9},{9,8},{10,11... | collective-permute-start | bytes 3145736 | tf_op jit(solution)/shard_map/ppermute | solution.py:44
  56.6 17.0 %copy-start.1 = (f32[64,1024]{1,0:T(8,128)}, f32[64,1024]{1,0:T(8,128)S(1)}, u32[]{:S(2)}) copy-start(f32[64,1024]{1,0:T(8,128)S(1)} %collective-permute-done.9.refs_9_) | copy-start | bytes 786436
  56.6 7.9 %collective-permute-start.4 = (f32[64,1024]{1,0:T(8,128)S(1)}, f32[64,1024]{1,0:T(8,128)S(1)}, u32[]{:S(2)}, u32[]{:S(2)}) collective-permute-start(f32[64,1024]{1,0:T(8,128)S(1)} %collective-permute-done.3.refs_3_), channel_id=1, source_target_pairs={{0,32},{1,33},{2,34},{3,35},{4,36},{5,37},{6,38},{7,39},{8,40},{9,... | collective-permute-start | bytes 786440 | tf_op jit(solution)/shard_map/ppermute | solution.py:44
  56.6 13.4 %collective-permute-start.7 = (f32[64,1024]{1,0:T(8,128)S(1)}, f32[64,1024]{1,0:T(8,128)S(1)}, u32[]{:S(2)}, u32[]{:S(2)}) collective-permute-start(f32[64,1024]{1,0:T(8,128)S(1)} %collective-permute-done.6.refs_6_), channel_id=1, source_target_pairs={{0,32},{1,33},{2,34},{3,35},{4,36},{5,37},{6,38},{7,39},{8,40},{9,... | collective-permute-start | bytes 786440 | tf_op jit(solution)/shard_map/ppermute | solution.py:44
  64.4 0.7 copy-start.5
  65.1 11.1 %collective-permute-start.10 = (f32[64,1024]{1,0:T(8,128)S(1)}, f32[64,1024]{1,0:T(8,128)S(1)}, u32[]{:S(2)}, u32[]{:S(2)}) collective-permute-start(f32[64,1024]{1,0:T(8,128)S(1)} %collective-permute-done.9.refs_9_), channel_id=1, source_target_pairs={{0,32},{1,33},{2,34},{3,35},{4,36},{5,37},{6,38},{7,39},{8,40},{9,... | collective-permute-start | bytes 786440 | tf_op jit(solution)/shard_map/ppermute | solution.py:44
  70.0 0.7 copy-start.7
  70.7 13.8 %collective-permute-start.18 = (f32[128,1024]{1,0:T(8,128)}, f32[128,1024]{1,0:T(8,128)}, u32[]{:S(2)}, u32[]{:S(2)}) collective-permute-start(f32[128,1024]{1,0:T(8,128)} %collective-permute-done.17.refs_19_.refs_14_), channel_id=1, source_target_pairs={{0,128},{1,129},{2,130},{3,131},{4,132},{5,133},{6,134},{7,135},{8... | collective-permute-start | bytes 1572872 | tf_op jit(solution)/shard_map/ppermute | solution.py:44
  73.6 13.2 %collective-permute-start.11 = (f32[128,1024]{1,0:T(8,128)}, f32[128,1024]{1,0:T(8,128)}, u32[]{:S(2)}, u32[]{:S(2)}) collective-permute-start(f32[128,1024]{1,0:T(8,128)} %collective-permute-done.5.refs_5_), channel_id=1, source_target_pairs={{0,4},{1,5},{2,6},{3,7},{4,8},{5,9},{6,10},{7,11},{8,12},{9,13},{1... | collective-permute-start | bytes 1572872 | tf_op jit(solution)/shard_map/ppermute | solution.py:44
  73.6 13.2 %collective-permute-start.14 = (f32[128,1024]{1,0:T(8,128)}, f32[128,1024]{1,0:T(8,128)}, u32[]{:S(2)}, u32[]{:S(2)}) collective-permute-start(f32[128,1024]{1,0:T(8,128)} %collective-permute-done.8.refs_8_), channel_id=1, source_target_pairs={{0,28},{1,29},{2,30},{3,31},{4,0},{5,1},{6,2},{7,3},{8,4},{9,5},{1... | collective-permute-start | bytes 1572872 | tf_op jit(solution)/shard_map/ppermute | solution.py:44
  76.3 0.7 copy-start.9
  77.0 5.8 %collective-permute-start.13 = (f32[64,1024]{1,0:T(8,128)}, f32[64,1024]{1,0:T(8,128)}, u32[]{:S(2)}, u32[]{:S(2)}) collective-permute-start(f32[64,1024]{1,0:T(8,128)} %collective-permute-done.12.refs_12_), channel_id=1, source_target_pairs={{0,32},{1,33},{2,34},{3,35},{4,36},{5,37},{6,38},{7,39},{8,40},{9,... | collective-permute-start | bytes 786440 | tf_op jit(solution)/shard_map/ppermute | solution.py:44
  77.1 7.4 %copy-start.2 = (f32[64,1024]{1,0:T(8,128)S(1)}, f32[64,1024]{1,0:T(8,128)}, u32[]{:S(2)}) copy-start(f32[64,1024]{1,0:T(8,128)} %copy-done.1) | copy-start | bytes 786436
  77.1 12.4 %copy-start.4 = (f32[64,1024]{1,0:T(8,128)S(1)}, f32[64,1024]{1,0:T(8,128)}, u32[]{:S(2)}) copy-start(f32[64,1024]{1,0:T(8,128)} %copy-done.3) | copy-start | bytes 786436
  82.8 28.3 %collective-permute-start.24 = (f32[64,1024]{1,0:T(8,128)}, f32[64,1024]{1,0:T(8,128)S(1)}, u32[]{:S(2)}, u32[]{:S(2)}) collective-permute-start(f32[64,1024]{1,0:T(8,128)} %collective-permute-done.12.refs_12_), channel_id=1, source_target_pairs={{0,28},{1,29},{2,30},{3,31},{4,0},{5,1},{6,2},{7,3},{8,4},{9,5},{1... | collective-permute-start | bytes 786440 | tf_op jit(solution)/shard_map/ppermute | solution.py:44
  84.5 26.7 %collective-permute-start.21 = (f32[64,1024]{1,0:T(8,128)S(1)}, f32[64,1024]{1,0:T(8,128)S(1)}, u32[]{:S(2)}, u32[]{:S(2)}) collective-permute-start(f32[64,1024]{1,0:T(8,128)S(1)} %copy-done.2), channel_id=1, source_target_pairs={{0,4},{1,5},{2,6},{3,7},{4,8},{5,9},{6,10},{7,11},{8,12},{9,13},{1... | collective-permute-start | bytes 786440 | tf_op jit(solution)/shard_map/ppermute | solution.py:44
  86.8 32.1 %collective-permute-start.23 = (f32[128,1024]{1,0:T(8,128)}, f32[128,1024]{1,0:T(8,128)S(1)}, u32[]{:S(2)}, u32[]{:S(2)}) collective-permute-start(f32[128,1024]{1,0:T(8,128)} %collective-permute-done.11.refs_11_), channel_id=1, source_target_pairs={{0,4},{1,5},{2,6},{3,7},{4,8},{5,9},{6,10},{7,11},{8,12},{9,13},{1... | collective-permute-start | bytes 1572872 | tf_op jit(solution)/shard_map/ppermute | solution.py:44
  86.8 33.5 %collective-permute-start.26 = (f32[128,1024]{1,0:T(8,128)}, f32[128,1024]{1,0:T(8,128)S(1)}, u32[]{:S(2)}, u32[]{:S(2)}) collective-permute-start(f32[128,1024]{1,0:T(8,128)} %collective-permute-done.14.refs_14_), channel_id=1, source_target_pairs={{0,28},{1,29},{2,30},{3,31},{4,0},{5,1},{6,2},{7,3},{8,4},{9,5},{1... | collective-permute-start | bytes 1572872 | tf_op jit(solution)/shard_map/ppermute | solution.py:44
  89.5 1.0 copy-start.6
  90.5 0.9 copy-start.8
  91.4 0.9 copy-start.10
  105.6 37.3 %collective-permute-start.19 = (f32[640,512]{1,0:T(8,128)S(1)}, f32[640,512]{1,0:T(8,128)S(1)}, u32[]{:S(2)}, u32[]{:S(2)}) collective-permute-start(f32[640,512]{1,0:T(8,128)S(1)} %get-tuple-element.20), channel_id=1, source_target_pairs={{0,1},{1,0},{2,3},{3,2},{4,5},{5,4},{6,7},{7,6},{8,9},{9,8},{10,11... | collective-permute-start | bytes 3932168 | tf_op jit(solution)/shard_map/ppermute | solution.py:44
  111.1 7.8 %collective-permute-start.27 = (f32[64,1024]{1,0:T(8,128)S(1)}, f32[64,1024]{1,0:T(8,128)S(1)}, u32[]{:S(2)}, u32[]{:S(2)}) collective-permute-start(f32[64,1024]{1,0:T(8,128)S(1)} %collective-permute-done.24.refs_3_), channel_id=1, source_target_pairs={{0,28},{1,29},{2,30},{3,31},{4,0},{5,1},{6,2},{7,3},{8,4},{9,5},{1... | collective-permute-start | bytes 786440 | tf_op jit(solution)/shard_map/ppermute | solution.py:44
  111.1 9.4 %collective-permute-start.22 = (f32[64,1024]{1,0:T(8,128)S(1)}, f32[64,1024]{1,0:T(8,128)S(1)}, u32[]{:S(2)}, u32[]{:S(2)}) collective-permute-start(f32[64,1024]{1,0:T(8,128)S(1)} %collective-permute-done.21.refs_0_), channel_id=1, source_target_pairs={{0,32},{1,33},{2,34},{3,35},{4,36},{5,37},{6,38},{7,39},{8,40},{9,... | collective-permute-start | bytes 786440 | tf_op jit(solution)/shard_map/ppermute | solution.py:44
  118.9 6.9 %collective-permute-start.25 = (f32[64,1024]{1,0:T(8,128)S(1)}, f32[64,1024]{1,0:T(8,128)S(1)}, u32[]{:S(2)}, u32[]{:S(2)}) collective-permute-start(f32[64,1024]{1,0:T(8,128)S(1)} %collective-permute-done.24.refs_3_), channel_id=1, source_target_pairs={{0,32},{1,33},{2,34},{3,35},{4,36},{5,37},{6,38},{7,39},{8,40},{9,... | collective-permute-start | bytes 786440 | tf_op jit(solution)/shard_map/ppermute | solution.py:44
  118.9 12.5 %collective-permute-start.28 = (f32[64,1024]{1,0:T(8,128)S(1)}, f32[64,1024]{1,0:T(8,128)S(1)}, u32[]{:S(2)}, u32[]{:S(2)}) collective-permute-start(f32[64,1024]{1,0:T(8,128)S(1)} %collective-permute-done.27.refs_6_), channel_id=1, source_target_pairs={{0,32},{1,33},{2,34},{3,35},{4,36},{5,37},{6,38},{7,39},{8,40},{9,... | collective-permute-start | bytes 786440 | tf_op jit(solution)/shard_map/ppermute | solution.py:44
  120.4 11.0 %collective-permute-start.29 = (f32[64,1024]{1,0:T(8,128)S(1)}, f32[64,1024]{1,0:T(8,128)S(1)}, u32[]{:S(2)}, u32[]{:S(2)}) collective-permute-start(f32[64,1024]{1,0:T(8,128)S(1)} %slice.71), channel_id=1, source_target_pairs={{0,4},{1,5},{2,6},{3,7},{4,8},{5,9},{6,10},{7,11},{8,12},{9,13},{1... | collective-permute-start | bytes 786440 | tf_op jit(solution)/shard_map/ppermute | solution.py:44
  120.5 10.9 %collective-permute-start.30 = (f32[64,1024]{1,0:T(8,128)S(1)}, f32[64,1024]{1,0:T(8,128)S(1)}, u32[]{:S(2)}, u32[]{:S(2)}) collective-permute-start(f32[64,1024]{1,0:T(8,128)S(1)} %slice.72), channel_id=1, source_target_pairs={{0,28},{1,29},{2,30},{3,31},{4,0},{5,1},{6,2},{7,3},{8,4},{9,5},{1... | collective-permute-start | bytes 786440 | tf_op jit(solution)/shard_map/ppermute | solution.py:44
  141.1 4.5 %collective-permute-start.35 = (f32[384,512]{1,0:T(8,128)S(1)}, f32[384,512]{1,0:T(8,128)S(1)}, u32[]{:S(2)}, u32[]{:S(2)}) collective-permute-start(f32[384,512]{1,0:T(8,128)S(1)} %get-tuple-element.29), channel_id=1, source_target_pairs={{0,1},{1,0},{2,3},{3,2},{4,5},{5,4},{6,7},{7,6},{8,9},{9,8},{10,11... | collective-permute-start | bytes 2359304 | tf_op jit(solution)/shard_map/ppermute | solution.py:44
  143.1 17.7 %collective-permute-start.20 = (f32[640,256]{1,0:T(8,128)S(1)}, f32[640,256]{1,0:T(8,128)S(1)}, u32[]{:S(2)}, u32[]{:S(2)}) collective-permute-start(f32[640,256]{1,0:T(8,128)S(1)} %slice_add_fusion), channel_id=1, source_target_pairs={{0,96},{1,97},{2,98},{3,99},{4,100},{5,101},{6,102},{7,103},{8,104... | collective-permute-start | bytes 1966088 | tf_op jit(solution)/shard_map/ppermute | solution.py:44
  145.7 23.4 %collective-permute-start.36 = (f32[384,256]{1,0:T(8,128)S(1)}, f32[384,256]{1,0:T(8,128)S(1)}, u32[]{:S(2)}, u32[]{:S(2)}) collective-permute-start(f32[384,256]{1,0:T(8,128)S(1)} %slice_add_fusion.2), channel_id=1, source_target_pairs={{0,96},{1,97},{2,98},{3,99},{4,100},{5,101},{6,102},{7,103},{8,104... | collective-permute-start | bytes 1179656 | tf_op jit(solution)/shard_map/ppermute | solution.py:44
  147.5 21.9 %collective-permute-start.31 = (f32[128,1024]{1,0:T(8,128)}, f32[128,1024]{1,0:T(8,128)}, u32[]{:S(2)}, u32[]{:S(2)}) collective-permute-start(f32[128,1024]{1,0:T(8,128)} %get-tuple-element.25), channel_id=1, source_target_pairs={{0,128},{1,129},{2,130},{3,131},{4,132},{5,133},{6,134},{7,135},{8... | collective-permute-start | bytes 1572872 | tf_op jit(solution)/shard_map/ppermute | solution.py:44
  147.5 32.9 %collective-permute-start.32 = (f32[128,1024]{1,0:T(8,128)}, f32[128,1024]{1,0:T(8,128)}, u32[]{:S(2)}, u32[]{:S(2)}) collective-permute-start(f32[128,1024]{1,0:T(8,128)} %get-tuple-element.26), channel_id=1, source_target_pairs={{0,96},{1,97},{2,98},{3,99},{4,100},{5,101},{6,102},{7,103},{8,104... | collective-permute-start | bytes 1572872 | tf_op jit(solution)/shard_map/ppermute | solution.py:44
  148.5 42.1 %collective-permute-start.33 = (f32[128,1024]{1,0:T(8,128)S(1)}, f32[128,1024]{1,0:T(8,128)}, u32[]{:S(2)}, u32[]{:S(2)}) collective-permute-start(f32[128,1024]{1,0:T(8,128)S(1)} %get-tuple-element.27), channel_id=1, source_target_pairs={{0,224},{1,225},{2,226},{3,227},{4,228},{5,229},{6,230},{7,231},{8... | collective-permute-start | bytes 1572872 | tf_op jit(solution)/shard_map/ppermute | solution.py:44
  161.0 29.6 %collective-permute-start.34 = (f32[320,256]{1,0:T(8,128)S(1)}, f32[320,256]{1,0:T(8,128)S(1)}, u32[]{:S(2)}, u32[]{:S(2)}) collective-permute-start(f32[320,256]{1,0:T(8,128)S(1)} %slice.91), channel_id=1, source_target_pairs={{0,2},{1,3},{2,0},{3,1},{4,6},{5,7},{6,4},{7,5},{8,10},{9,11},{10,... | collective-permute-start | bytes 983048 | tf_op jit(solution)/shard_map/ppermute | solution.py:44
  169.2 21.4 %collective-permute-start.37 = (f32[192,256]{1,0:T(8,128)S(1)}, f32[192,256]{1,0:T(8,128)S(1)}, u32[]{:S(2)}, u32[]{:S(2)}) collective-permute-start(f32[192,256]{1,0:T(8,128)S(1)} %slice.94), channel_id=1, source_target_pairs={{0,2},{1,3},{2,0},{3,1},{4,6},{5,7},{6,4},{7,5},{8,10},{9,11},{10,... | collective-permute-start | bytes 589832 | tf_op jit(solution)/shard_map/ppermute | solution.py:44

commit v4 on v3

--- a/solution.py
+++ b/solution.py
@@ -62,7 +62,7 @@
     wg_in = None if first else take(1)[0]
     keep_ref, send_ref = take(2)
     wg_refs = take(4 if last else 1)
-    gl, thi, tlo, wcat = refs
+    bufs, (thi, tlo) = (refs[:2], refs[2:4]), refs[4:]
     n = len(turns)
     span = n * ROWS
     spin, tok, fout, z, y = (s_ref[k] for k in range(5))
@@ -89,8 +89,7 @@
     other = lambda base: pl.ds(pl.multiple_of(base + (1 - tok) * 128, 128), 128)
     high, low = pl.ds(0, tile), pl.ds(tile, tile)
 
-    @pl.loop(0, COLS // tile)
-    def _(step):
+    def tile_at(step, gl, wcat):
         cols = pl.ds(pl.multiple_of(step * tile, tile), tile)
         for ref, parts in zip(pieces, layout):
             for start, e, k in parts:
@@ -120,6 +119,11 @@
         else:
             wg_refs[0][:, cols] = acc
 
+    @pl.loop(0, COLS // tile // 2)
+    def _(pair):
+        for k in range(2):
+            tile_at(2 * pair + k, bufs[0][k], bufs[1][k])
+
 
 def group(index, scalars, pieces, layout, acts, weights, wg):
     turns, tile = GROUPS[index], TILES[index]
@@ -140,15 +144,43 @@
         in_specs=[pl.BlockSpec(memory_space=pltpu.SMEM)] + [vmem] * (len(args) - 1),
         out_specs=[vmem] * (2 + len(grads)),
         out_shape=[share, share, *grads],
-        scratch_shapes=[pltpu.VMEM((rows, 2 * tile), jnp.bfloat16)]
-        + [pltpu.VMEM((2 * FEAT, rows), jnp.bfloat16)] * 2
-        + [pltpu.VMEM((2 * FEAT, tile), jnp.float32)],
+        scratch_shapes=[pltpu.VMEM((rows, 2 * tile), jnp.bfloat16)] * 2
+        + [pltpu.VMEM((2 * FEAT, tile), jnp.float32)] * 2
+        + [pltpu.VMEM((2 * FEAT, rows), jnp.bfloat16)] * 2,
         input_output_aliases={} if first or last else {len(args) - 1: 2},
         compiler_params=pltpu.CompilerParams(vmem_limit_bytes=20 << 20),
         cost_estimate=pl.CostEstimate(
             flops=24 * rows * COLS * FEAT, bytes_accessed=4 * (rows * COLS + 4 * FEAT * COLS), transcendentals=0
         ),
     )(*args)
+
+
+def finish_body(s_ref, *refs):
+    shares, grads, (in_ref, wg_ref) = refs[:4], refs[4:8], refs[8:]
+    z, half = s_ref[3], s_ref[5]
+    for g, turns in enumerate(GROUPS):
+        for k, r in enumerate(turns):
+            at = pl.multiple_of(lax.rem(z + r, NZ) * ROWS, ROWS)
+            rows = pl.ds(k * ROWS, ROWS)
+            in_ref[pl.ds(at, ROWS), :] = shares[2 * g][rows, :] + shares[2 * g + 1][rows, :]
+    here = pl.ds(pl.multiple_of(half * COLS, COLS), COLS)
+    there = pl.ds(pl.multiple_of((1 - half) * COLS, COLS), COLS)
+    wg_ref[:, here] = grads[0][...] + grads[1][...]
+    wg_ref[:, there] = grads[2][...] + grads[3][...]
+
+
+def finish(scalars, shares, grads):
+    vmem = pl.BlockSpec(memory_space=pltpu.VMEM)
+    return pl.pallas_call(
+        finish_body,
+        in_specs=[pl.BlockSpec(memory_space=pltpu.SMEM)] + [vmem] * 8,
+        out_shape=[
+            jax.ShapeDtypeStruct((NZ * ROWS, FEAT), jnp.float32),
+            jax.ShapeDtypeStruct((FEAT // 2, 2 * COLS), jnp.float32),
+        ],
+        compiler_params=pltpu.CompilerParams(vmem_limit_bytes=16 << 20),
+        cost_estimate=pl.CostEstimate(flops=1 << 20, bytes_accessed=4 << 20, transcendentals=0),
+    )(scalars, *shares, *grads)
 
 
 def pick(stacked, index, axis):
@@ -185,7 +217,7 @@
     for r in range(NZ):
         ss[r] = send(zs[r], SIDE)
 
-    scalars = jnp.stack([x ^ fout, tok, fout, z, y]).astype(jnp.int32)
+    scalars = jnp.stack([x ^ fout, tok, fout, z, y, half]).astype(jnp.int32)
     wg = None
     shares = []
     for i, turns in enumerate(GROUPS):
@@ -207,22 +239,11 @@
         wg = out[2] if len(out) == 3 else out[2:]
         span = ROWS * len(turns)
         got = send(give, CORE)
-        both = keep[:, :FEAT] + got[:, :FEAT] + send(keep[:, FEAT:] + got[:, FEAT:], MATE)
-        shares.append((both[:span], send(both[span:], YLOW)))
-
-    far = [send(wg[1], TOK), send(wg[2], MATE), send(wg[3], DIAG)]
-    far, last = lax.optimization_barrier((far, [v[1] for v in shares]))
-    parts = {}
-    for turns, (mine, _), other in zip(GROUPS, shares, last):
-        total = mine + other
-        for k, r in enumerate(turns):
-            parts[r] = total[k * ROWS : (k + 1) * ROWS]
-    rel = jnp.stack([parts[r] for r in range(NZ)])
-    twice = jnp.concatenate([rel, rel], axis=0)
-    in_grad = lax.dynamic_slice_in_dim(twice, (NZ - z) % NZ, NZ, axis=0).reshape(NZ * ROWS, FEAT)
-    here, there = wg[0] + far[0], far[1] + far[2]
-    weight_grad = jnp.where(half == 0, jnp.concatenate([here, there], axis=1), jnp.concatenate([there, here], axis=1))
-    return (in_grad, weight_grad)
+        mine = keep[:span] + got[:span] + send(keep[span:] + got[span:], YLOW)
+        shares += [mine[:, :FEAT], send(mine[:, FEAT:], MATE)]
+
+    far = (send(wg[1], TOK), send(wg[2], MATE), send(wg[3], DIAG))
+    return finish(scalars, shares, (wg[0], *far))
 
 
 def solution(mesh):

time: 196 us -> 196 us (level)
  other arithmetic: 4.1 us -> 0.45 us
    add x8 -> x4, other arithmetic: 2.97 us -> 0.45 us  [local(): mine = keep[:span] + got[:span] + send(keep[span:] + got[span:], YLOW)]
    pallas_call x2, Pallas kernels: 22.9 us -> 20.8 us  [group(): pl.pallas_call(functools.partial(group_body, layout, turns, tile, first,...]
    unnamed x40 -> x35, local copies, waits for them, and re-layouts: 6.75 us -> 8.07 us
  transfers between devices with their start and end apart: 38 -> 38, of which waited for: 14 -> 12; matrix products, arithmetic and copies ran while one was open for 2% -> 2% of each run, Pallas kernels for 12% -> 11%
where the time goes in v4:
time: 196 us; the launch traced here: 194 us
  waiting for transfers between devices  90.8 us (46%)
  starting transfers between devices  65 us (33%)
  Pallas kernels  22.6 us (12%)
  local copies, waits for them, and re-layouts  14.2 us (7%)
    ppermute x38, waiting for transfers between devices, send(): return lax.ppermute(value, AXES, perm)  90.8 us
    ppermute x38, starting transfers between devices, send(): return lax.ppermute(value, AXES, perm)  65 us
    pallas_call x2, Pallas kernels, group(): pl.pallas_call(functools.partial(group_body, layout, turns, tile, first,...  20.8 us
    unnamed x35, local copies, waits for them, and re-layouts  8.07 us
  transfers between devices with their start and end apart: 38, of which 12 were waited for; matrix products, arithmetic and copies ran while one was open for 2% of the time, Pallas kernels for 11%

profile of v4, /device:TPU:1, one launch (start us, length us, event | category | flops | bytes accessed | tf_op | source)
XLA Modules:
  0.0 194.0 jit_solution(1971653335557234483)
XLA Ops:
  0.7 2.3 %constant_dynamic-slice_fusion.1 = f32[2,1,512,256]{3,2,1,0:T(8,128)} fusion(f32[2,2,512,256]{3,2,1,0:T(8,128)} %bitcast.10, s32[]{:T(128)S(6)} %select_n.43), kind=kLoop, calls=%fused_computation.9 | loop fusion | bytes 2097156 | tf_op jit(solution)/shard_map/jit(dynamic_index_in_dim)/dynamic_slice | solution.py:187
  3.0 3.3 %collective-permute-start.15 = (f32[1024,256]{1,0:T(8,128)}, f32[1024,256]{1,0:T(8,128)}, u32[]{:S(2)}, u32[]{:S(2)}) collective-permute-start(f32[1024,256]{1,0:T(8,128)} %bitcast.7), channel_id=1, source_target_pairs={{0,96},{1,97},{2,98},{3,99},{4,100},{5,101},{6,102},{7,103},{8,104... | collective-permute-start | bytes 3145736 | tf_op jit(solution)/shard_map/ppermute | solution.py:44
  6.3 0.1 collective-permute-start.1
  6.4 1.8 collective-permute-start.3
  8.3 4.0 %collective-permute-start.6 = (f32[64,1024]{1,0:T(8,128)S(1)}, f32[64,1024]{1,0:T(8,128)}, u32[]{:S(2)}, u32[]{:S(2)}) collective-permute-start(f32[64,1024]{1,0:T(8,128)S(1)} %get-tuple-element.29.refs_0_), channel_id=1, source_target_pairs={{0,28},{1,29},{2,30},{3,31},{4,0},{5,1},{6,2},{7,3},{8,4},{9,5},{1... | collective-permute-start | bytes 786440 | tf_op jit(solution)/shard_map/ppermute | solution.py:44
  12.3 21.7 %collective-permute-done.1 = f32[64,1024]{1,0:T(8,128)S(1)} collective-permute-done((f32[64,1024]{1,0:T(8,128)S(1)}, f32[64,1024]{1,0:T(8,128)S(1)}, u32[]{:S(2)}, u32[]{:S(2)}) %collective-permute-start.1) | collective-permute-done | bytes 262176 | tf_op jit(solution)/shard_map/ppermute | solution.py:44
  33.9 0.9 collective-permute-start.2
  34.9 0.5 collective-permute-start.4
  35.4 0.7 copy-done.1
  36.1 2.6 %collective-permute-start.9 = (f32[64,1024]{1,0:T(8,128)}, f32[64,1024]{1,0:T(8,128)}, u32[]{:S(2)}, u32[]{:S(2)}) collective-permute-start(f32[64,1024]{1,0:T(8,128)} %collective-permute-done.3.refs_3_), channel_id=1, source_target_pairs={{0,4},{1,5},{2,6},{3,7},{4,8},{5,9},{6,10},{7,11},{8,12},{9,13},{1... | collective-permute-start | bytes 786440 | tf_op jit(solution)/shard_map/ppermute | solution.py:44
  38.7 1.1 dynamic_slice.20
  39.8 2.6 %collective-permute-start.17 = (f32[128,1024]{1,0:T(8,128)S(1)}, f32[128,1024]{1,0:T(8,128)S(1)}, u32[]{:S(2)}, u32[]{:S(2)}) collective-permute-start(f32[128,1024]{1,0:T(8,128)S(1)} %dynamic_slice.20), channel_id=1, source_target_pairs={{0,96},{1,97},{2,98},{3,99},{4,100},{5,101},{6,102},{7,103},{8,104... | collective-permute-start | bytes 1572872 | tf_op jit(solution)/shard_map/ppermute | solution.py:44
  42.4 2.8 %collective-permute-done.4.refs_4_ = f32[64,1024]{1,0:T(8,128)S(1)} collective-permute-done((f32[64,1024]{1,0:T(8,128)}, f32[64,1024]{1,0:T(8,128)S(1)}, u32[]{:S(2)}, u32[]{:S(2)}) %collective-permute-start.4) | collective-permute-done | bytes 262176 | tf_op jit(solution)/shard_map/ppermute | solution.py:44
  45.2 0.7 copy-done.3
  45.9 7.2 %collective-permute-start.12 = (f32[64,1024]{1,0:T(8,128)}, f32[64,1024]{1,0:T(8,128)S(1)}, u32[]{:S(2)}, u32[]{:S(2)}) collective-permute-start(f32[64,1024]{1,0:T(8,128)} %collective-permute-done.6.refs_6_), channel_id=1, source_target_pairs={{0,28},{1,29},{2,30},{3,31},{4,0},{5,1},{6,2},{7,3},{8,4},{9,5},{1... | collective-permute-start | bytes 786440 | tf_op jit(solution)/shard_map/ppermute | solution.py:44
  53.1 0.0 copy-start
  53.2 0.1 collective-permute-start.10
  53.3 1.1 constant_dynamic-update-slice_fusion.refs_2_
  54.4 0.7 copy-done.5
  55.1 1.7 collective-permute-done.12.refs_12_
  56.8 3.0 %collective-permute-start.8 = (f32[128,1024]{1,0:T(8,128)S(1)}, f32[128,1024]{1,0:T(8,128)}, u32[]{:S(2)}, u32[]{:S(2)}) collective-permute-start(f32[128,1024]{1,0:T(8,128)S(1)} %constant_dynamic-update-slice_fusion.refs_2_), channel_id=1, source_target_pairs={{0,28},{1,29},{2,30},{3,31},{4,0},{5,1},{6,2},{7,3},{8,4},{9,5},{1... | collective-permute-start | bytes 1572872 | tf_op jit(solution)/shard_map/ppermute | solution.py:44
  59.8 7.0 %collective-permute-start.16 = (f32[1024,256]{1,0:T(8,128)}, f32[1024,256]{1,0:T(8,128)}, u32[]{:S(2)}, u32[]{:S(2)}) collective-permute-start(f32[1024,256]{1,0:T(8,128)} %collective-permute-done.15.refs_16_.refs_11_), channel_id=1, source_target_pairs={{0,1},{1,0},{2,3},{3,2},{4,5},{5,4},{6,7},{7,6},{8,9},{9,8},{10,11... | collective-permute-start | bytes 3145736 | tf_op jit(solution)/shard_map/ppermute | solution.py:44
  66.8 0.7 copy-done.11
  67.5 7.1 %collective-permute-done.13.refs_13_ = f32[64,1024]{1,0:T(8,128)S(1)} collective-permute-done((f32[64,1024]{1,0:T(8,128)S(1)}, f32[64,1024]{1,0:T(8,128)S(1)}, u32[]{:S(2)}, u32[]{:S(2)}) %collective-permute-start.13) | collective-permute-done | bytes 262176 | tf_op jit(solution)/shard_map/ppermute | solution.py:44
  74.6 0.7 copy-done.13
  75.3 2.9 %collective-permute-start.18 = (f32[128,1024]{1,0:T(8,128)S(1)}, f32[128,1024]{1,0:T(8,128)}, u32[]{:S(2)}, u32[]{:S(2)}) collective-permute-start(f32[128,1024]{1,0:T(8,128)S(1)} %collective-permute-done.17.refs_19_.refs_14_), channel_id=1, source_target_pairs={{0,128},{1,129},{2,130},{3,131},{4,132},{5,133},{6,134},{7,135},{8... | collective-permute-start | bytes 1572872 | tf_op jit(solution)/shard_map/ppermute | solution.py:44
  78.2 0.7 copy-done.9
  78.9 1.4 collective-permute-start.11
  80.4 1.3 collective-permute-start.14
  81.6 3.3 %collective-permute-done.25.refs_3_ = f32[64,1024]{1,0:T(8,128)} collective-permute-done((f32[64,1024]{1,0:T(8,128)S(1)}, f32[64,1024]{1,0:T(8,128)}, u32[]{:S(2)}, u32[]{:S(2)}) %collective-permute-start.25) | collective-permute-done | bytes 262176 | tf_op jit(solution)/shard_map/ppermute | solution.py:44
  84.9 1.4 collective-permute-start.28
  86.3 0.1 stack.27.s_ref
  86.4 1.4 constant_dynamic-slice_fusion.refs_18_.refs_13_
  87.8 1.6 collective-permute-done.18.refs_20_.refs_15_
  89.4 12.4 %collective-permute-done.28.refs_6_ = f32[64,1024]{1,0:T(8,128)} collective-permute-done((f32[64,1024]{1,0:T(8,128)}, f32[64,1024]{1,0:T(8,128)}, u32[]{:S(2)}, u32[]{:S(2)}) %collective-permute-start.28) | collective-permute-done | bytes 262176 | tf_op jit(solution)/shard_map/ppermute | solution.py:44
  101.8 1.5 collective-permute-start.29
  103.3 2.7 %collective-permute-start.27 = (f32[128,1024]{1,0:T(8,128)}, f32[128,1024]{1,0:T(8,128)S(1)}, u32[]{:S(2)}, u32[]{:S(2)}) collective-permute-start(f32[128,1024]{1,0:T(8,128)} %collective-permute-done.14.refs_14_), channel_id=1, source_target_pairs={{0,28},{1,29},{2,30},{3,31},{4,0},{5,1},{6,2},{7,3},{8,4},{9,5},{1... | collective-permute-start | bytes 1572872 | tf_op jit(solution)/shard_map/ppermute | solution.py:44
  105.9 0.9 copy-done.6
  106.9 0.9 copy-done.10
  107.8 0.9 copy-done.12
  108.8 0.9 copy-done.14
  109.7 12.7 %shard_map.50 = (f32[640,512]{1,0:T(8,128)S(1)}, f32[640,512]{1,0:T(8,128)S(1)}, f32[512,1024]{1,0:T(8,128)S(1)}) custom-call(s32[6]{0:T(128)S(1)} %stack.27.s_ref, f32[64,1024]{1,0:T(8,128)S(1)} %get-tuple-element.29.refs_0_, f32[64,1024]{1,0:T(8,128)S(1)} %copy-done.2, f32[128,1024]{1,0:T(8,128)S(1)} %constant_dynamic-update-slice_fusion.refs_2_, ...), custom_call_target="tpu_custom_call" | custom-call | flops 8053063680 | bytes 9437184 | tf_op jit(solution)/shard_map/pallas_call | solution.py:142
  122.5 0.1 collective-permute-start.30
  122.6 2.7 %collective-permute-start.31 = (f32[64,1024]{1,0:T(8,128)S(1)}, f32[64,1024]{1,0:T(8,128)S(1)}, u32[]{:S(2)}, u32[]{:S(2)}) collective-permute-start(f32[64,1024]{1,0:T(8,128)S(1)} %slice.49), channel_id=1, source_target_pairs={{0,28},{1,29},{2,30},{3,31},{4,0},{5,1},{6,2},{7,3},{8,4},{9,5},{1... | collective-permute-start | bytes 786440 | tf_op jit(solution)/shard_map/ppermute | solution.py:44
  125.3 3.8 %collective-permute-start.19 = (f32[640,512]{1,0:T(8,128)S(1)}, f32[640,512]{1,0:T(8,128)S(1)}, u32[]{:S(2)}, u32[]{:S(2)}) collective-permute-start(f32[640,512]{1,0:T(8,128)S(1)} %get-tuple-element.15), channel_id=1, source_target_pairs={{0,1},{1,0},{2,3},{3,2},{4,5},{5,4},{6,7},{7,6},{8,9},{9,8},{10,11... | collective-permute-start | bytes 3932168 | tf_op jit(solution)/shard_map/ppermute | solution.py:44
  129.1 8.1 %shard_map.51 = (f32[384,512]{1,0:T(8,128)S(1)}, f32[384,512]{1,0:T(8,128)S(1)}, f32[128,1024]{1,0:T(8,128)S(1)}, f32[128,1024]{1,0:T(8,128)S(1)}, f32[128,1024]{1,0:T(8,128)S(1)}, /*index=5*/f32[128,1024]{1,0:T(8,128)S(1)}) custom-call(s32[6]{0:T(128)S(1)} %stack.27.s_ref, f32[64,1024]{1,0:T(8,128)S(1)} %copy-done.8, ...), custom_call_target="tpu_custom_call" | custom-call | flops 4831838208 | bytes 7340032 | tf_op jit(solution)/shard_map/pallas_call | solution.py:142
  137.2 4.3 %collective-permute-start.32 = (f32[384,512]{1,0:T(8,128)S(1)}, f32[384,512]{1,0:T(8,128)S(1)}, u32[]{:S(2)}, u32[]{:S(2)}) collective-permute-start(f32[384,512]{1,0:T(8,128)S(1)} %get-tuple-element.21), channel_id=1, source_target_pairs={{0,1},{1,0},{2,3},{3,2},{4,5},{5,4},{6,7},{7,6},{8,9},{9,8},{10,11... | collective-permute-start | bytes 2359304 | tf_op jit(solution)/shard_map/ppermute | solution.py:44
  141.5 1.9 collective-permute-done.32
  143.4 0.1 slice_add_fusion.2
  143.5 0.5 collective-permute-start.33
  144.0 0.1 slice_add_fusion
  144.1 1.1 collective-permute-start.20
  145.3 1.2 collective-permute-start.35
  146.4 2.7 %collective-permute-start.36 = (f32[128,1024]{1,0:T(8,128)S(1)}, f32[128,1024]{1,0:T(8,128)S(1)}, u32[]{:S(2)}, u32[]{:S(2)}) collective-permute-start(f32[128,1024]{1,0:T(8,128)S(1)} %get-tuple-element.24), channel_id=1, source_target_pairs={{0,96},{1,97},{2,98},{3,99},{4,100},{5,101},{6,102},{7,103},{8,104... | collective-permute-start | bytes 1572872 | tf_op jit(solution)/shard_map/ppermute | solution.py:44
  149.2 1.5 collective-permute-start.37
  150.6 3.3 %collective-permute-done.33 = f32[192,512]{1,0:T(8,128)S(1)} collective-permute-done((f32[192,512]{1,0:T(8,128)S(1)}, f32[192,512]{1,0:T(8,128)S(1)}, u32[]{:S(2)}, u32[]{:S(2)}) %collective-permute-start.33) | collective-permute-done | bytes 393248 | tf_op jit(solution)/shard_map/ppermute | solution.py:44
  153.9 0.1 fusion.1
  154.0 25.2 %collective-permute-done.20 = f32[320,512]{1,0:T(8,128)S(1)} collective-permute-done((f32[320,512]{1,0:T(8,128)S(1)}, f32[320,512]{1,0:T(8,128)S(1)}, u32[]{:S(2)}, u32[]{:S(2)}) %collective-permute-start.20) | collective-permute-done | bytes 655392 | tf_op jit(solution)/shard_map/ppermute | solution.py:44
  179.2 0.2 fusion
  179.4 2.6 %collective-permute-start.21 = (f32[320,256]{1,0:T(8,128)S(1)}, f32[320,256]{1,0:T(8,128)S(1)}, u32[]{:S(2)}, u32[]{:S(2)}) collective-permute-start(f32[320,256]{1,0:T(8,128)S(1)} %get-tuple-element.26), channel_id=1, source_target_pairs={{0,96},{1,97},{2,98},{3,99},{4,100},{5,101},{6,102},{7,103},{8,104... | collective-permute-start | bytes 983048 | tf_op jit(solution)/shard_map/ppermute | solution.py:44
  182.0 0.3 collective-permute-start.34
  182.3 8.8 %collective-permute-done.35.refs_5_ = f32[128,1024]{1,0:T(8,128)S(1)} collective-permute-done((f32[128,1024]{1,0:T(8,128)S(1)}, f32[128,1024]{1,0:T(8,128)S(1)}, u32[]{:S(2)}, u32[]{:S(2)}) %collective-permute-start.35) | collective-permute-done | bytes 524320 | tf_op jit(solution)/shard_map/ppermute | solution.py:44
  191.1 1.0 collective-permute-done.34.refs_3_
  192.1 1.8 shard_map.52
  (64 shorter events, 0.3 us)
Async XLA Ops:
  0.6 5.7 %copy-start.15 = (f32[64,2048]{1,0:T(8,128)S(1)}, f32[64,2048]{1,0:T(8,128)}, u32[]{:S(2)}) copy-start(f32[64,2048]{1,0:T(8,128)} %param.4) | copy-start | bytes 1572868
  3.0 56.8 %collective-permute-start.15 = (f32[1024,256]{1,0:T(8,128)}, f32[1024,256]{1,0:T(8,128)}, u32[]{:S(2)}, u32[]{:S(2)}) collective-permute-start(f32[1024,256]{1,0:T(8,128)} %bitcast.7), channel_id=1, source_target_pairs={{0,96},{1,97},{2,98},{3,99},{4,100},{5,101},{6,102},{7,103},{8,104... | collective-permute-start | bytes 3145736 | tf_op jit(solution)/shard_map/ppermute | solution.py:44
  6.3 27.6 %collective-permute-start.1 = (f32[64,1024]{1,0:T(8,128)S(1)}, f32[64,1024]{1,0:T(8,128)S(1)}, u32[]{:S(2)}, u32[]{:S(2)}) collective-permute-start(f32[64,1024]{1,0:T(8,128)S(1)} %get-tuple-element.28), channel_id=1, source_target_pairs={{0,96},{1,97},{2,98},{3,99},{4,100},{5,101},{6,102},{7,103},{8,104... | collective-permute-start | bytes 786440 | tf_op jit(solution)/shard_map/ppermute | solution.py:44
  6.4 28.5 %collective-permute-start.3 = (f32[64,1024]{1,0:T(8,128)S(1)}, f32[64,1024]{1,0:T(8,128)}, u32[]{:S(2)}, u32[]{:S(2)}) collective-permute-start(f32[64,1024]{1,0:T(8,128)S(1)} %get-tuple-element.29.refs_0_), channel_id=1, source_target_pairs={{0,4},{1,5},{2,6},{3,7},{4,8},{5,9},{6,10},{7,11},{8,12},{9,13},{1... | collective-permute-start | bytes 786440 | tf_op jit(solution)/shard_map/ppermute | solution.py:44
  8.3 27.2 %collective-permute-start = (f32[64,1024]{1,0:T(8,128)S(1)}, f32[64,1024]{1,0:T(8,128)S(1)}, u32[]{:S(2)}, u32[]{:S(2)}) collective-permute-start(f32[64,1024]{1,0:T(8,128)S(1)} %get-tuple-element.29.refs_0_), channel_id=1, source_target_pairs={{0,32},{1,33},{2,34},{3,35},{4,36},{5,37},{6,38},{7,39},{8,40},{9,... | collective-permute-start | bytes 786440 | tf_op jit(solution)/shard_map/ppermute | solution.py:44
  8.3 31.5 %collective-permute-start.6 = (f32[64,1024]{1,0:T(8,128)S(1)}, f32[64,1024]{1,0:T(8,128)}, u32[]{:S(2)}, u32[]{:S(2)}) collective-permute-start(f32[64,1024]{1,0:T(8,128)S(1)} %get-tuple-element.29.refs_0_), channel_id=1, source_target_pairs={{0,28},{1,29},{2,30},{3,31},{4,0},{5,1},{6,2},{7,3},{8,4},{9,5},{1... | collective-permute-start | bytes 786440 | tf_op jit(solution)/shard_map/ppermute | solution.py:44
  33.9 8.4 %collective-permute-start.2 = (f32[64,1024]{1,0:T(8,128)S(1)}, f32[64,1024]{1,0:T(8,128)S(1)}, u32[]{:S(2)}, u32[]{:S(2)}) collective-permute-start(f32[64,1024]{1,0:T(8,128)S(1)} %collective-permute-done.1), channel_id=1, source_target_pairs={{0,32},{1,33},{2,34},{3,35},{4,36},{5,37},{6,38},{7,39},{8,40},{9,... | collective-permute-start | bytes 786440 | tf_op jit(solution)/shard_map/ppermute | solution.py:44
  34.9 10.3 %collective-permute-start.4 = (f32[64,1024]{1,0:T(8,128)}, f32[64,1024]{1,0:T(8,128)S(1)}, u32[]{:S(2)}, u32[]{:S(2)}) collective-permute-start(f32[64,1024]{1,0:T(8,128)} %collective-permute-done.3.refs_3_), channel_id=1, source_target_pairs={{0,32},{1,33},{2,34},{3,35},{4,36},{5,37},{6,38},{7,39},{8,40},{9,... | collective-permute-start | bytes 786440 | tf_op jit(solution)/shard_map/ppermute | solution.py:44
  35.4 0.7 copy-start.1
  36.1 17.0 %collective-permute-start.9 = (f32[64,1024]{1,0:T(8,128)}, f32[64,1024]{1,0:T(8,128)}, u32[]{:S(2)}, u32[]{:S(2)}) collective-permute-start(f32[64,1024]{1,0:T(8,128)} %collective-permute-done.3.refs_3_), channel_id=1, source_target_pairs={{0,4},{1,5},{2,6},{3,7},{4,8},{5,9},{6,10},{7,11},{8,12},{9,13},{1... | collective-permute-start | bytes 786440 | tf_op jit(solution)/shard_map/ppermute | solution.py:44
  39.8 27.0 %collective-permute-start.17 = (f32[128,1024]{1,0:T(8,128)S(1)}, f32[128,1024]{1,0:T(8,128)S(1)}, u32[]{:S(2)}, u32[]{:S(2)}) collective-permute-start(f32[128,1024]{1,0:T(8,128)S(1)} %dynamic_slice.20), channel_id=1, source_target_pairs={{0,96},{1,97},{2,98},{3,99},{4,100},{5,101},{6,102},{7,103},{8,104... | collective-permute-start | bytes 1572872 | tf_op jit(solution)/shard_map/ppermute | solution.py:44
  42.4 10.8 %copy-start.16 = (f32[64,1024]{1,0:T(8,128)}, f32[64,1024]{1,0:T(8,128)S(1)}, u32[]{:S(2)}) copy-start(f32[64,1024]{1,0:T(8,128)S(1)} %collective-permute-done.2) | copy-start | bytes 786436
  42.4 12.0 %collective-permute-start.7 = (f32[64,1024]{1,0:T(8,128)}, f32[64,1024]{1,0:T(8,128)S(1)}, u32[]{:S(2)}, u32[]{:S(2)}) collective-permute-start(f32[64,1024]{1,0:T(8,128)} %collective-permute-done.6.refs_6_), channel_id=1, source_target_pairs={{0,32},{1,33},{2,34},{3,35},{4,36},{5,37},{6,38},{7,39},{8,40},{9,... | collective-permute-start | bytes 786440 | tf_op jit(solution)/shard_map/ppermute | solution.py:44
  45.2 0.7 copy-start.3
  45.9 10.9 %collective-permute-start.12 = (f32[64,1024]{1,0:T(8,128)}, f32[64,1024]{1,0:T(8,128)S(1)}, u32[]{:S(2)}, u32[]{:S(2)}) collective-permute-start(f32[64,1024]{1,0:T(8,128)} %collective-permute-done.6.refs_6_), channel_id=1, source_target_pairs={{0,28},{1,29},{2,30},{3,31},{4,0},{5,1},{6,2},{7,3},{8,4},{9,5},{1... | collective-permute-start | bytes 786440 | tf_op jit(solution)/shard_map/ppermute | solution.py:44
  53.1 52.8 %copy-start = (f32[2048,256]{1,0:T(8,128)S(1)}, f32[2048,256]{1,0:T(8,128)}, u32[]{:S(2)}) copy-start(f32[2048,256]{1,0:T(8,128)} %refs_10_.1) | copy-start | bytes 6291460
  53.2 13.6 %collective-permute-start.10 = (f32[64,1024]{1,0:T(8,128)}, f32[64,1024]{1,0:T(8,128)S(1)}, u32[]{:S(2)}, u32[]{:S(2)}) collective-permute-start(f32[64,1024]{1,0:T(8,128)} %collective-permute-done.9.refs_9_), channel_id=1, source_target_pairs={{0,32},{1,33},{2,34},{3,35},{4,36},{5,37},{6,38},{7,39},{8,40},{9,... | collective-permute-start | bytes 786440 | tf_op jit(solution)/shard_map/ppermute | solution.py:44
  54.4 0.7 copy-start.5
  55.1 23.9 %collective-permute-start.5 = (f32[128,1024]{1,0:T(8,128)S(1)}, f32[128,1024]{1,0:T(8,128)}, u32[]{:S(2)}, u32[]{:S(2)}) collective-permute-start(f32[128,1024]{1,0:T(8,128)S(1)} %constant_dynamic-update-slice_fusion.refs_2_), channel_id=1, source_target_pairs={{0,4},{1,5},{2,6},{3,7},{4,8},{5,9},{6,10},{7,11},{8,12},{9,13},{1... | collective-permute-start | bytes 1572872 | tf_op jit(solution)/shard_map/ppermute | solution.py:44
  56.8 23.6 %collective-permute-start.8 = (f32[128,1024]{1,0:T(8,128)S(1)}, f32[128,1024]{1,0:T(8,128)}, u32[]{:S(2)}, u32[]{:S(2)}) collective-permute-start(f32[128,1024]{1,0:T(8,128)S(1)} %constant_dynamic-update-slice_fusion.refs_2_), channel_id=1, source_target_pairs={{0,28},{1,29},{2,30},{3,31},{4,0},{5,1},{6,2},{7,3},{8,4},{9,5},{1... | collective-permute-start | bytes 1572872 | tf_op jit(solution)/shard_map/ppermute | solution.py:44
  59.8 43.5 %collective-permute-start.16 = (f32[1024,256]{1,0:T(8,128)}, f32[1024,256]{1,0:T(8,128)}, u32[]{:S(2)}, u32[]{:S(2)}) collective-permute-start(f32[1024,256]{1,0:T(8,128)} %collective-permute-done.15.refs_16_.refs_11_), channel_id=1, source_target_pairs={{0,1},{1,0},{2,3},{3,2},{4,5},{5,4},{6,7},{7,6},{8,9},{9,8},{10,11... | collective-permute-start | bytes 3145736 | tf_op jit(solution)/shard_map/ppermute | solution.py:44
  66.8 7.8 %collective-permute-start.13 = (f32[64,1024]{1,0:T(8,128)S(1)}, f32[64,1024]{1,0:T(8,128)S(1)}, u32[]{:S(2)}, u32[]{:S(2)}) collective-permute-start(f32[64,1024]{1,0:T(8,128)S(1)} %collective-permute-done.12.refs_12_), channel_id=1, source_target_pairs={{0,32},{1,33},{2,34},{3,35},{4,36},{5,37},{6,38},{7,39},{8,40},{9,... | collective-permute-start | bytes 786440 | tf_op jit(solution)/shard_map/ppermute | solution.py:44
  66.8 0.7 copy-start.11
  67.5 10.7 %collective-permute-start.22 = (f32[64,1024]{1,0:T(8,128)}, f32[64,1024]{1,0:T(8,128)S(1)}, u32[]{:S(2)}, u32[]{:S(2)}) collective-permute-start(f32[64,1024]{1,0:T(8,128)} %collective-permute-done.9.refs_9_), channel_id=1, source_target_pairs={{0,4},{1,5},{2,6},{3,7},{4,8},{5,9},{6,10},{7,11},{8,12},{9,13},{1... | collective-permute-start | bytes 786440 | tf_op jit(solution)/shard_map/ppermute | solution.py:44
  74.6 0.7 copy-start.13
  75.3 14.1 %collective-permute-start.18 = (f32[128,1024]{1,0:T(8,128)S(1)}, f32[128,1024]{1,0:T(8,128)}, u32[]{:S(2)}, u32[]{:S(2)}) collective-permute-start(f32[128,1024]{1,0:T(8,128)S(1)} %collective-permute-done.17.refs_19_.refs_14_), channel_id=1, source_target_pairs={{0,128},{1,129},{2,130},{3,131},{4,132},{5,133},{6,134},{7,135},{8... | collective-permute-start | bytes 1572872 | tf_op jit(solution)/shard_map/ppermute | solution.py:44
  78.2 2.2 %copy-start.7 = (f32[64,1024]{1,0:T(8,128)}, f32[64,1024]{1,0:T(8,128)S(1)}, u32[]{:S(2)}) copy-start(f32[64,1024]{1,0:T(8,128)S(1)} %collective-permute-done.22.refs_0_) | copy-start | bytes 786436
  78.2 6.7 %collective-permute-start.25 = (f32[64,1024]{1,0:T(8,128)S(1)}, f32[64,1024]{1,0:T(8,128)}, u32[]{:S(2)}, u32[]{:S(2)}) collective-permute-start(f32[64,1024]{1,0:T(8,128)S(1)} %collective-permute-done.12.refs_12_), channel_id=1, source_target_pairs={{0,28},{1,29},{2,30},{3,31},{4,0},{5,1},{6,2},{7,3},{8,4},{9,5},{1... | collective-permute-start | bytes 786440 | tf_op jit(solution)/shard_map/ppermute | solution.py:44
  78.2 0.7 copy-start.9
  78.9 22.9 %collective-permute-start.11 = (f32[128,1024]{1,0:T(8,128)}, f32[128,1024]{1,0:T(8,128)}, u32[]{:S(2)}, u32[]{:S(2)}) collective-permute-start(f32[128,1024]{1,0:T(8,128)} %collective-permute-done.5.refs_5_), channel_id=1, source_target_pairs={{0,4},{1,5},{2,6},{3,7},{4,8},{5,9},{6,10},{7,11},{8,12},{9,13},{1... | collective-permute-start | bytes 1572872 | tf_op jit(solution)/shard_map/ppermute | solution.py:44
  80.4 22.9 %collective-permute-start.14 = (f32[128,1024]{1,0:T(8,128)}, f32[128,1024]{1,0:T(8,128)}, u32[]{:S(2)}, u32[]{:S(2)}) collective-permute-start(f32[128,1024]{1,0:T(8,128)} %collective-permute-done.8.refs_8_), channel_id=1, source_target_pairs={{0,28},{1,29},{2,30},{3,31},{4,0},{5,1},{6,2},{7,3},{8,4},{9,5},{1... | collective-permute-start | bytes 1572872 | tf_op jit(solution)/shard_map/ppermute | solution.py:44
  84.9 16.9 %collective-permute-start.28 = (f32[64,1024]{1,0:T(8,128)}, f32[64,1024]{1,0:T(8,128)}, u32[]{:S(2)}, u32[]{:S(2)}) collective-permute-start(f32[64,1024]{1,0:T(8,128)} %collective-permute-done.25.refs_3_), channel_id=1, source_target_pairs={{0,28},{1,29},{2,30},{3,31},{4,0},{5,1},{6,2},{7,3},{8,4},{9,5},{1... | collective-permute-start | bytes 786440 | tf_op jit(solution)/shard_map/ppermute | solution.py:44
  86.4 19.5 %copy-start.2 = (f32[64,1024]{1,0:T(8,128)S(1)}, f32[64,1024]{1,0:T(8,128)}, u32[]{:S(2)}) copy-start(f32[64,1024]{1,0:T(8,128)} %copy-done.1) | copy-start | bytes 786436
  86.4 19.5 %copy-start.4 = (f32[64,1024]{1,0:T(8,128)S(1)}, f32[64,1024]{1,0:T(8,128)}, u32[]{:S(2)}) copy-start(f32[64,1024]{1,0:T(8,128)} %copy-done.3) | copy-start | bytes 786436
  89.4 39.7 %collective-permute-start.26 = (f32[64,1024]{1,0:T(8,128)}, f32[64,1024]{1,0:T(8,128)S(1)}, u32[]{:S(2)}, u32[]{:S(2)}) collective-permute-start(f32[64,1024]{1,0:T(8,128)} %collective-permute-done.25.refs_3_), channel_id=1, source_target_pairs={{0,32},{1,33},{2,34},{3,35},{4,36},{5,37},{6,38},{7,39},{8,40},{9,... | collective-permute-start | bytes 786440 | tf_op jit(solution)/shard_map/ppermute | solution.py:44
  101.8 23.6 %collective-permute-start.23 = (f32[64,1024]{1,0:T(8,128)}, f32[64,1024]{1,0:T(8,128)S(1)}, u32[]{:S(2)}, u32[]{:S(2)}) collective-permute-start(f32[64,1024]{1,0:T(8,128)} %copy-done.7), channel_id=1, source_target_pairs={{0,32},{1,33},{2,34},{3,35},{4,36},{5,37},{6,38},{7,39},{8,40},{9,... | collective-permute-start | bytes 786440 | tf_op jit(solution)/shard_map/ppermute | solution.py:44
  101.8 27.3 %collective-permute-start.29 = (f32[64,1024]{1,0:T(8,128)}, f32[64,1024]{1,0:T(8,128)S(1)}, u32[]{:S(2)}, u32[]{:S(2)}) collective-permute-start(f32[64,1024]{1,0:T(8,128)} %collective-permute-done.28.refs_6_), channel_id=1, source_target_pairs={{0,32},{1,33},{2,34},{3,35},{4,36},{5,37},{6,38},{7,39},{8,40},{9,... | collective-permute-start | bytes 786440 | tf_op jit(solution)/shard_map/ppermute | solution.py:44
  103.3 19.2 %collective-permute-start.24 = (f32[128,1024]{1,0:T(8,128)}, f32[128,1024]{1,0:T(8,128)S(1)}, u32[]{:S(2)}, u32[]{:S(2)}) collective-permute-start(f32[128,1024]{1,0:T(8,128)} %collective-permute-done.11.refs_11_), channel_id=1, source_target_pairs={{0,4},{1,5},{2,6},{3,7},{4,8},{5,9},{6,10},{7,11},{8,12},{9,13},{1... | collective-permute-start | bytes 1572872 | tf_op jit(solution)/shard_map/ppermute | solution.py:44
  103.3 19.2 %collective-permute-start.27 = (f32[128,1024]{1,0:T(8,128)}, f32[128,1024]{1,0:T(8,128)S(1)}, u32[]{:S(2)}, u32[]{:S(2)}) collective-permute-start(f32[128,1024]{1,0:T(8,128)} %collective-permute-done.14.refs_14_), channel_id=1, source_target_pairs={{0,28},{1,29},{2,30},{3,31},{4,0},{5,1},{6,2},{7,3},{8,4},{9,5},{1... | collective-permute-start | bytes 1572872 | tf_op jit(solution)/shard_map/ppermute | solution.py:44
  105.9 1.0 copy-start.6
  106.9 0.9 copy-start.10
  107.8 0.9 copy-start.12
  108.8 0.9 copy-start.14
  109.7 19.4 %copy-start.8 = (f32[64,1024]{1,0:T(8,128)S(1)}, f32[64,1024]{1,0:T(8,128)}, u32[]{:S(2)}) copy-start(f32[64,1024]{1,0:T(8,128)} %copy-done.7) | copy-start | bytes 786436
  122.5 6.6 %collective-permute-start.30 = (f32[64,1024]{1,0:T(8,128)S(1)}, f32[64,1024]{1,0:T(8,128)S(1)}, u32[]{:S(2)}, u32[]{:S(2)}) collective-permute-start(f32[64,1024]{1,0:T(8,128)S(1)} %slice.48), channel_id=1, source_target_pairs={{0,4},{1,5},{2,6},{3,7},{4,8},{5,9},{6,10},{7,11},{8,12},{9,13},{1... | collective-permute-start | bytes 786440 | tf_op jit(solution)/shard_map/ppermute | solution.py:44
  122.6 6.5 %collective-permute-start.31 = (f32[64,1024]{1,0:T(8,128)S(1)}, f32[64,1024]{1,0:T(8,128)S(1)}, u32[]{:S(2)}, u32[]{:S(2)}) collective-permute-start(f32[64,1024]{1,0:T(8,128)S(1)} %slice.49), channel_id=1, source_target_pairs={{0,28},{1,29},{2,30},{3,31},{4,0},{5,1},{6,2},{7,3},{8,4},{9,5},{1... | collective-permute-start | bytes 786440 | tf_op jit(solution)/shard_map/ppermute | solution.py:44
  125.3 18.7 %collective-permute-start.19 = (f32[640,512]{1,0:T(8,128)S(1)}, f32[640,512]{1,0:T(8,128)S(1)}, u32[]{:S(2)}, u32[]{:S(2)}) collective-permute-start(f32[640,512]{1,0:T(8,128)S(1)} %get-tuple-element.15), channel_id=1, source_target_pairs={{0,1},{1,0},{2,3},{3,2},{4,5},{5,4},{6,7},{7,6},{8,9},{9,8},{10,11... | collective-permute-start | bytes 3932168 | tf_op jit(solution)/shard_map/ppermute | solution.py:44
  137.2 6.2 %collective-permute-start.32 = (f32[384,512]{1,0:T(8,128)S(1)}, f32[384,512]{1,0:T(8,128)S(1)}, u32[]{:S(2)}, u32[]{:S(2)}) collective-permute-start(f32[384,512]{1,0:T(8,128)S(1)} %get-tuple-element.21), channel_id=1, source_target_pairs={{0,1},{1,0},{2,3},{3,2},{4,5},{5,4},{6,7},{7,6},{8,9},{9,8},{10,11... | collective-permute-start | bytes 2359304 | tf_op jit(solution)/shard_map/ppermute | solution.py:44
  143.5 10.4 %collective-permute-start.33 = (f32[192,512]{1,0:T(8,128)S(1)}, f32[192,512]{1,0:T(8,128)S(1)}, u32[]{:S(2)}, u32[]{:S(2)}) collective-permute-start(f32[192,512]{1,0:T(8,128)S(1)} %slice_add_fusion.2), channel_id=1, source_target_pairs={{0,2},{1,3},{2,0},{3,1},{4,6},{5,7},{6,4},{7,5},{8,10},{9,11},{10,... | collective-permute-start | bytes 1179656 | tf_op jit(solution)/shard_map/ppermute | solution.py:44
  144.1 35.1 %collective-permute-start.20 = (f32[320,512]{1,0:T(8,128)S(1)}, f32[320,512]{1,0:T(8,128)S(1)}, u32[]{:S(2)}, u32[]{:S(2)}) collective-permute-start(f32[320,512]{1,0:T(8,128)S(1)} %slice_add_fusion), channel_id=1, source_target_pairs={{0,2},{1,3},{2,0},{3,1},{4,6},{5,7},{6,4},{7,5},{8,10},{9,11},{10,... | collective-permute-start | bytes 1966088 | tf_op jit(solution)/shard_map/ppermute | solution.py:44
  145.3 45.9 %collective-permute-start.35 = (f32[128,1024]{1,0:T(8,128)S(1)}, f32[128,1024]{1,0:T(8,128)S(1)}, u32[]{:S(2)}, u32[]{:S(2)}) collective-permute-start(f32[128,1024]{1,0:T(8,128)S(1)} %get-tuple-element.23), channel_id=1, source_target_pairs={{0,128},{1,129},{2,130},{3,131},{4,132},{5,133},{6,134},{7,135},{8... | collective-permute-start | bytes 1572872 | tf_op jit(solution)/shard_map/ppermute | solution.py:44
  146.4 44.7 %collective-permute-start.36 = (f32[128,1024]{1,0:T(8,128)S(1)}, f32[128,1024]{1,0:T(8,128)S(1)}, u32[]{:S(2)}, u32[]{:S(2)}) collective-permute-start(f32[128,1024]{1,0:T(8,128)S(1)} %get-tuple-element.24), channel_id=1, source_target_pairs={{0,96},{1,97},{2,98},{3,99},{4,100},{5,101},{6,102},{7,103},{8,104... | collective-permute-start | bytes 1572872 | tf_op jit(solution)/shard_map/ppermute | solution.py:44
  149.2 41.9 %collective-permute-start.37 = (f32[128,1024]{1,0:T(8,128)S(1)}, f32[128,1024]{1,0:T(8,128)S(1)}, u32[]{:S(2)}, u32[]{:S(2)}) collective-permute-start(f32[128,1024]{1,0:T(8,128)S(1)} %get-tuple-element.25), channel_id=1, source_target_pairs={{0,224},{1,225},{2,226},{3,227},{4,228},{5,229},{6,230},{7,231},{8... | collective-permute-start | bytes 1572872 | tf_op jit(solution)/shard_map/ppermute | solution.py:44
  179.4 12.7 %collective-permute-start.21 = (f32[320,256]{1,0:T(8,128)S(1)}, f32[320,256]{1,0:T(8,128)S(1)}, u32[]{:S(2)}, u32[]{:S(2)}) collective-permute-start(f32[320,256]{1,0:T(8,128)S(1)} %get-tuple-element.26), channel_id=1, source_target_pairs={{0,96},{1,97},{2,98},{3,99},{4,100},{5,101},{6,102},{7,103},{8,104... | collective-permute-start | bytes 983048 | tf_op jit(solution)/shard_map/ppermute | solution.py:44
  182.0 10.1 %collective-permute-start.34 = (f32[192,256]{1,0:T(8,128)S(1)}, f32[192,256]{1,0:T(8,128)S(1)}, u32[]{:S(2)}, u32[]{:S(2)}) collective-permute-start(f32[192,256]{1,0:T(8,128)S(1)} %get-tuple-element.30), channel_id=1, source_target_pairs={{0,96},{1,97},{2,98},{3,99},{4,100},{5,101},{6,102},{7,103},{8,104... | collective-permute-start | bytes 589832 | tf_op jit(solution)/shard_map/ppermute | solution.py:44

commit v5 on v4

--- a/solution.py
+++ b/solution.py
@@ -12,8 +12,9 @@
 ROWS = 64
 COLS = 1024
 FEAT = 256
-GROUPS = ((0, 7, 1, 6, 2), (5, 3, 4))
-TILES = (256, 256)
+GROUPS = ((0, 7, 1, 6, 2), (5, 3), (5, 3, 4))
+BATCHES = ((0, 7, 1, 6, 2), (5, 3), (4,))
+TILES = (256, 256, 512)
 
 
 def pairs(move):
@@ -37,7 +38,6 @@
 CORE = pairs(lambda t, x, z, y, c: (t, x, z, y, 1 - c))
 YLOW = pairs(lambda t, x, z, y, c: (t, x, z, 1 - y, c))
 TOK = pairs(lambda t, x, z, y, c: (1 - t, x, z, y, c))
-DIAG = pairs(lambda t, x, z, y, c: (1 - t, x ^ 3, z, y, c))
 
 
 def send(value, perm):
@@ -54,15 +54,17 @@
     return lax.dot_general(a, b, (dims, ((), ())), preferred_element_type=jnp.float32)
 
 
-def group_body(layout, turns, tile, first, last, s_ref, *refs):
+def group_body(layout, turns, tile, emit, outer, first, last, s_ref, *refs):
     refs = list(refs)
     take = lambda k: [refs.pop(0) for _ in range(k)]
     pieces = take(len(layout))
-    a_own, a_near, a_far, w_own, w_a, w_b = take(6)
-    wg_in = None if first else take(1)[0]
+    a_own, a_near, a_far = take(3) if outer else (None,) * 3
+    w_own, w_a, w_b = take(3)
+    wg_in = take(1)[0] if outer and not first else None
     keep_ref, send_ref = take(2)
-    wg_refs = take(4 if last else 1)
-    bufs, (thi, tlo) = (refs[:2], refs[2:4]), refs[4:]
+    wg_refs = take((4 if last else 1) if outer else 0)
+    bufs = (refs[:2], refs[2:4])
+    thi, tlo = refs[4:] if outer else (None, None)
     n = len(turns)
     span = n * ROWS
     spin, tok, fout, z, y = (s_ref[k] for k in range(5))
@@ -74,7 +76,7 @@
         return ref[pl.ds(pl.multiple_of(at, ROWS), ROWS), :]
 
     slots = [(cr, yr, r) for cr in range(2) for yr in range(2) for r in turns]
-    for g in range(n):
+    for g in range(n if outer else 0):
         four = slots[4 * g : 4 * g + 4]
         own = [rows_of(a_own, fout ^ (cr | yr << 1), r) for cr, yr, r in four]
         mate = [rows_of(a_far if cr else a_near, y ^ yr, r) for cr, yr, r in four]
@@ -104,9 +106,15 @@
         wcat[other(FEAT), :] = w_b[:, cols]
         whi, wlo = split(wcat[...])
         w2 = jnp.concatenate([whi, whi], axis=1)
-        sums = dot(gl[...], w2, nt) + dot(gl[:, high], wlo, nt)
-        keep_ref[...] += sums[: 2 * span]
-        send_ref[...] += sums[2 * span :]
+        if len(emit) == n:
+            rows = gl[...]
+        else:
+            rows = jnp.concatenate([gl[pl.ds(q * span + k * ROWS, ROWS), :] for q in range(4) for k in emit], axis=0)
+        sums = dot(rows, w2, nt) + dot(rows[:, :tile], wlo, nt)
+        keep_ref[...] += sums[: 2 * len(emit) * ROWS]
+        send_ref[...] += sums[2 * len(emit) * ROWS :]
+        if not outer:
+            return
         acc = dot(thi[...], gl[:, high], nn) + dot(thi[...], gl[:, low], nn) + dot(tlo[...], gl[:, high], nn)
         if not first:
             acc = acc + wg_in[:, cols]
@@ -127,27 +135,28 @@
 
 def group(index, scalars, pieces, layout, acts, weights, wg):
     turns, tile = GROUPS[index], TILES[index]
-    first, last = wg is None, index == len(GROUPS) - 1
-    span = len(turns) * ROWS
-    rows = 4 * span
-    args = [scalars, *pieces, *acts, *weights]
-    if not first:
+    emit = tuple(k for k, r in enumerate(turns) if r in BATCHES[index])
+    outer, first, last = index != 1, wg is None, index == len(GROUPS) - 1
+    rows = 4 * len(turns) * ROWS
+    args = [scalars, *pieces, *(acts if outer else ()), *weights]
+    if outer and not first:
         args.append(wg)
     vmem = pl.BlockSpec(memory_space=pltpu.VMEM)
-    share = jax.ShapeDtypeStruct((2 * span, 2 * FEAT), jnp.float32)
-    if last:
+    share = jax.ShapeDtypeStruct((2 * len(emit) * ROWS, 2 * FEAT), jnp.float32)
+    grads = []
+    if outer and last:
         grads = [jax.ShapeDtypeStruct((128, COLS), jnp.float32)] * 4
-    else:
+    elif outer:
         grads = [jax.ShapeDtypeStruct((2 * FEAT, COLS), jnp.float32)]
+    scratch = [pltpu.VMEM((rows, 2 * tile), jnp.bfloat16)] * 2 + [pltpu.VMEM((2 * FEAT, tile), jnp.float32)] * 2
+    if outer:
+        scratch += [pltpu.VMEM((2 * FEAT, rows), jnp.bfloat16)] * 2
     return pl.pallas_call(
-        functools.partial(group_body, layout, turns, tile, first, last),
+        functools.partial(group_body, layout, turns, tile, emit, outer, first, last),
         in_specs=[pl.BlockSpec(memory_space=pltpu.SMEM)] + [vmem] * (len(args) - 1),
         out_specs=[vmem] * (2 + len(grads)),
         out_shape=[share, share, *grads],
-        scratch_shapes=[pltpu.VMEM((rows, 2 * tile), jnp.bfloat16)] * 2
-        + [pltpu.VMEM((2 * FEAT, tile), jnp.float32)] * 2
-        + [pltpu.VMEM((2 * FEAT, rows), jnp.bfloat16)] * 2,
-        input_output_aliases={} if first or last else {len(args) - 1: 2},
+        scratch_shapes=scratch,
         compiler_params=pltpu.CompilerParams(vmem_limit_bytes=20 << 20),
         cost_estimate=pl.CostEstimate(
             flops=24 * rows * COLS * FEAT, bytes_accessed=4 * (rows * COLS + 4 * FEAT * COLS), transcendentals=0
@@ -156,9 +165,9 @@
 
 
 def finish_body(s_ref, *refs):
-    shares, grads, (in_ref, wg_ref) = refs[:4], refs[4:8], refs[8:]
+    shares, grads, (in_ref, wg_ref) = refs[:6], refs[6:9], refs[9:]
     z, half = s_ref[3], s_ref[5]
-    for g, turns in enumerate(GROUPS):
+    for g, turns in enumerate(BATCHES):
         for k, r in enumerate(turns):
             at = pl.multiple_of(lax.rem(z + r, NZ) * ROWS, ROWS)
             rows = pl.ds(k * ROWS, ROWS)
@@ -166,14 +175,14 @@
     here = pl.ds(pl.multiple_of(half * COLS, COLS), COLS)
     there = pl.ds(pl.multiple_of((1 - half) * COLS, COLS), COLS)
     wg_ref[:, here] = grads[0][...] + grads[1][...]
-    wg_ref[:, there] = grads[2][...] + grads[3][...]
+    wg_ref[:, there] = grads[2][...]
 
 
 def finish(scalars, shares, grads):
     vmem = pl.BlockSpec(memory_space=pltpu.VMEM)
     return pl.pallas_call(
         finish_body,
-        in_specs=[pl.BlockSpec(memory_space=pltpu.SMEM)] + [vmem] * 8,
+        in_specs=[pl.BlockSpec(memory_space=pltpu.SMEM)] + [vmem] * 9,
         out_shape=[
             jax.ShapeDtypeStruct((NZ * ROWS, FEAT), jnp.float32),
             jax.ShapeDtypeStruct((FEAT // 2, 2 * COLS), jnp.float32),
@@ -236,13 +245,22 @@
                 layout.append(((0, 3, k), (ROWS, 2, k)))
         out = group(i, scalars, pieces, tuple(layout), (acts, a_near, a_far), (w_own, w_a, w_b), wg)
         keep, give = out[:2]
-        wg = out[2] if len(out) == 3 else out[2:]
-        span = ROWS * len(turns)
+        if i != 1:
+            wg = out[2] if len(out) == 3 else out[2:]
+        span = ROWS * len(BATCHES[i])
         got = send(give, CORE)
-        mine = keep[:span] + got[:span] + send(keep[span:] + got[span:], YLOW)
-        shares += [mine[:, :FEAT], send(mine[:, FEAT:], MATE)]
-
-    far = (send(wg[1], TOK), send(wg[2], MATE), send(wg[3], DIAG))
+        if i == 0:
+            other = send(keep[span:] + got[span:], YLOW)
+            mine = keep[:span] + got[:span] + other
+            give = mine[:, FEAT:]
+            shares += [mine[:, :FEAT], send(give, MATE)]
+        else:
+            give = keep[:, FEAT:] + got[:, FEAT:]
+            both = keep[:, :FEAT] + got[:, :FEAT] + send(give, MATE)
+            shares += [both[:span], send(both[span:], YLOW)]
+
+    there = send(wg[2] + send(wg[3], TOK), MATE)
+    far = (send(wg[1], TOK), there)
     return finish(scalars, shares, (wg[0], *far))
 
 

time: 196 us -> 192 us (0.980)
  waiting for transfers between devices: 90.8 us -> 83.5 us
  starting transfers between devices: 65 us -> 69.4 us
    ppermute x38 -> x41, waiting for transfers between devices: 90.8 us -> 83.5 us  [send(): return lax.ppermute(value, AXES, perm)]
    ppermute x38 -> x41, starting transfers between devices: 65 us -> 69.4 us  [send(): return lax.ppermute(value, AXES, perm)]
    unnamed x35 -> x27, local copies, waits for them, and re-layouts: 8.07 us -> 6.38 us
    pallas_call x2 -> x3, Pallas kernels: 20.8 us -> 22.2 us  [group(): pl.pallas_call(functools.partial(group_body, layout, turns, tile, emit, o...]
  transfers between devices with their start and end apart: 38 -> 41, of which waited for: 12 -> 10; matrix products, arithmetic and copies ran while one was open for 2% -> 2% of each run, Pallas kernels for 11% -> 12%
where the time goes in v5:
time: 192 us; the launch traced here: 191 us
  waiting for transfers between devices  83.5 us (43%)
  starting transfers between devices  69.4 us (36%)
  Pallas kernels  24 us (12%)
  local copies, waits for them, and re-layouts  12.4 us (6%)
    ppermute x41, waiting for transfers between devices, send(): return lax.ppermute(value, AXES, perm)  83.5 us
    ppermute x41, starting transfers between devices, send(): return lax.ppermute(value, AXES, perm)  69.4 us
    pallas_call x3, Pallas kernels, group(): pl.pallas_call(functools.partial(group_body, layout, turns, tile, emit, o...  22.2 us
    unnamed x27, local copies, waits for them, and re-layouts  6.38 us
  transfers between devices with their start and end apart: 41, of which 10 were waited for; matrix products, arithmetic and copies ran while one was open for 2% of the time, Pallas kernels for 12%

profile of v5, /device:TPU:1, one launch (start us, length us, event | category | flops | bytes accessed | tf_op | source)
XLA Modules:
  0.0 190.6 jit_solution(650563808931114304)
XLA Ops:
  0.7 2.3 %constant_dynamic-slice_fusion.1 = f32[2,1,512,256]{3,2,1,0:T(8,128)} fusion(f32[2,2,512,256]{3,2,1,0:T(8,128)} %bitcast.10, s32[]{:T(128)S(6)} %select_n.43), kind=kLoop, calls=%fused_computation.12 | loop fusion | bytes 2097156 | tf_op jit(solution)/shard_map/jit(dynamic_index_in_dim)/dynamic_slice | solution.py:196
  3.0 3.3 %collective-permute-start.15 = (f32[1024,256]{1,0:T(8,128)}, f32[1024,256]{1,0:T(8,128)}, u32[]{:S(2)}, u32[]{:S(2)}) collective-permute-start(f32[1024,256]{1,0:T(8,128)} %bitcast.7), channel_id=1, source_target_pairs={{0,96},{1,97},{2,98},{3,99},{4,100},{5,101},{6,102},{7,103},{8,104... | collective-permute-start | bytes 3145736 | tf_op jit(solution)/shard_map/ppermute | solution.py:44
  6.3 0.1 collective-permute-start.1
  6.4 1.8 collective-permute-start.3
  8.3 4.0 %collective-permute-start.6 = (f32[64,1024]{1,0:T(8,128)S(1)}, f32[64,1024]{1,0:T(8,128)}, u32[]{:S(2)}, u32[]{:S(2)}) collective-permute-start(f32[64,1024]{1,0:T(8,128)S(1)} %get-tuple-element.33.refs_0_), channel_id=1, source_target_pairs={{0,28},{1,29},{2,30},{3,31},{4,0},{5,1},{6,2},{7,3},{8,4},{9,5},{1... | collective-permute-start | bytes 786440 | tf_op jit(solution)/shard_map/ppermute | solution.py:44
  12.3 21.7 %collective-permute-done.1 = f32[64,1024]{1,0:T(8,128)S(1)} collective-permute-done((f32[64,1024]{1,0:T(8,128)S(1)}, f32[64,1024]{1,0:T(8,128)S(1)}, u32[]{:S(2)}, u32[]{:S(2)}) %collective-permute-start.1) | collective-permute-done | bytes 262176 | tf_op jit(solution)/shard_map/ppermute | solution.py:44
  33.9 0.9 collective-permute-start.2
  34.9 0.5 collective-permute-start.4
  35.4 1.1 dynamic_slice.20
  36.5 0.7 copy-done.1
  37.2 3.4 %collective-permute-start.17 = (f32[128,1024]{1,0:T(8,128)S(1)}, f32[128,1024]{1,0:T(8,128)S(1)}, u32[]{:S(2)}, u32[]{:S(2)}) collective-permute-start(f32[128,1024]{1,0:T(8,128)S(1)} %dynamic_slice.20), channel_id=1, source_target_pairs={{0,96},{1,97},{2,98},{3,99},{4,100},{5,101},{6,102},{7,103},{8,104... | collective-permute-start | bytes 1572872 | tf_op jit(solution)/shard_map/ppermute | solution.py:44
  40.6 2.2 %collective-permute-start.9 = (f32[64,1024]{1,0:T(8,128)}, f32[64,1024]{1,0:T(8,128)S(1)}, u32[]{:S(2)}, u32[]{:S(2)}) collective-permute-start(f32[64,1024]{1,0:T(8,128)} %collective-permute-done.3.refs_3_), channel_id=1, source_target_pairs={{0,4},{1,5},{2,6},{3,7},{4,8},{5,9},{6,10},{7,11},{8,12},{9,13},{1... | collective-permute-start | bytes 786440 | tf_op jit(solution)/shard_map/ppermute | solution.py:44
  42.9 2.4 %collective-permute-done.4.refs_4_ = f32[64,1024]{1,0:T(8,128)} collective-permute-done((f32[64,1024]{1,0:T(8,128)}, f32[64,1024]{1,0:T(8,128)}, u32[]{:S(2)}, u32[]{:S(2)}) %collective-permute-start.4) | collective-permute-done | bytes 262176 | tf_op jit(solution)/shard_map/ppermute | solution.py:44
  45.3 7.2 %collective-permute-start.12 = (f32[64,1024]{1,0:T(8,128)}, f32[64,1024]{1,0:T(8,128)}, u32[]{:S(2)}, u32[]{:S(2)}) collective-permute-start(f32[64,1024]{1,0:T(8,128)} %collective-permute-done.6.refs_6_), channel_id=1, source_target_pairs={{0,28},{1,29},{2,30},{3,31},{4,0},{5,1},{6,2},{7,3},{8,4},{9,5},{1... | collective-permute-start | bytes 786440 | tf_op jit(solution)/shard_map/ppermute | solution.py:44
  52.5 1.0 constant_dynamic-update-slice_fusion.refs_2_
  53.5 0.7 copy-done.3
  54.2 0.6 collective-permute-start.5
  54.8 3.9 %collective-permute-start.8 = (f32[128,1024]{1,0:T(8,128)S(1)}, f32[128,1024]{1,0:T(8,128)}, u32[]{:S(2)}, u32[]{:S(2)}) collective-permute-start(f32[128,1024]{1,0:T(8,128)S(1)} %constant_dynamic-update-slice_fusion.refs_2_), channel_id=1, source_target_pairs={{0,28},{1,29},{2,30},{3,31},{4,0},{5,1},{6,2},{7,3},{8,4},{9,5},{1... | collective-permute-start | bytes 1572872 | tf_op jit(solution)/shard_map/ppermute | solution.py:44
  58.8 3.4 %collective-permute-start.16 = (f32[1024,256]{1,0:T(8,128)}, f32[1024,256]{1,0:T(8,128)}, u32[]{:S(2)}, u32[]{:S(2)}) collective-permute-start(f32[1024,256]{1,0:T(8,128)} %collective-permute-done.15.refs_16_.refs_11_), channel_id=1, source_target_pairs={{0,1},{1,0},{2,3},{3,2},{4,5},{5,4},{6,7},{7,6},{8,9},{9,8},{10,11... | collective-permute-start | bytes 3145736 | tf_op jit(solution)/shard_map/ppermute | solution.py:44
  62.1 1.5 collective-permute-start.13
  63.6 5.6 %collective-permute-done.10.refs_10_ = f32[64,1024]{1,0:T(8,128)S(1)} collective-permute-done((f32[64,1024]{1,0:T(8,128)S(1)}, f32[64,1024]{1,0:T(8,128)S(1)}, u32[]{:S(2)}, u32[]{:S(2)}) %collective-permute-start.10) | collective-permute-done | bytes 262176 | tf_op jit(solution)/shard_map/ppermute | solution.py:44
  69.2 0.7 copy-done.7
  69.9 0.7 copy-done.5
  70.6 4.1 %collective-permute-done.13.refs_13_ = f32[64,1024]{1,0:T(8,128)S(1)} collective-permute-done((f32[64,1024]{1,0:T(8,128)}, f32[64,1024]{1,0:T(8,128)S(1)}, u32[]{:S(2)}, u32[]{:S(2)}) %collective-permute-start.13) | collective-permute-done | bytes 262176 | tf_op jit(solution)/shard_map/ppermute | solution.py:44
  74.7 0.7 copy-done.9
  75.4 2.9 %collective-permute-start.18 = (f32[128,1024]{1,0:T(8,128)S(1)}, f32[128,1024]{1,0:T(8,128)}, u32[]{:S(2)}, u32[]{:S(2)}) collective-permute-start(f32[128,1024]{1,0:T(8,128)S(1)} %collective-permute-done.17.refs_19_.refs_7_.refs_14_), channel_id=1, source_target_pairs={{0,128},{1,129},{2,130},{3,131},{4,132},{5,133},{6,134},{7,135},{8... | collective-permute-start | bytes 1572872 | tf_op jit(solution)/shard_map/ppermute | solution.py:44
  78.3 2.7 %collective-permute-start.14 = (f32[128,1024]{1,0:T(8,128)}, f32[128,1024]{1,0:T(8,128)}, u32[]{:S(2)}, u32[]{:S(2)}) collective-permute-start(f32[128,1024]{1,0:T(8,128)} %collective-permute-done.8.refs_8_), channel_id=1, source_target_pairs={{0,28},{1,29},{2,30},{3,31},{4,0},{5,1},{6,2},{7,3},{8,4},{9,5},{1... | collective-permute-start | bytes 1572872 | tf_op jit(solution)/shard_map/ppermute | solution.py:44
  81.0 0.1 collective-permute-start.25
  81.1 0.1 stack.27.s_ref
  81.2 1.4 constant_dynamic-slice_fusion.refs_18_.refs_6_.refs_13_
  82.6 13.3 %collective-permute-done.25.refs_3_ = f32[64,1024]{1,0:T(8,128)} collective-permute-done((f32[64,1024]{1,0:T(8,128)}, f32[64,1024]{1,0:T(8,128)}, u32[]{:S(2)}, u32[]{:S(2)}) %collective-permute-start.25) | collective-permute-done | bytes 262176 | tf_op jit(solution)/shard_map/ppermute | solution.py:44
  95.9 3.4 %collective-permute-start.31 = (f32[64,1024]{1,0:T(8,128)}, f32[64,1024]{1,0:T(8,128)S(1)}, u32[]{:S(2)}, u32[]{:S(2)}) collective-permute-start(f32[64,1024]{1,0:T(8,128)} %collective-permute-done.25.refs_3_), channel_id=1, source_target_pairs={{0,28},{1,29},{2,30},{3,31},{4,0},{5,1},{6,2},{7,3},{8,4},{9,5},{1... | collective-permute-start | bytes 786440 | tf_op jit(solution)/shard_map/ppermute | solution.py:44
  99.4 2.7 %collective-permute-start.27 = (f32[128,1024]{1,0:T(8,128)}, f32[128,1024]{1,0:T(8,128)S(1)}, u32[]{:S(2)}, u32[]{:S(2)}) collective-permute-start(f32[128,1024]{1,0:T(8,128)} %collective-permute-done.14.refs_14_), channel_id=1, source_target_pairs={{0,28},{1,29},{2,30},{3,31},{4,0},{5,1},{6,2},{7,3},{8,4},{9,5},{1... | collective-permute-start | bytes 1572872 | tf_op jit(solution)/shard_map/ppermute | solution.py:44
  102.1 0.9 copy-done.6
  103.0 0.9 copy-done.8
  104.0 0.9 copy-done.10
  104.9 12.7 %shard_map.50 = (f32[640,512]{1,0:T(8,128)S(1)}, f32[640,512]{1,0:T(8,128)S(1)}, f32[512,1024]{1,0:T(8,128)S(1)}) custom-call(s32[6]{0:T(128)S(1)} %stack.27.s_ref, f32[64,1024]{1,0:T(8,128)S(1)} %get-tuple-element.33.refs_0_, f32[64,1024]{1,0:T(8,128)S(1)} %copy-done.2, f32[128,1024]{1,0:T(8,128)S(1)} %constant_dynamic-update-slice_fusion.refs_2_, ...), custom_call_target="tpu_custom_call" | custom-call | flops 8053063680 | bytes 9437184 | tf_op jit(solution)/shard_map/pallas_call | solution.py:154
  117.6 4.4 %collective-permute-start.19 = (f32[640,512]{1,0:T(8,128)S(1)}, f32[640,512]{1,0:T(8,128)S(1)}, u32[]{:S(2)}, u32[]{:S(2)}) collective-permute-start(f32[640,512]{1,0:T(8,128)S(1)} %get-tuple-element.17), channel_id=1, source_target_pairs={{0,1},{1,0},{2,3},{3,2},{4,5},{5,4},{6,7},{7,6},{8,9},{9,8},{10,11... | collective-permute-start | bytes 3932168 | tf_op jit(solution)/shard_map/ppermute | solution.py:44
  122.0 1.5 collective-permute-start.26
  123.5 0.1 collective-permute-start.32
  123.6 0.1 collective-permute-start.33
  123.7 3.0 %collective-permute-start.34 = (f32[64,1024]{1,0:T(8,128)S(1)}, f32[64,1024]{1,0:T(8,128)S(1)}, u32[]{:S(2)}, u32[]{:S(2)}) collective-permute-start(f32[64,1024]{1,0:T(8,128)S(1)} %slice.73), channel_id=1, source_target_pairs={{0,28},{1,29},{2,30},{3,31},{4,0},{5,1},{6,2},{7,3},{8,4},{9,5},{1... | collective-permute-start | bytes 786440 | tf_op jit(solution)/shard_map/ppermute | solution.py:44
  126.7 3.3 %collective-permute-done.26.refs_4_ = f32[64,1024]{1,0:T(8,128)S(1)} collective-permute-done((f32[64,1024]{1,0:T(8,128)}, f32[64,1024]{1,0:T(8,128)S(1)}, u32[]{:S(2)}, u32[]{:S(2)}) %collective-permute-start.26) | collective-permute-done | bytes 262176 | tf_op jit(solution)/shard_map/ppermute | solution.py:44
  130.0 5.6 %collective-permute-done.32.refs_7_ = f32[64,1024]{1,0:T(8,128)S(1)} collective-permute-done((f32[64,1024]{1,0:T(8,128)S(1)}, f32[64,1024]{1,0:T(8,128)S(1)}, u32[]{:S(2)}, u32[]{:S(2)}) %collective-permute-start.32) | collective-permute-done | bytes 262176 | tf_op jit(solution)/shard_map/ppermute | solution.py:44
  135.6 5.9 %shard_map.52 = (f32[128,512]{1,0:T(8,128)S(1)}, f32[128,512]{1,0:T(8,128)S(1)}, f32[128,1024]{1,0:T(8,128)S(1)}, f32[128,1024]{1,0:T(8,128)S(1)}, f32[128,1024]{1,0:T(8,128)S(1)}, /*index=5*/f32[128,1024]{1,0:T(8,128)S(1)}) custom-call(s32[6]{0:T(128)S(1)} %stack.27.s_ref, f32[64,1024]{1,0:T(8,128)} %collective-permute-done.22.refs_0_, ...), custom_call_target="tpu_custom_call" | custom-call | flops 4831838208 | bytes 7340032 | tf_op jit(solution)/shard_map/pallas_call | solution.py:154
  141.5 1.0 collective-permute-start.35
  142.6 3.5 %shard_map.51 = (f32[256,512]{1,0:T(8,128)S(1)}, f32[256,512]{1,0:T(8,128)S(1)}) custom-call(s32[6]{0:T(128)S(1)} %stack.27.s_ref, f32[64,1024]{1,0:T(8,128)} %collective-permute-done.22.refs_0_, f32[64,1024]{1,0:T(8,128)S(1)} %collective-permute-done.23.refs_1_, f32[128,1024]{1,0:T(8,128)S(1)} %collective-permute-done.24.refs_2_, ...), custom_call_target="tpu_custom_call" | custom-call | flops 3221225472 | bytes 6291456 | tf_op jit(solution)/shard_map/pallas_call | solution.py:154
  146.1 0.1 collective-permute-start.28
  146.3 0.1 collective-permute-start.39
  146.4 2.9 %collective-permute-start.36 = (f32[128,256]{1,0:T(8,128)S(1)}, f32[128,256]{1,0:T(8,128)S(1)}, u32[]{:S(2)}, u32[]{:S(2)}) collective-permute-start(f32[128,256]{1,0:T(8,128)S(1)} %slice_add_fusion.4), channel_id=1, source_target_pairs={{0,96},{1,97},{2,98},{3,99},{4,100},{5,101},{6,102},{7,103},{8,104... | collective-permute-start | bytes 393224 | tf_op jit(solution)/shard_map/ppermute | solution.py:44
  149.3 0.1 slice_add_fusion
  149.4 1.4 collective-permute-start.20
  150.8 0.2 collective-permute-start.29
  151.0 2.6 %collective-permute-start.38 = (f32[128,1024]{1,0:T(8,128)S(1)}, f32[128,1024]{1,0:T(8,128)S(1)}, u32[]{:S(2)}, u32[]{:S(2)}) collective-permute-start(f32[128,1024]{1,0:T(8,128)S(1)} %get-tuple-element.27), channel_id=1, source_target_pairs={{0,128},{1,129},{2,130},{3,131},{4,132},{5,133},{6,134},{7,135},{8... | collective-permute-start | bytes 1572872 | tf_op jit(solution)/shard_map/ppermute | solution.py:44
  153.7 7.2 %collective-permute-done.39 = f32[128,1024]{1,0:T(8,128)S(1)} collective-permute-done((f32[128,1024]{1,0:T(8,128)S(1)}, f32[128,1024]{1,0:T(8,128)S(1)}, u32[]{:S(2)}, u32[]{:S(2)}) %collective-permute-start.39) | collective-permute-done | bytes 524320 | tf_op jit(solution)/shard_map/ppermute | solution.py:44
  161.0 2.9 %collective-permute-start.40 = (f32[128,1024]{1,0:T(8,128)S(1)}, f32[128,1024]{1,0:T(8,128)S(1)}, u32[]{:S(2)}, u32[]{:S(2)}) collective-permute-start(f32[128,1024]{1,0:T(8,128)S(1)} %add.70), channel_id=1, source_target_pairs={{0,96},{1,97},{2,98},{3,99},{4,100},{5,101},{6,102},{7,103},{8,104... | collective-permute-start | bytes 1572872 | tf_op jit(solution)/shard_map/ppermute | solution.py:44
  163.8 0.1 fusion.1
  163.9 9.4 %collective-permute-done.20 = f32[320,512]{1,0:T(8,128)S(1)} collective-permute-done((f32[320,512]{1,0:T(8,128)S(1)}, f32[320,512]{1,0:T(8,128)S(1)}, u32[]{:S(2)}, u32[]{:S(2)}) %collective-permute-start.20) | collective-permute-done | bytes 655392 | tf_op jit(solution)/shard_map/ppermute | solution.py:44
  173.3 0.2 fusion
  173.6 2.8 %collective-permute-start.21 = (f32[320,256]{1,0:T(8,128)S(1)}, f32[320,256]{1,0:T(8,128)S(1)}, u32[]{:S(2)}, u32[]{:S(2)}) collective-permute-start(f32[320,256]{1,0:T(8,128)S(1)} %get-tuple-element.30), channel_id=1, source_target_pairs={{0,96},{1,97},{2,98},{3,99},{4,100},{5,101},{6,102},{7,103},{8,104... | collective-permute-start | bytes 983048 | tf_op jit(solution)/shard_map/ppermute | solution.py:44
  176.5 0.3 collective-permute-start.30
  176.7 1.4 collective-permute-start.37
  178.1 10.7 %collective-permute-done.37.refs_5_ = f32[64,256]{1,0:T(8,128)S(1)} collective-permute-done((f32[64,256]{1,0:T(8,128)S(1)}, f32[64,256]{1,0:T(8,128)S(1)}, u32[]{:S(2)}, u32[]{:S(2)}) %collective-permute-start.37) | collective-permute-done | bytes 65568 | tf_op jit(solution)/shard_map/ppermute | solution.py:44
  188.8 1.8 shard_map.53
  (67 shorter events, 0.5 us)
Async XLA Ops:
  0.6 5.7 %copy-start.11 = (f32[64,2048]{1,0:T(8,128)S(1)}, f32[64,2048]{1,0:T(8,128)}, u32[]{:S(2)}) copy-start(f32[64,2048]{1,0:T(8,128)} %param.4) | copy-start | bytes 1572868
  3.0 55.8 %collective-permute-start.15 = (f32[1024,256]{1,0:T(8,128)}, f32[1024,256]{1,0:T(8,128)}, u32[]{:S(2)}, u32[]{:S(2)}) collective-permute-start(f32[1024,256]{1,0:T(8,128)} %bitcast.7), channel_id=1, source_target_pairs={{0,96},{1,97},{2,98},{3,99},{4,100},{5,101},{6,102},{7,103},{8,104... | collective-permute-start | bytes 3145736 | tf_op jit(solution)/shard_map/ppermute | solution.py:44
  6.3 27.6 %collective-permute-start.1 = (f32[64,1024]{1,0:T(8,128)S(1)}, f32[64,1024]{1,0:T(8,128)S(1)}, u32[]{:S(2)}, u32[]{:S(2)}) collective-permute-start(f32[64,1024]{1,0:T(8,128)S(1)} %get-tuple-element.32), channel_id=1, source_target_pairs={{0,96},{1,97},{2,98},{3,99},{4,100},{5,101},{6,102},{7,103},{8,104... | collective-permute-start | bytes 786440 | tf_op jit(solution)/shard_map/ppermute | solution.py:44
  6.4 28.5 %collective-permute-start.3 = (f32[64,1024]{1,0:T(8,128)S(1)}, f32[64,1024]{1,0:T(8,128)}, u32[]{:S(2)}, u32[]{:S(2)}) collective-permute-start(f32[64,1024]{1,0:T(8,128)S(1)} %get-tuple-element.33.refs_0_), channel_id=1, source_target_pairs={{0,4},{1,5},{2,6},{3,7},{4,8},{5,9},{6,10},{7,11},{8,12},{9,13},{1... | collective-permute-start | bytes 786440 | tf_op jit(solution)/shard_map/ppermute | solution.py:44
  8.3 28.3 %collective-permute-start = (f32[64,1024]{1,0:T(8,128)S(1)}, f32[64,1024]{1,0:T(8,128)S(1)}, u32[]{:S(2)}, u32[]{:S(2)}) collective-permute-start(f32[64,1024]{1,0:T(8,128)S(1)} %get-tuple-element.33.refs_0_), channel_id=1, source_target_pairs={{0,32},{1,33},{2,34},{3,35},{4,36},{5,37},{6,38},{7,39},{8,40},{9,... | collective-permute-start | bytes 786440 | tf_op jit(solution)/shard_map/ppermute | solution.py:44
  8.3 32.4 %collective-permute-start.6 = (f32[64,1024]{1,0:T(8,128)S(1)}, f32[64,1024]{1,0:T(8,128)}, u32[]{:S(2)}, u32[]{:S(2)}) collective-permute-start(f32[64,1024]{1,0:T(8,128)S(1)} %get-tuple-element.33.refs_0_), channel_id=1, source_target_pairs={{0,28},{1,29},{2,30},{3,31},{4,0},{5,1},{6,2},{7,3},{8,4},{9,5},{1... | collective-permute-start | bytes 786440 | tf_op jit(solution)/shard_map/ppermute | solution.py:44
  33.9 6.7 %collective-permute-start.2 = (f32[64,1024]{1,0:T(8,128)S(1)}, f32[64,1024]{1,0:T(8,128)S(1)}, u32[]{:S(2)}, u32[]{:S(2)}) collective-permute-start(f32[64,1024]{1,0:T(8,128)S(1)} %collective-permute-done.1), channel_id=1, source_target_pairs={{0,32},{1,33},{2,34},{3,35},{4,36},{5,37},{6,38},{7,39},{8,40},{9,... | collective-permute-start | bytes 786440 | tf_op jit(solution)/shard_map/ppermute | solution.py:44
  34.9 10.4 %collective-permute-start.4 = (f32[64,1024]{1,0:T(8,128)}, f32[64,1024]{1,0:T(8,128)}, u32[]{:S(2)}, u32[]{:S(2)}) collective-permute-start(f32[64,1024]{1,0:T(8,128)} %collective-permute-done.3.refs_3_), channel_id=1, source_target_pairs={{0,32},{1,33},{2,34},{3,35},{4,36},{5,37},{6,38},{7,39},{8,40},{9,... | collective-permute-start | bytes 786440 | tf_op jit(solution)/shard_map/ppermute | solution.py:44
  36.5 0.7 copy-start.1
  37.2 24.9 %collective-permute-start.17 = (f32[128,1024]{1,0:T(8,128)S(1)}, f32[128,1024]{1,0:T(8,128)S(1)}, u32[]{:S(2)}, u32[]{:S(2)}) collective-permute-start(f32[128,1024]{1,0:T(8,128)S(1)} %dynamic_slice.20), channel_id=1, source_target_pairs={{0,96},{1,97},{2,98},{3,99},{4,100},{5,101},{6,102},{7,103},{8,104... | collective-permute-start | bytes 1572872 | tf_op jit(solution)/shard_map/ppermute | solution.py:44
  40.6 12.9 %collective-permute-start.7 = (f32[64,1024]{1,0:T(8,128)}, f32[64,1024]{1,0:T(8,128)S(1)}, u32[]{:S(2)}, u32[]{:S(2)}) collective-permute-start(f32[64,1024]{1,0:T(8,128)} %collective-permute-done.6.refs_6_), channel_id=1, source_target_pairs={{0,32},{1,33},{2,34},{3,35},{4,36},{5,37},{6,38},{7,39},{8,40},{9,... | collective-permute-start | bytes 786440 | tf_op jit(solution)/shard_map/ppermute | solution.py:44
  40.6 2.2 %copy-start.12 = (f32[64,1024]{1,0:T(8,128)}, f32[64,1024]{1,0:T(8,128)S(1)}, u32[]{:S(2)}) copy-start(f32[64,1024]{1,0:T(8,128)S(1)} %collective-permute-done.2) | copy-start | bytes 786436
  40.6 14.2 %collective-permute-start.9 = (f32[64,1024]{1,0:T(8,128)}, f32[64,1024]{1,0:T(8,128)S(1)}, u32[]{:S(2)}, u32[]{:S(2)}) collective-permute-start(f32[64,1024]{1,0:T(8,128)} %collective-permute-done.3.refs_3_), channel_id=1, source_target_pairs={{0,4},{1,5},{2,6},{3,7},{4,8},{5,9},{6,10},{7,11},{8,12},{9,13},{1... | collective-permute-start | bytes 786440 | tf_op jit(solution)/shard_map/ppermute | solution.py:44
  42.9 59.2 %copy-start = (f32[2048,256]{1,0:T(8,128)S(1)}, f32[2048,256]{1,0:T(8,128)}, u32[]{:S(2)}) copy-start(f32[2048,256]{1,0:T(8,128)} %refs_10_.1) | copy-start | bytes 6291460
  45.3 16.8 %collective-permute-start.12 = (f32[64,1024]{1,0:T(8,128)}, f32[64,1024]{1,0:T(8,128)}, u32[]{:S(2)}, u32[]{:S(2)}) collective-permute-start(f32[64,1024]{1,0:T(8,128)} %collective-permute-done.6.refs_6_), channel_id=1, source_target_pairs={{0,28},{1,29},{2,30},{3,31},{4,0},{5,1},{6,2},{7,3},{8,4},{9,5},{1... | collective-permute-start | bytes 786440 | tf_op jit(solution)/shard_map/ppermute | solution.py:44
  53.5 0.7 copy-start.3
  54.2 24.1 %collective-permute-start.5 = (f32[128,1024]{1,0:T(8,128)S(1)}, f32[128,1024]{1,0:T(8,128)}, u32[]{:S(2)}, u32[]{:S(2)}) collective-permute-start(f32[128,1024]{1,0:T(8,128)S(1)} %constant_dynamic-update-slice_fusion.refs_2_), channel_id=1, source_target_pairs={{0,4},{1,5},{2,6},{3,7},{4,8},{5,9},{6,10},{7,11},{8,12},{9,13},{1... | collective-permute-start | bytes 1572872 | tf_op jit(solution)/shard_map/ppermute | solution.py:44
  54.8 23.5 %collective-permute-start.8 = (f32[128,1024]{1,0:T(8,128)S(1)}, f32[128,1024]{1,0:T(8,128)}, u32[]{:S(2)}, u32[]{:S(2)}) collective-permute-start(f32[128,1024]{1,0:T(8,128)S(1)} %constant_dynamic-update-slice_fusion.refs_2_), channel_id=1, source_target_pairs={{0,28},{1,29},{2,30},{3,31},{4,0},{5,1},{6,2},{7,3},{8,4},{9,5},{1... | collective-permute-start | bytes 1572872 | tf_op jit(solution)/shard_map/ppermute | solution.py:44
  58.8 43.3 %collective-permute-start.16 = (f32[1024,256]{1,0:T(8,128)}, f32[1024,256]{1,0:T(8,128)}, u32[]{:S(2)}, u32[]{:S(2)}) collective-permute-start(f32[1024,256]{1,0:T(8,128)} %collective-permute-done.15.refs_16_.refs_11_), channel_id=1, source_target_pairs={{0,1},{1,0},{2,3},{3,2},{4,5},{5,4},{6,7},{7,6},{8,9},{9,8},{10,11... | collective-permute-start | bytes 3145736 | tf_op jit(solution)/shard_map/ppermute | solution.py:44
  62.1 7.1 %collective-permute-start.10 = (f32[64,1024]{1,0:T(8,128)S(1)}, f32[64,1024]{1,0:T(8,128)S(1)}, u32[]{:S(2)}, u32[]{:S(2)}) collective-permute-start(f32[64,1024]{1,0:T(8,128)S(1)} %collective-permute-done.9.refs_9_), channel_id=1, source_target_pairs={{0,32},{1,33},{2,34},{3,35},{4,36},{5,37},{6,38},{7,39},{8,40},{9,... | collective-permute-start | bytes 786440 | tf_op jit(solution)/shard_map/ppermute | solution.py:44
  62.1 12.6 %collective-permute-start.13 = (f32[64,1024]{1,0:T(8,128)}, f32[64,1024]{1,0:T(8,128)S(1)}, u32[]{:S(2)}, u32[]{:S(2)}) collective-permute-start(f32[64,1024]{1,0:T(8,128)} %collective-permute-done.12.refs_12_), channel_id=1, source_target_pairs={{0,32},{1,33},{2,34},{3,35},{4,36},{5,37},{6,38},{7,39},{8,40},{9,... | collective-permute-start | bytes 786440 | tf_op jit(solution)/shard_map/ppermute | solution.py:44
  69.2 0.7 copy-start.7
  69.9 11.1 %collective-permute-start.22 = (f32[64,1024]{1,0:T(8,128)S(1)}, f32[64,1024]{1,0:T(8,128)}, u32[]{:S(2)}, u32[]{:S(2)}) collective-permute-start(f32[64,1024]{1,0:T(8,128)S(1)} %collective-permute-done.9.refs_9_), channel_id=1, source_target_pairs={{0,4},{1,5},{2,6},{3,7},{4,8},{5,9},{6,10},{7,11},{8,12},{9,13},{1... | collective-permute-start | bytes 786440 | tf_op jit(solution)/shard_map/ppermute | solution.py:44
  69.9 0.7 copy-start.5
  74.7 0.7 copy-start.9
  75.4 20.5 %collective-permute-start.18 = (f32[128,1024]{1,0:T(8,128)S(1)}, f32[128,1024]{1,0:T(8,128)}, u32[]{:S(2)}, u32[]{:S(2)}) collective-permute-start(f32[128,1024]{1,0:T(8,128)S(1)} %collective-permute-done.17.refs_19_.refs_7_.refs_14_), channel_id=1, source_target_pairs={{0,128},{1,129},{2,130},{3,131},{4,132},{5,133},{6,134},{7,135},{8... | collective-permute-start | bytes 1572872 | tf_op jit(solution)/shard_map/ppermute | solution.py:44
  78.3 21.0 %collective-permute-start.11 = (f32[128,1024]{1,0:T(8,128)}, f32[128,1024]{1,0:T(8,128)}, u32[]{:S(2)}, u32[]{:S(2)}) collective-permute-start(f32[128,1024]{1,0:T(8,128)} %collective-permute-done.5.refs_5_), channel_id=1, source_target_pairs={{0,4},{1,5},{2,6},{3,7},{4,8},{5,9},{6,10},{7,11},{8,12},{9,13},{1... | collective-permute-start | bytes 1572872 | tf_op jit(solution)/shard_map/ppermute | solution.py:44
  78.3 21.0 %collective-permute-start.14 = (f32[128,1024]{1,0:T(8,128)}, f32[128,1024]{1,0:T(8,128)}, u32[]{:S(2)}, u32[]{:S(2)}) collective-permute-start(f32[128,1024]{1,0:T(8,128)} %collective-permute-done.8.refs_8_), channel_id=1, source_target_pairs={{0,28},{1,29},{2,30},{3,31},{4,0},{5,1},{6,2},{7,3},{8,4},{9,5},{1... | collective-permute-start | bytes 1572872 | tf_op jit(solution)/shard_map/ppermute | solution.py:44
  81.0 14.9 %collective-permute-start.25 = (f32[64,1024]{1,0:T(8,128)}, f32[64,1024]{1,0:T(8,128)}, u32[]{:S(2)}, u32[]{:S(2)}) collective-permute-start(f32[64,1024]{1,0:T(8,128)} %collective-permute-done.12.refs_12_), channel_id=1, source_target_pairs={{0,28},{1,29},{2,30},{3,31},{4,0},{5,1},{6,2},{7,3},{8,4},{9,5},{1... | collective-permute-start | bytes 786440 | tf_op jit(solution)/shard_map/ppermute | solution.py:44
  81.2 20.9 %copy-start.2 = (f32[64,1024]{1,0:T(8,128)S(1)}, f32[64,1024]{1,0:T(8,128)}, u32[]{:S(2)}) copy-start(f32[64,1024]{1,0:T(8,128)} %copy-done.1) | copy-start | bytes 786436
  81.2 20.9 %copy-start.4 = (f32[64,1024]{1,0:T(8,128)S(1)}, f32[64,1024]{1,0:T(8,128)}, u32[]{:S(2)}) copy-start(f32[64,1024]{1,0:T(8,128)} %copy-done.3) | copy-start | bytes 786436
  95.9 27.8 %collective-permute-start.23 = (f32[64,1024]{1,0:T(8,128)}, f32[64,1024]{1,0:T(8,128)S(1)}, u32[]{:S(2)}, u32[]{:S(2)}) collective-permute-start(f32[64,1024]{1,0:T(8,128)} %collective-permute-done.22.refs_0_), channel_id=1, source_target_pairs={{0,32},{1,33},{2,34},{3,35},{4,36},{5,37},{6,38},{7,39},{8,40},{9,... | collective-permute-start | bytes 786440 | tf_op jit(solution)/shard_map/ppermute | solution.py:44
  95.9 26.1 %collective-permute-start.31 = (f32[64,1024]{1,0:T(8,128)}, f32[64,1024]{1,0:T(8,128)S(1)}, u32[]{:S(2)}, u32[]{:S(2)}) collective-permute-start(f32[64,1024]{1,0:T(8,128)} %collective-permute-done.25.refs_3_), channel_id=1, source_target_pairs={{0,28},{1,29},{2,30},{3,31},{4,0},{5,1},{6,2},{7,3},{8,4},{9,5},{1... | collective-permute-start | bytes 786440 | tf_op jit(solution)/shard_map/ppermute | solution.py:44
  99.3 24.1 %collective-permute-start.24 = (f32[128,1024]{1,0:T(8,128)}, f32[128,1024]{1,0:T(8,128)S(1)}, u32[]{:S(2)}, u32[]{:S(2)}) collective-permute-start(f32[128,1024]{1,0:T(8,128)} %collective-permute-done.11.refs_11_), channel_id=1, source_target_pairs={{0,4},{1,5},{2,6},{3,7},{4,8},{5,9},{6,10},{7,11},{8,12},{9,13},{1... | collective-permute-start | bytes 1572872 | tf_op jit(solution)/shard_map/ppermute | solution.py:44
  99.4 24.2 %collective-permute-start.27 = (f32[128,1024]{1,0:T(8,128)}, f32[128,1024]{1,0:T(8,128)S(1)}, u32[]{:S(2)}, u32[]{:S(2)}) collective-permute-start(f32[128,1024]{1,0:T(8,128)} %collective-permute-done.14.refs_14_), channel_id=1, source_target_pairs={{0,28},{1,29},{2,30},{3,31},{4,0},{5,1},{6,2},{7,3},{8,4},{9,5},{1... | collective-permute-start | bytes 1572872 | tf_op jit(solution)/shard_map/ppermute | solution.py:44
  102.1 1.0 copy-start.6
  103.0 0.9 copy-start.8
  104.0 0.9 copy-start.10
  117.6 31.6 %collective-permute-start.19 = (f32[640,512]{1,0:T(8,128)S(1)}, f32[640,512]{1,0:T(8,128)S(1)}, u32[]{:S(2)}, u32[]{:S(2)}) collective-permute-start(f32[640,512]{1,0:T(8,128)S(1)} %get-tuple-element.17), channel_id=1, source_target_pairs={{0,1},{1,0},{2,3},{3,2},{4,5},{5,4},{6,7},{7,6},{8,9},{9,8},{10,11... | collective-permute-start | bytes 3932168 | tf_op jit(solution)/shard_map/ppermute | solution.py:44
  122.0 8.0 %collective-permute-start.26 = (f32[64,1024]{1,0:T(8,128)}, f32[64,1024]{1,0:T(8,128)S(1)}, u32[]{:S(2)}, u32[]{:S(2)}) collective-permute-start(f32[64,1024]{1,0:T(8,128)} %collective-permute-done.25.refs_3_), channel_id=1, source_target_pairs={{0,32},{1,33},{2,34},{3,35},{4,36},{5,37},{6,38},{7,39},{8,40},{9,... | collective-permute-start | bytes 786440 | tf_op jit(solution)/shard_map/ppermute | solution.py:44
  123.5 12.1 %collective-permute-start.32 = (f32[64,1024]{1,0:T(8,128)S(1)}, f32[64,1024]{1,0:T(8,128)S(1)}, u32[]{:S(2)}, u32[]{:S(2)}) collective-permute-start(f32[64,1024]{1,0:T(8,128)S(1)} %collective-permute-done.31.refs_6_), channel_id=1, source_target_pairs={{0,32},{1,33},{2,34},{3,35},{4,36},{5,37},{6,38},{7,39},{8,40},{9,... | collective-permute-start | bytes 786440 | tf_op jit(solution)/shard_map/ppermute | solution.py:44
  123.6 12.0 %collective-permute-start.33 = (f32[64,1024]{1,0:T(8,128)S(1)}, f32[64,1024]{1,0:T(8,128)S(1)}, u32[]{:S(2)}, u32[]{:S(2)}) collective-permute-start(f32[64,1024]{1,0:T(8,128)S(1)} %slice.72), channel_id=1, source_target_pairs={{0,4},{1,5},{2,6},{3,7},{4,8},{5,9},{6,10},{7,11},{8,12},{9,13},{1... | collective-permute-start | bytes 786440 | tf_op jit(solution)/shard_map/ppermute | solution.py:44
  123.7 11.9 %collective-permute-start.34 = (f32[64,1024]{1,0:T(8,128)S(1)}, f32[64,1024]{1,0:T(8,128)S(1)}, u32[]{:S(2)}, u32[]{:S(2)}) collective-permute-start(f32[64,1024]{1,0:T(8,128)S(1)} %slice.73), channel_id=1, source_target_pairs={{0,28},{1,29},{2,30},{3,31},{4,0},{5,1},{6,2},{7,3},{8,4},{9,5},{1... | collective-permute-start | bytes 786440 | tf_op jit(solution)/shard_map/ppermute | solution.py:44
  141.5 4.8 %collective-permute-start.35 = (f32[128,512]{1,0:T(8,128)S(1)}, f32[128,512]{1,0:T(8,128)S(1)}, u32[]{:S(2)}, u32[]{:S(2)}) collective-permute-start(f32[128,512]{1,0:T(8,128)S(1)} %get-tuple-element.25), channel_id=1, source_target_pairs={{0,1},{1,0},{2,3},{3,2},{4,5},{5,4},{6,7},{7,6},{8,9},{9,8},{10,11... | collective-permute-start | bytes 786440 | tf_op jit(solution)/shard_map/ppermute | solution.py:44
  146.1 4.6 %collective-permute-start.28 = (f32[256,512]{1,0:T(8,128)S(1)}, f32[256,512]{1,0:T(8,128)S(1)}, u32[]{:S(2)}, u32[]{:S(2)}) collective-permute-start(f32[256,512]{1,0:T(8,128)S(1)} %get-tuple-element.19), channel_id=1, source_target_pairs={{0,1},{1,0},{2,3},{3,2},{4,5},{5,4},{6,7},{7,6},{8,9},{9,8},{10,11... | collective-permute-start | bytes 1572872 | tf_op jit(solution)/shard_map/ppermute | solution.py:44
  146.3 14.6 %collective-permute-start.39 = (f32[128,1024]{1,0:T(8,128)S(1)}, f32[128,1024]{1,0:T(8,128)S(1)}, u32[]{:S(2)}, u32[]{:S(2)}) collective-permute-start(f32[128,1024]{1,0:T(8,128)S(1)} %get-tuple-element.29), channel_id=1, source_target_pairs={{0,128},{1,129},{2,130},{3,131},{4,132},{5,133},{6,134},{7,135},{8... | collective-permute-start | bytes 1572872 | tf_op jit(solution)/shard_map/ppermute | solution.py:44
  146.4 7.2 %collective-permute-start.36 = (f32[128,256]{1,0:T(8,128)S(1)}, f32[128,256]{1,0:T(8,128)S(1)}, u32[]{:S(2)}, u32[]{:S(2)}) collective-permute-start(f32[128,256]{1,0:T(8,128)S(1)} %slice_add_fusion.4), channel_id=1, source_target_pairs={{0,96},{1,97},{2,98},{3,99},{4,100},{5,101},{6,102},{7,103},{8,104... | collective-permute-start | bytes 393224 | tf_op jit(solution)/shard_map/ppermute | solution.py:44
  149.4 24.0 %collective-permute-start.20 = (f32[320,512]{1,0:T(8,128)S(1)}, f32[320,512]{1,0:T(8,128)S(1)}, u32[]{:S(2)}, u32[]{:S(2)}) collective-permute-start(f32[320,512]{1,0:T(8,128)S(1)} %slice_add_fusion), channel_id=1, source_target_pairs={{0,2},{1,3},{2,0},{3,1},{4,6},{5,7},{6,4},{7,5},{8,10},{9,11},{10,... | collective-permute-start | bytes 1966088 | tf_op jit(solution)/shard_map/ppermute | solution.py:44
  150.8 13.0 %collective-permute-start.29 = (f32[256,256]{1,0:T(8,128)S(1)}, f32[256,256]{1,0:T(8,128)S(1)}, u32[]{:S(2)}, u32[]{:S(2)}) collective-permute-start(f32[256,256]{1,0:T(8,128)S(1)} %slice_add_fusion.2), channel_id=1, source_target_pairs={{0,96},{1,97},{2,98},{3,99},{4,100},{5,101},{6,102},{7,103},{8,104... | collective-permute-start | bytes 786440 | tf_op jit(solution)/shard_map/ppermute | solution.py:44
  151.0 37.7 %collective-permute-start.38 = (f32[128,1024]{1,0:T(8,128)S(1)}, f32[128,1024]{1,0:T(8,128)S(1)}, u32[]{:S(2)}, u32[]{:S(2)}) collective-permute-start(f32[128,1024]{1,0:T(8,128)S(1)} %get-tuple-element.27), channel_id=1, source_target_pairs={{0,128},{1,129},{2,130},{3,131},{4,132},{5,133},{6,134},{7,135},{8... | collective-permute-start | bytes 1572872 | tf_op jit(solution)/shard_map/ppermute | solution.py:44
  161.0 27.8 %collective-permute-start.40 = (f32[128,1024]{1,0:T(8,128)S(1)}, f32[128,1024]{1,0:T(8,128)S(1)}, u32[]{:S(2)}, u32[]{:S(2)}) collective-permute-start(f32[128,1024]{1,0:T(8,128)S(1)} %add.70), channel_id=1, source_target_pairs={{0,96},{1,97},{2,98},{3,99},{4,100},{5,101},{6,102},{7,103},{8,104... | collective-permute-start | bytes 1572872 | tf_op jit(solution)/shard_map/ppermute | solution.py:44
  173.6 15.2 %collective-permute-start.21 = (f32[320,256]{1,0:T(8,128)S(1)}, f32[320,256]{1,0:T(8,128)S(1)}, u32[]{:S(2)}, u32[]{:S(2)}) collective-permute-start(f32[320,256]{1,0:T(8,128)S(1)} %get-tuple-element.30), channel_id=1, source_target_pairs={{0,96},{1,97},{2,98},{3,99},{4,100},{5,101},{6,102},{7,103},{8,104... | collective-permute-start | bytes 983048 | tf_op jit(solution)/shard_map/ppermute | solution.py:44
  176.5 12.3 %collective-permute-start.30 = (f32[128,256]{1,0:T(8,128)S(1)}, f32[128,256]{1,0:T(8,128)S(1)}, u32[]{:S(2)}, u32[]{:S(2)}) collective-permute-start(f32[128,256]{1,0:T(8,128)S(1)} %get-tuple-element.34), channel_id=1, source_target_pairs={{0,2},{1,3},{2,0},{3,1},{4,6},{5,7},{6,4},{7,5},{8,10},{9,11},{10,... | collective-permute-start | bytes 393224 | tf_op jit(solution)/shard_map/ppermute | solution.py:44
  176.7 12.1 %collective-permute-start.37 = (f32[64,256]{1,0:T(8,128)S(1)}, f32[64,256]{1,0:T(8,128)S(1)}, u32[]{:S(2)}, u32[]{:S(2)}) collective-permute-start(f32[64,256]{1,0:T(8,128)S(1)} %get-tuple-element.36), channel_id=1, source_target_pairs={{0,2},{1,3},{2,0},{3,1},{4,6},{5,7},{6,4},{7,5},{8,10},{9,11},{10,... | collective-permute-start | bytes 196616 | tf_op jit(solution)/shard_map/ppermute | solution.py:44
